TPU v7x, 32 devices: a whole 2x2x4 slice. The times are simulated.
32 devices in a mesh: rep: 2 (over y), shard: 16 (over z, x, core).
Axes of the slice: x: 2, y: 2, z: 4, core: 2. Of those that a mesh axis runs over, the one named last changes fastest.
Arguments:
- tokens: bfloat16 [32768, 1024], P(('rep', 'shard')), may hold values from -6 to 6
- teacher: bfloat16 [32768, 1024], P(('rep', 'shard')), may hold values from -6 to 6
- valid: int32 [32768], P(('rep', 'shard')), may hold values from 0 to 1
- segments: int32 [32, 1024], P(('rep', 'shard')), may hold values from 0 to 7, as said below
- positions: int32 [32, 1024], P(('rep', 'shard')), may hold values from 0 to 2046, as said below
- w_qkv: bfloat16 [1024, 3072], P('shard'), may hold values from -0.1875 to 0.1875
- w_out: bfloat16 [1024, 1024], P('shard'), may hold values from -0.1875 to 0.1875
- w_upgate: bfloat16 [1024, 8192], P('shard'), may hold values from -0.1875 to 0.1875
- w_down: bfloat16 [4096, 1024], P('shard'), may hold values from -0.09375 to 0.09375
- s_qk: bfloat16 [1024], P('shard'), may hold values from 0.69921875 to 1.5
- alpha_attn: bfloat16 [1024], P('shard'), may hold values from 0.049804688 to 0.5
- s_up: bfloat16 [4096], P('shard'), may hold values from 0.5 to 1.5
- s_gate: bfloat16 [4096], P('shard'), may hold values from 0.5 to 2
- alpha_mlp: bfloat16 [1024], P('shard'), may hold values from 0.049804688 to 0.5
Outputs:
- output: bfloat16 [32768, 1024], P(('rep', 'shard'))
- loss: float32 [], replicated
- grad_x: float32 [32768, 1024], P(('rep', 'shard'))
- grad_w_qkv: float32 [1024, 3072], P('shard')
- grad_w_out: float32 [1024, 1024], P('shard')
- grad_w_upgate: float32 [1024, 8192], P('shard')
- grad_w_down: float32 [4096, 1024], P('shard')
- grad_s_qk: float32 [1024], P('shard')
- grad_alpha_attn: float32 [1024], P('shard')
- grad_s_up: float32 [4096], P('shard')
- grad_s_gate: float32 [4096], P('shard')
- grad_alpha_mlp: float32 [1024], P('shard')
Inputs may be any that keep to these rules, and one draw needn't show every extreme that they name: `segments`: in each sequence document numbers start at 0 at the first token, never fall, and every number up to 7 appears. Within a document positions rise by 1 or 2 from token to token; in each sequence the first document starts at position 0 and the last token has position 2046.
All inputs are finite; a program needn't handle non-finite values.
Results may differ from a plain program's by a relative error of at most 0.02.
Values may be sent and summed in bfloat16 or wider, within the bound.
No kernel may reach another device: no remote copies, remote signals or barrier semaphores. Data moves between devices by JAX's collectives and lax.ppermute only.
A program may use at most 384 MiB of HBM per device.

v0:
```python
from functools import partial
import math

import jax
import jax.numpy as jnp
from jax import lax
from jax.sharding import PartitionSpec as P

HEADS = 16


EPS = 1e-06


def row_norm(value):
    factor = lax.rsqrt(jnp.mean(value * value, axis=-1, keepdims=True) + EPS)
    return (value * factor, factor)


def norm_back(grad, normed, factor):
    return factor * (grad - normed * jnp.mean(grad * normed, axis=-1, keepdims=True))


def unit_heads(value):
    factor = lax.rsqrt(jnp.sum(value * value, axis=-1, keepdims=True) + EPS)
    return (value * factor, factor)


def unit_back(grad, unit, factor):
    return factor * (grad - unit * jnp.sum(grad * unit, axis=-1, keepdims=True))


def rotate(value, cosine, sine):
    half = value.shape[-1] // 2
    first = value[..., :half]
    second = value[..., half:]
    return jnp.concatenate(
        [first * cosine - second * sine, second * cosine + first * sine], axis=-1
    )


def rotary_tables(positions, head_dim):
    half = head_dim // 2
    freq = jnp.power(10000.0, -2.0 * jnp.arange(half, dtype=jnp.float32) / head_dim)
    angle = positions.astype(jnp.float32)[..., None] * freq
    return (jnp.cos(angle)[..., None, :], jnp.sin(angle)[..., None, :])


def regroup(value, axis, groups, copies):
    shape = value.shape
    width = shape[axis] // (groups * copies)
    parts = value.reshape(shape[:axis] + (groups, copies, width) + shape[axis + 1 :])
    return jnp.swapaxes(parts, axis, axis + 1).reshape(shape)


def body(
    tokens,
    teacher,
    valid,
    segments,
    positions,
    w_qkv,
    w_out,
    w_upgate,
    w_down,
    s_qk,
    alpha_attn,
    s_up,
    s_gate,
    alpha_mlp,
):
    shards = (w_qkv, w_out, w_upgate, w_down, s_qk, alpha_attn, s_up, s_gate, alpha_mlp)
    full = (
        lax.all_gather(shards[0], "shard", axis=0, tiled=True),
        lax.all_gather(shards[1], "shard", axis=0, tiled=True),
        lax.all_gather(shards[2], "shard", axis=0, tiled=True),
        lax.all_gather(shards[3], "shard", axis=0, tiled=True),
        lax.all_gather(shards[4], "shard", axis=0, tiled=True),
        lax.all_gather(shards[5], "shard", axis=0, tiled=True),
        lax.all_gather(shards[6], "shard", axis=0, tiled=True),
        lax.all_gather(shards[7], "shard", axis=0, tiled=True),
        lax.all_gather(shards[8], "shard", axis=0, tiled=True),
    )
    f_qkv, f_out, f_ug, f_down, f_sqk, f_aa, f_su, f_sg, f_am = full
    rows, width = tokens.shape
    seqs, length = segments.shape
    head_dim = width // HEADS
    ffw = f_down.shape[0]
    block = math.gcd(length, 512)
    temper = math.sqrt(head_dim)
    rep_count = lax.axis_size("rep")
    shard_count = lax.axis_size("shard")
    f32 = jnp.float32
    bf16 = jnp.bfloat16
    cosine, sine = rotary_tables(positions, head_dim)
    x_full = tokens.astype(f32)
    qkv = jnp.dot(tokens, f_qkv, preferred_element_type=f32).astype(bf16)
    heads_shape = (seqs, length, HEADS, head_dim)
    q_rot = rotate(qkv[:, :width].astype(f32).reshape(heads_shape), cosine, sine)
    k_rot = rotate(qkv[:, width : 2 * width].astype(f32).reshape(heads_shape), cosine, sine)
    values = qkv[:, 2 * width :].reshape(heads_shape)
    scale_qk = f_sqk.astype(f32).reshape(HEADS, head_dim)
    q_unit, q_factor = unit_heads(q_rot)
    k_unit, k_factor = unit_heads(k_rot)
    q_two = (q_unit * scale_qk).astype(bf16)
    k_two = (k_unit * scale_qk).astype(bf16)
    spots = jnp.arange(length)

    def scores_of(start):
        q_block = q_two[:, start : start + block]
        raw = jnp.einsum("sqhd,skhd->shqk", q_block, k_two, preferred_element_type=f32) * temper
        seg_rows = segments[:, start : start + block]
        causal = spots[start : start + block][:, None] >= spots[None, :]
        allowed = (seg_rows[:, :, None] == segments[:, None, :]) & causal[None]
        return (q_block, raw, allowed[:, None])

    pieces = []
    lse_list = []
    for start in range(0, length, block):
        q_block, raw, allowed = scores_of(start)
        masked = jnp.where(allowed, raw, -jnp.inf)
        peak = jnp.max(masked, axis=-1, keepdims=True)
        expo = jnp.exp(masked - peak)
        total = jnp.sum(expo, axis=-1, keepdims=True)
        probs = (expo / total).astype(bf16)
        lse_list.append(peak + jnp.log(total))
        pieces.append(
            jnp.einsum("shqk,skhd->sqhd", probs, values, preferred_element_type=f32).astype(bf16)
        )
    attended = jnp.concatenate(pieces, axis=1).reshape(rows, width)
    a_attn = f_aa.astype(f32)
    a_mlp = f_am.astype(f32)
    scale_up = f_su.astype(f32)
    scale_gate = f_sg.astype(f32)
    branch_a = jnp.dot(attended, f_out, preferred_element_type=f32)
    a_normed, a_factor = row_norm(branch_a)
    h_one, one_factor = row_norm(x_full + a_attn * (a_normed - x_full))
    h_low = h_one.astype(bf16)
    up_gate = jnp.dot(h_low, f_ug, preferred_element_type=f32)
    up_part = up_gate[:, :ffw]
    gate_part = up_gate[:, ffw:]
    gate_value = gate_part * scale_gate
    sigma = jax.nn.sigmoid(gate_value)
    active = jax.nn.silu(gate_value)
    hidden = (up_part * scale_up * active).astype(bf16)
    branch_m = jnp.dot(hidden, f_down, preferred_element_type=f32)
    m_normed, m_factor = row_norm(branch_m)
    h_two, two_factor = row_norm(h_one + a_mlp * (m_normed - h_one))
    output = h_two.astype(bf16)
    mask_f = valid.astype(f32)
    diff = h_two - teacher.astype(f32)
    count_all, loss_all = lax.psum(
        (jnp.sum(mask_f), jnp.sum(mask_f[:, None] * diff * diff)), ("rep", "shard")
    )
    count = jnp.maximum(count_all, 1.0)
    loss = loss_all / count
    scale = rows * rep_count * shard_count / count
    f_qkv, f_out, f_ug, f_down, f_sqk, f_aa, f_su, f_sg, f_am = (
        lax.all_gather(shards[0], "shard", axis=0, tiled=True),
        lax.all_gather(shards[1], "shard", axis=0, tiled=True),
        lax.all_gather(shards[2], "shard", axis=0, tiled=True),
        lax.all_gather(shards[3], "shard", axis=0, tiled=True),
        lax.all_gather(shards[4], "shard", axis=0, tiled=True),
        lax.all_gather(shards[5], "shard", axis=0, tiled=True),
        lax.all_gather(shards[6], "shard", axis=0, tiled=True),
        lax.all_gather(shards[7], "shard", axis=0, tiled=True),
        lax.all_gather(shards[8], "shard", axis=0, tiled=True),
    )
    order = partial(regroup, groups=1, copies=1)
    g_h2 = 2.0 * scale * mask_f[:, None] * diff
    g_z2 = norm_back(g_h2, h_two, two_factor)
    grad_am = jnp.sum(g_z2 * (m_normed - h_one), axis=0)
    g_bm = norm_back(g_z2 * a_mlp, m_normed, m_factor).astype(bf16)
    grad_wd = jnp.einsum("tf,td->fd", order(hidden, 1), g_bm, preferred_element_type=f32)
    g_hidden = jnp.einsum("td,fd->tf", g_bm, f_down, preferred_element_type=f32)
    grad_su = jnp.sum(g_hidden * up_part * active, axis=0)
    g_gv = g_hidden * up_part * scale_up * sigma * (1.0 + gate_value * (1.0 - sigma))
    grad_sg = jnp.sum(g_gv * gate_part, axis=0)
    g_ug = jnp.concatenate([g_hidden * active * scale_up, g_gv * scale_gate], axis=1).astype(bf16)
    grad_wug = jnp.einsum("td,tf->df", order(h_low, 1), g_ug, preferred_element_type=f32)
    g_h1 = g_z2 * (1.0 - a_mlp) + jnp.einsum("tf,df->td", g_ug, f_ug, preferred_element_type=f32)
    g_z1 = norm_back(g_h1, h_one, one_factor)
    grad_aa = jnp.sum(g_z1 * (a_normed - x_full), axis=0)
    g_ba = norm_back(g_z1 * a_attn, a_normed, a_factor).astype(bf16)
    grad_wo = jnp.einsum("td,te->de", order(attended, 1), g_ba, preferred_element_type=f32)
    g_att = (
        jnp.einsum("te,de->td", g_ba, f_out, preferred_element_type=f32)
        .astype(bf16)
        .reshape(heads_shape)
    )
    g_keys = jnp.zeros(heads_shape, f32)
    g_vals = jnp.zeros(heads_shape, f32)
    g_queries = []
    for index, start in enumerate(range(0, length, block)):
        q_block, raw, allowed = scores_of(start)
        probs_f = jnp.where(allowed, jnp.exp(raw - lse_list[index]), 0.0)
        g_block = g_att[:, start : start + block]
        g_probs = jnp.einsum("sqhd,skhd->shqk", g_block, values, preferred_element_type=f32)
        g_vals = g_vals + jnp.einsum(
            "shqk,sqhd->skhd", probs_f.astype(bf16), g_block, preferred_element_type=f32
        )
        spread = jnp.sum(probs_f * g_probs, axis=-1, keepdims=True)
        g_scores = (probs_f * (g_probs - spread)).astype(bf16)
        g_queries.append(
            jnp.einsum("shqk,skhd->sqhd", g_scores, k_two, preferred_element_type=f32) * temper
        )
        g_keys = (
            g_keys
            + jnp.einsum("shqk,sqhd->skhd", g_scores, q_block, preferred_element_type=f32) * temper
        )
    g_q2 = jnp.concatenate(g_queries, axis=1)
    grad_sqk = jnp.sum(g_q2 * q_unit + g_keys * k_unit, axis=(0, 1)).reshape(width)
    g_q_rot = unit_back(g_q2 * scale_qk, q_unit, q_factor)
    g_k_rot = unit_back(g_keys * scale_qk, k_unit, k_factor)
    g_q_raw = rotate(g_q_rot, cosine, -sine).reshape(rows, width)
    g_k_raw = rotate(g_k_rot, cosine, -sine).reshape(rows, width)
    g_qkv = jnp.concatenate([g_q_raw, g_k_raw, g_vals.reshape(rows, width)], axis=1).astype(bf16)
    grad_wqkv = jnp.einsum("td,te->de", order(tokens, 1), g_qkv, preferred_element_type=f32)
    grad_x = g_z1 * (1.0 - a_attn) + jnp.einsum(
        "te,de->td", g_qkv, f_qkv, preferred_element_type=f32
    )
    group_sum = (
        lax.psum_scatter(
            grad_wqkv.astype(jnp.bfloat16), "shard", scatter_dimension=0, tiled=True
        ).astype(jnp.float32),
        lax.psum_scatter(
            grad_wo.astype(jnp.bfloat16), "shard", scatter_dimension=0, tiled=True
        ).astype(jnp.float32),
        lax.psum_scatter(
            grad_wug.astype(jnp.bfloat16), "shard", scatter_dimension=0, tiled=True
        ).astype(jnp.float32),
        lax.psum_scatter(
            grad_wd.astype(jnp.bfloat16), "shard", scatter_dimension=0, tiled=True
        ).astype(jnp.float32),
        lax.psum_scatter(
            grad_sqk.astype(jnp.bfloat16), "shard", scatter_dimension=0, tiled=True
        ).astype(jnp.float32),
        lax.psum_scatter(
            grad_aa.astype(jnp.bfloat16), "shard", scatter_dimension=0, tiled=True
        ).astype(jnp.float32),
        lax.psum_scatter(
            grad_su.astype(jnp.bfloat16), "shard", scatter_dimension=0, tiled=True
        ).astype(jnp.float32),
        lax.psum_scatter(
            grad_sg.astype(jnp.bfloat16), "shard", scatter_dimension=0, tiled=True
        ).astype(jnp.float32),
        lax.psum_scatter(
            grad_am.astype(jnp.bfloat16), "shard", scatter_dimension=0, tiled=True
        ).astype(jnp.float32),
    )
    owned = (
        lax.psum(group_sum[0].astype(jnp.bfloat16), "rep").astype(jnp.float32),
        lax.psum(group_sum[1].astype(jnp.bfloat16), "rep").astype(jnp.float32),
        lax.psum(group_sum[2].astype(jnp.bfloat16), "rep").astype(jnp.float32),
        lax.psum(group_sum[3].astype(jnp.bfloat16), "rep").astype(jnp.float32),
        lax.psum(group_sum[4].astype(jnp.bfloat16), "rep").astype(jnp.float32),
        lax.psum(group_sum[5].astype(jnp.bfloat16), "rep").astype(jnp.float32),
        lax.psum(group_sum[6].astype(jnp.bfloat16), "rep").astype(jnp.float32),
        lax.psum(group_sum[7].astype(jnp.bfloat16), "rep").astype(jnp.float32),
        lax.psum(group_sum[8].astype(jnp.bfloat16), "rep").astype(jnp.float32),
    )
    return (
        output,
        loss,
        grad_x,
        owned[0],
        owned[1],
        owned[2],
        owned[3],
        owned[4],
        owned[5],
        owned[6],
        owned[7],
        owned[8],
    )


def solution(mesh):
    return jax.shard_map(
        body,
        mesh=mesh,
        in_specs=(
            P(("rep", "shard"), None),
            P(("rep", "shard"), None),
            P(("rep", "shard")),
            P(("rep", "shard"), None),
            P(("rep", "shard"), None),
            P("shard", None),
            P("shard", None),
            P("shard", None),
            P("shard", None),
            P("shard"),
            P("shard"),
            P("shard"),
            P("shard"),
            P("shard"),
        ),
        out_specs=(
            P(("rep", "shard"), None),
            P(),
            P(("rep", "shard"), None),
            P("shard", None),
            P("shard", None),
            P("shard", None),
            P("shard", None),
            P("shard"),
            P("shard"),
            P("shard"),
            P("shard"),
            P("shard"),
        ),
        check_vma=False,
    )
```

profile of v0, /device:TPU:0, one launch (start us, length us, event | category | flops | bytes accessed | tf_op | source)
XLA Modules:
  0.0 1245.0 jit_solution(13155853618179346191)
XLA Ops:
  14.6 36.4 %all-reduce.9 = (bf16[1024]{0:T(1024)(128)(2,1)S(1)}, bf16[1024]{0:T(1024)(128)(2,1)S(1)}, bf16[1024]{0:T(1024)(128)(2,1)S(1)}) all-reduce(bf16[1024]{0:T(1024)(128)(2,1)S(1)} %dynamic-update-slice.1, bf16[1024]{0:T(1024)(128)(2,1)S(1)} %dynamic-update-slice, ...), channel_id=1, replica_groups=mesh['rep'=2,'shard'=16] {'shard'}, use_global_device_ids=true, to_apply=%add.1 | all-reduce | flops 3072 | bytes 12288
  54.7 37.4 %psum.78 = f32[]{:T(128)} all-reduce(f32[]{:T(128)} %convert_reduce_fusion), channel_id=1, replica_groups=mesh['rep'=2,'shard'=16] {'rep','shard'}, use_global_device_ids=true, to_apply=%region_13.14 | all-reduce | flops 1 | bytes 8 | tf_op jit(solution)/shard_map/psum | solution.py:152
  98.1 21.1 %all-gather.1 = bf16[16,1,256]{2,1,0:T(2,128)(2,1)S(1)} all-gather(bf16[1,1,256]{2,1,0:T(2,128)(2,1)S(1)} %reshape.860), channel_id=1, replica_groups=mesh['rep'=2,'shard'=16] {'shard'}, dimensions={0}, use_global_device_ids=true | all-gather | bytes 8704 | tf_op jit(solution)/shard_map/all_gather | solution.py:81
  119.9 17.6 %all-gather = bf16[16,1,256]{2,1,0:T(2,128)(2,1)S(1)} all-gather(bf16[1,1,256]{2,1,0:T(2,128)(2,1)S(1)} %reshape.858), channel_id=1, replica_groups=mesh['rep'=2,'shard'=16] {'shard'}, dimensions={0}, use_global_device_ids=true | all-gather | bytes 8704 | tf_op jit(solution)/shard_map/all_gather | solution.py:80
  185.0 14.0 %select_reduce_fusion = (f32[16,512]{1,0:T(8,128)S(1)}, f32[16,512,1024]{2,1,0:T(8,128)}) fusion(pred[512,1024]{1,0:T(8,128)(4,1)S(1)} %get-tuple-element.103, bf16[1024,16,64]{0,2,1:T(8,128)(2,1)S(1)} %fusion.16, bf16[1,1024,16,64]{1,3,2,0:T(8,128)(2,1)S(1)} %multiply_convert_fusion.7), kind=kOutput, calls=%fused_computation.10 | convolution fusion | flops 1098899456 | bytes 37257216 | tf_op jit(solution)/shard_map/sqhd,skhd->shqk/dot_general | solution.py:111
  198.9 13.7 %select_reduce_fusion.1 = (f32[16,512]{1,0:T(8,128)S(1)}, f32[16,512,1024]{2,1,0:T(8,128)}) fusion(pred[512,1024]{1,0:T(8,128)(4,1)S(1)} %get-tuple-element.102, bf16[1024,16,64]{0,2,1:T(8,128)(2,1)S(1)} %fusion.16, bf16[1,1024,16,64]{1,3,2,0:T(8,128)(2,1)S(1)} %multiply_convert_fusion.7), kind=kOutput, calls=%fused_computation.11 | convolution fusion | flops 1098899456 | bytes 37257216 | tf_op jit(solution)/shard_map/sqhd,skhd->shqk/dot_general | solution.py:111
  212.7 15.1 %fusion.1 = f32[16,512]{1,0:T(8,128)S(1)} fusion(f32[16,512,1024]{2,1,0:T(8,128)} %get-tuple-element.109, f32[16,512]{1,0:T(8,128)S(1)} %get-tuple-element.108, pred[512,1024]{1,0:T(8,128)(4,1)S(1)} %get-tuple-element.103), kind=kLoop, calls=%fused_computation.13 | loop fusion | flops 33546240 | bytes 34144256 | tf_op jit(solution)/shard_map/reduce_sum | solution.py:124
  227.8 14.7 %fusion.30 = bf16[1,512,16,64]{1,3,2,0:T(8,128)(2,1)S(1)} fusion(bf16[1024,16,64]{0,2,1:T(8,128)(2,1)S(1)} %bitcast.121, f32[16,512,1024]{2,1,0:T(8,128)} %get-tuple-element.109, f32[16,512]{1,0:T(8,128)S(1)} %fusion.1, f32[16,512]{1,0:T(8,128)S(1)} %get-tuple-element.108, pred[512,1024]{1,0:T(8,128)(4,1)S(1)} %get-tuple-element.103), kind=kOutput, calls=%fused_computation.112 | convolution fusion | flops 1116209152 | bytes 37289984 | tf_op jit(solution)/shard_map/shqk,skhd->sqhd/dot_general | solution.py:128
  242.5 15.3 %fusion = f32[16,512]{1,0:T(8,128)S(1)} fusion(f32[16,512,1024]{2,1,0:T(8,128)} %get-tuple-element.111, f32[16,512]{1,0:T(8,128)S(1)} %get-tuple-element.110, pred[512,1024]{1,0:T(8,128)(4,1)S(1)} %get-tuple-element.102), kind=kLoop, calls=%fused_computation.12 | loop fusion | flops 33546240 | bytes 34144256 | tf_op jit(solution)/shard_map/reduce_sum | solution.py:124
  257.8 14.7 %fusion.29 = bf16[1,512,16,64]{1,3,2,0:T(8,128)(2,1)S(1)} fusion(bf16[1024,16,64]{0,2,1:T(8,128)(2,1)S(1)} %bitcast.122, f32[16,512,1024]{2,1,0:T(8,128)} %get-tuple-element.111, f32[16,512]{1,0:T(8,128)S(1)} %fusion, f32[16,512]{1,0:T(8,128)S(1)} %get-tuple-element.110, pred[512,1024]{1,0:T(8,128)(4,1)S(1)} %get-tuple-element.102), kind=kOutput, calls=%fused_computation.111 | convolution fusion | flops 1116209152 | bytes 37289984 | tf_op jit(solution)/shard_map/shqk,skhd->sqhd/dot_general | solution.py:128
  282.5 28.6 %fusion.36 = f32[1024,8192]{1,0:T(8,128)} fusion(bf16[1024,8192]{1,0:T(8,128)(2,1)} %all-gather.11.cloned.1.call-done, f32[1024,1024]{0,1:T(8,128)} %get-tuple-element.80, f32[1024]{0:T(1024)S(1)} %add_rsqrt_fusion.4), kind=kOutput, calls=%fused_computation.122 | convolution fusion | flops 17181966336 | bytes 54530048 | tf_op jit(solution)/shard_map/dot_general | solution.py:139
  311.2 15.4 %multiply_convert_fusion.4 = bf16[1024,4096]{1,0:T(8,128)(2,1)} fusion(f32[1024,8192]{1,0:T(8,128)} %fusion.36, f32[4096]{0:T(1024)S(1)} %bitcast.140, f32[4096]{0:T(1024)S(1)} %bitcast.137), kind=kLoop, calls=%fused_computation.22 | loop fusion | flops 33554432 | bytes 41975808 | tf_op jit(solution)/shard_map/convert_element_type | solution.py:145
  326.6 13.9 %multiply_reduce_fusion.12 = (f32[1024]{0:T(1024)S(1)}, f32[1024,1024]{0,1:T(8,128)S(1)}) fusion(bf16[1024,4096]{1,0:T(8,128)(2,1)} %multiply_convert_fusion.4, bf16[4096,1024]{1,0:T(8,128)(2,1)} %all-gather.13.cloned.1.call-done), kind=kOutput, calls=%fused_computation.76 | convolution fusion | flops 8592030720 | bytes 20975616 | tf_op jit(solution)/shard_map/dot_general | solution.py:146
  351.3 32.2 %multiply_reduce_fusion.2 = (bf16[4096]{0:T(1024)(128)(2,1)}, bf16[4096]{0:T(1024)(128)(2,1)}, f32[1024,4096]{1,0:T(8,128)}, bf16[1024,4096]{1,0:T(8,128)(2,1)}) fusion(f32[1024,8192]{1,0:T(8,128)} %fusion.36, f32[4096]{0:T(1024)S(1)} %bitcast.138, f32[4096]{0:T(1024)S(1)} %bitcast.141, bf16[1024,1024]{0,1:T(8,128)(2,1)} %get-tuple-element.93, ...), kind=kOutput, calls=%fused_computation.17 | convolution fusion | flops 8669618176 | bytes 69255168 | tf_op jit(solution)/shard_map/td,fd->tf/dot_general | solution.py:175
  394.2 27.5 %multiply_reduce_fusion.8 = (f32[1024]{0:T(1024)S(1)}, f32[1024,1024]{0,1:T(8,128)}) fusion(f32[1024,1024]{0,1:T(8,128)S(1)} %copy-done.3, f32[1024]{0:T(1024)S(1)} %add_rsqrt_fusion.4, bf16[1024,8192]{1,0:T(8,128)(2,1)} %all-gather.11.cloned.1.call-done, bf16[1024,4096]{1,0:T(8,128)(2,1)} %multiply_convert_fusion.2, ...), kind=kOutput, calls=%fused_computation.67 | convolution fusion | flops 17226006528 | bytes 48259072 | tf_op jit(solution)/shard_map/tf,df->td/dot_general | solution.py:181
  434.8 15.8 %fusion.5 = f32[16,64,1024]{2,1,0:T(8,128)} fusion(f32[16,512,1024]{2,1,0:T(8,128)} %get-tuple-element.109, f32[16,512]{1,0:T(8,128)S(1)} %copy-done.46, pred[512,1024]{1,0:T(8,128)(4,1)S(1)} %copy-done.23, bf16[1,1024,16,64]{1,3,2,0:T(8,128)(2,1)S(1)} %bitcast.127), kind=kOutput, calls=%fused_computation.25 | convolution fusion | flops 1107296256 | bytes 39354368 | tf_op jit(solution)/shard_map/shqk,sqhd->skhd/dot_general | solution.py:199
  450.6 25.3 %multiply_reduce_fusion = (f32[16,512]{1,0:T(8,128)S(1)}, f32[16,512,1024]{2,1,0:T(8,128)}) fusion(f32[16,512,1024]{2,1,0:T(8,128)} %get-tuple-element.109, f32[16,512]{1,0:T(8,128)S(1)} %copy-done.46, pred[512,1024]{1,0:T(8,128)(4,1)S(1)} %copy-done.23, bf16[1024,16,64]{0,2,1:T(8,128)(2,1)S(1)} %bitcast.123, bf16[1,1024,16,64]{1,3,2,0:T(8,128)(2,1)} %bitcast.128), kind=kOutput, calls=%fused_computation.1 | convolution fusion | flops 1115676672 | bytes 70844416 | tf_op jit(solution)/shard_map/sqhd,skhd->shqk/dot_general | solution.py:198
  475.9 25.7 %multiply_reduce_fusion.1 = (f32[16,512]{1,0:T(8,128)S(1)}, f32[16,512,1024]{2,1,0:T(8,128)}) fusion(f32[16,512,1024]{2,1,0:T(8,128)} %get-tuple-element.111, f32[16,512]{1,0:T(8,128)S(1)} %copy-done.45, pred[512,1024]{1,0:T(8,128)(4,1)S(1)} %copy-done.21, bf16[1024,16,64]{0,2,1:T(8,128)(2,1)S(1)} %bitcast.124, bf16[1,1024,16,64]{1,3,2,0:T(8,128)(2,1)S(1)} %bitcast.130), kind=kOutput, calls=%fused_computation.4 | convolution fusion | flops 1115676672 | bytes 70844416 | tf_op jit(solution)/shard_map/sqhd,skhd->shqk/dot_general | solution.py:198
  501.6 54.9 %multiply_convert_fusion = (bf16[16,512,1024]{2,1,0:T(8,128)(2,1)}, bf16[16,512,1024]{2,1,0:T(8,128)(2,1)}) fusion(f32[16,512,1024]{2,1,0:T(8,128)} %get-tuple-element.119, f32[16,512,1024]{2,1,0:T(8,128)} %get-tuple-element.109, f32[16,512]{1,0:T(8,128)S(1)} %get-tuple-element.118, f32[16,512]{1,0:T(8,128)S(1)} %copy-done.46, ...), kind=kLoop, calls=%fused_computation | loop fusion | flops 100663296 | bytes 168951808 | tf_op jit(solution)/shard_map/convert_element_type | solution.py:203
  580.0 17.7 %add_convert_fusion = bf16[16,64,1024]{2,1,0:T(8,128)(2,1)} fusion(f32[16,64,1024]{2,1,0:T(8,128)} %fusion.5, f32[16,512,1024]{2,1,0:T(8,128)} %get-tuple-element.111, f32[16,512]{1,0:T(8,128)S(1)} %copy-done.45, pred[512,1024]{1,0:T(8,128)(4,1)S(1)} %copy-done.21, bf16[1,1024,16,64]{1,3,2,0:T(8,128)(2,1)} %bitcast.129), kind=kOutput, calls=%fused_computation.60 | convolution fusion | flops 1109393408 | bytes 41451520 | tf_op jit(solution)/shard_map/shqk,sqhd->skhd/dot_general | solution.py:199
  597.7 12.3 multiply_bitcast_fusion
  610.0 16.0 %fusion.18 = (bf16[16,64]{1,0:T(8,128)(2,1)S(1)}, f32[1024,16]{0,1:T(8,128)S(1)}, f32[1024,16]{0,1:T(8,128)S(1)}, f32[16,64,1024]{2,1,0:T(8,128)}) fusion(f32[1,512,16,64]{1,3,2,0:T(8,128)} %multiply_bitcast_fusion, f32[1,512,16,64]{1,3,2,0:T(8,128)} %multiply_bitcast_fusion.1, f32[1024,16]{0,1:T(8,128)S(1)} %copy-done.41, ...), kind=kOutput, calls=%fused_computation.51 | convolution fusion | flops 1091533824 | bytes 39069696 | tf_op jit(solution)/shard_map/shqk,sqhd->skhd/dot_general | solution.py:209
  636.8 13.9 %convert_bitcast_fusion = bf16[1024,3072]{0,1:T(8,128)(2,1)} fusion(bf16[1024,1024]{1,0:T(8,128)(2,1)S(1)} %copy-done.32, bf16[1024,1024]{0,1:T(8,128)(2,1)S(1)} %bitcast.147, bf16[1024,1024]{0,1:T(8,128)(2,1)S(1)} %bitcast.135, bf16[1024,1024]{0,1:T(8,128)(2,1)S(1)} %bitcast.133), kind=kOutput, calls=%fused_computation.37 | convolution fusion | flops 6464471040 | bytes 14680064 | tf_op jit(solution)/shard_map/td,te->de/dot_general | solution.py:218
  666.3 16.0 %convolution_convert_fusion.1 = bf16[4096,1024]{1,0:T(8,128)(2,1)} fusion(bf16[1024,4096]{1,0:T(8,128)(2,1)} %multiply_convert_fusion.4, bf16[1024,1024]{0,1:T(8,128)(2,1)} %get-tuple-element.93), kind=kOutput, calls=%fused_computation.35 | convolution fusion | flops 8594128896 | bytes 18874368 | tf_op jit(solution)/shard_map/tf,td->fd/dot_general | solution.py:174
  682.9 24.8 %convolution_convert_fusion = bf16[1024,8192]{1,0:T(8,128)(2,1)} fusion(bf16[1024,4096]{1,0:T(8,128)(2,1)} %multiply_convert_fusion.2, bf16[1024,4096]{1,0:T(8,128)(2,1)} %get-tuple-element.81, f32[1024,1024]{0,1:T(8,128)} %get-tuple-element.80, f32[1024]{0:T(1024)S(1)} %copy-done.53), kind=kOutput, calls=%fused_computation.33 | convolution fusion | flops 17223909376 | bytes 37752832 | tf_op jit(solution)/shard_map/td,tf->df/dot_general | solution.py:180
  707.9 35.7 %reduce-scatter.13.cloned.1.call-done = bf16[64,3072]{1,0:T(8,128)(2,1)} async-done(((bf16[1024,3072]{1,0:T(8,128)(2,1)}), bf16[64,3072]{1,0:T(8,128)(2,1)}) %reduce-scatter.13.cloned.1.call-update) | async-done | bytes 393232
  745.7 63.2 %reduce-scatter.7.cloned.1.call-done = bf16[64,1024]{1,0:T(8,128)(2,1)} async-done(((bf16[1024,1024]{1,0:T(8,128)(2,1)}), bf16[64,1024]{1,0:T(8,128)(2,1)}) %reduce-scatter.7.cloned.1.call-update) | async-done | bytes 131088 | tf_op jit(solution)/shard_map/reduce_scatter | solution.py:226
  808.9 107.8 %reduce-scatter.11.cloned.1.call-done = bf16[256,1024]{1,0:T(8,128)(2,1)} async-done(((bf16[4096,1024]{1,0:T(8,128)(2,1)}), bf16[256,1024]{1,0:T(8,128)(2,1)}) %reduce-scatter.11.cloned.1.call-update) | async-done | bytes 524304 | tf_op jit(solution)/shard_map/reduce_scatter | solution.py:232
  916.7 182.5 %reduce-scatter.9.cloned.1.call-done = bf16[64,8192]{1,0:T(8,128)(2,1)} async-done(((bf16[1024,8192]{1,0:T(8,128)(2,1)}), bf16[64,8192]{1,0:T(8,128)(2,1)}) %reduce-scatter.9.cloned.1.call-update) | async-done | bytes 1048592 | tf_op jit(solution)/shard_map/reduce_scatter | solution.py:229
  1100.6 39.7 %psum.77 = f32[]{:T(128)} all-reduce(f32[]{:T(128)} %get-tuple-element.57), channel_id=1, replica_groups=mesh['rep'=2,'shard'=16] {'rep','shard'}, use_global_device_ids=true, to_apply=%region_11.12 | all-reduce | flops 1 | bytes 8 | tf_op jit(solution)/shard_map/psum | solution.py:152
  1143.6 59.8 %all-reduce.8 = (bf16[1024]{0:T(1024)(128)(2,1)S(1)}, bf16[1024]{0:T(1024)(128)(2,1)S(1)}, bf16[4096]{0:T(1024)(128)(2,1)S(1)}, bf16[4096]{0:T(1024)(128)(2,1)S(1)}, bf16[1024]{0:T(1024)(128)(2,1)S(1)}) all-reduce(bf16[1024]{0:T(1024)(128)(2,1)S(1)} %convert_element_type.229, ...), channel_id=6, replica_groups=mesh['rep'=2,'shard'=16] {'shard'}, use_global_device_ids=true, to_apply=%region_31.32.clone | all-reduce | flops 11264 | bytes 45056
  1211.4 12.6 %multiply_add_fusion = f32[1024,1024]{0,1:T(8,128)} fusion(f32[1024,1024]{0,1:T(8,128)} %copy-done.27, f32[1024]{0:T(1024)S(1)} %broadcast_subtract_fusion, bf16[1024,3072]{1,0:T(8,128)(2,1)} %all-gather.7.cloned.1.call-done, bf16[1024,1024]{0,1:T(8,128)(2,1)} %bitcast.146, bf16[1024,1024]{0,1:T(8,128)(2,1)} %bitcast.136, bf16[1024,1024]{0,1:T(8,128)(2,1)} %bitcast.134), kind=kOutput, calls=%fused_computation.65 | convolution fusion | flops 6463422464 | bytes 20975616 | tf_op jit(solution)/shard_map/te,de->td/dot_general | solution.py:219
  (259 shorter events, 184.1 us)
Async XLA Ops:
  7.2 134.9 %copy-start.31 = (bf16[1024,1024]{1,0:T(8,128)(2,1)S(1)}, bf16[1024,1024]{1,0:T(8,128)(2,1)}, u32[]{:S(2)}) copy-start(bf16[1024,1024]{1,0:T(8,128)(2,1)} %param.14) | copy-start | bytes 6291460
  7.2 139.8 %all-gather.7.cloned.1.call-start = ((), (), s32[]{:S(2)}) async-start(), calls=%async_computation.4 | async-start | bytes 6684672 | tf_op jit(solution)/shard_map/all_gather | solution.py:74
  7.9 264.9 %all-gather.9.cloned.1.call-start = ((), (), s32[]{:S(2)}) async-start(), calls=%async_computation.5 | async-start | bytes 2228224 | tf_op jit(solution)/shard_map/all_gather | solution.py:75
  8.7 273.8 %all-gather.11.cloned.1.call-start = ((), (), s32[]{:S(2)}) async-start(), calls=%async_computation.6 | async-start | bytes 17825792 | tf_op jit(solution)/shard_map/all_gather | solution.py:76
  9.4 317.2 %all-gather.13.cloned.1.call-start = ((), (), s32[]{:S(2)}) async-start(), calls=%async_computation.7 | async-start | bytes 8912896 | tf_op jit(solution)/shard_map/all_gather | solution.py:77
  10.0 733.6 %reduce-scatter.13.cloned.1.call-start = ((), (), s32[]{:S(2)}) async-start(), calls=%async_computation.11 | async-start | bytes 6684672
  51.0 45.1 %copy-start.65 = (bf16[1024]{0:T(1024)(128)(2,1)}, bf16[1024]{0:T(1024)(128)(2,1)S(1)}, u32[]{:S(2)}) copy-start(bf16[1024]{0:T(1024)(128)(2,1)S(1)} %get-tuple-element.64) | copy-start | bytes 6148
  97.5 85.9 %copy-start.48 = (f32[16,64]{1,0:T(8,128)}, f32[16,64]{1,0:T(8,128)S(1)}, u32[]{:S(2)}) copy-start(f32[16,64]{1,0:T(8,128)S(1)} %reshape.846) | copy-start | bytes 12292
  145.8 30.4 %copy-start.38 = (f32[1024,32]{0,1:T(8,128)}, f32[1024,32]{0,1:T(8,128)S(1)}, u32[]{:S(2)}) copy-start(f32[1024,32]{0,1:T(8,128)S(1)} %get-tuple-element.101) | copy-start | bytes 393220
  147.0 80.8 %copy-start.22 = (pred[512,1024]{1,0:T(8,128)(4,1)}, pred[512,1024]{1,0:T(8,128)(4,1)S(1)}, u32[]{:S(2)}) copy-start(pred[512,1024]{1,0:T(8,128)(4,1)S(1)} %get-tuple-element.103) | copy-start | bytes 1572868
  147.0 110.8 %copy-start.20 = (pred[512,1024]{1,0:T(8,128)(4,1)}, pred[512,1024]{1,0:T(8,128)(4,1)S(1)}, u32[]{:S(2)}) copy-start(pred[512,1024]{1,0:T(8,128)(4,1)S(1)} %get-tuple-element.102) | copy-start | bytes 1572868
  169.8 88.0 %copy-start.15 = (bf16[1024,1024]{0,1:T(8,128)(2,1)}, bf16[1024,1024]{0,1:T(8,128)(2,1)S(1)}, u32[]{:S(2)}) copy-start(bf16[1024,1024]{0,1:T(8,128)(2,1)S(1)} %copy.50) | copy-start | bytes 6291460
  281.3 140.4 %copy-start.52 = (f32[1024]{0:T(1024)}, f32[1024]{0:T(1024)S(1)}, u32[]{:S(2)}) copy-start(f32[1024]{0:T(1024)S(1)} %add_rsqrt_fusion.4) | copy-start | bytes 12292
  282.5 28.6 %copy-start.50 = (f32[16,1,256]{2,1,0:T(1,128)S(1)}, f32[16,1,256]{2,1,0:T(1,128)}, u32[]{:S(2)}) copy-start(f32[16,1,256]{2,1,0:T(1,128)} %convert_element_type.240) | copy-start | bytes 49156
  282.5 28.6 %copy-start.58 = (f32[16,1,256]{2,1,0:T(1,128)S(1)}, f32[16,1,256]{2,1,0:T(1,128)}, u32[]{:S(2)}) copy-start(f32[16,1,256]{2,1,0:T(1,128)} %convert_element_type.239) | copy-start | bytes 49156
  394.2 27.5 %copy-start.55 = (f32[1024]{0:T(1024)S(1)}, f32[1024]{0:T(1024)}, u32[]{:S(2)}) copy-start(f32[1024]{0:T(1024)} %convert_element_type.191) | copy-start | bytes 12292
  394.2 27.5 %copy-start.57 = (f32[1024]{0:T(1024)S(1)}, f32[1024]{0:T(1024)}, u32[]{:S(2)}) copy-start(f32[1024]{0:T(1024)} %copy-done.56) | copy-start | bytes 12292
  450.6 25.3 %copy-start.21 = (pred[512,1024]{1,0:T(8,128)(4,1)S(1)}, pred[512,1024]{1,0:T(8,128)(4,1)}, u32[]{:S(2)}) copy-start(pred[512,1024]{1,0:T(8,128)(4,1)} %copy-done.20) | copy-start | bytes 1572868
  450.6 25.3 %copy-start.30 = (bf16[1024,1024]{0,1:T(8,128)(2,1)S(1)}, bf16[1024,1024]{0,1:T(8,128)(2,1)}, u32[]{:S(2)}) copy-start(bf16[1024,1024]{0,1:T(8,128)(2,1)} %copy-done.29) | copy-start | bytes 6291460
  450.6 25.3 %copy-start.45 = (f32[16,512]{1,0:T(8,128)S(1)}, f32[16,512]{1,0:T(8,128)}, u32[]{:S(2)}) copy-start(f32[16,512]{1,0:T(8,128)} %log_add_fusion.1) | copy-start | bytes 98308
  501.6 54.9 %copy-start.1 = (bf16[1024,16,64]{0,2,1:T(8,128)(2,1)S(1)}, bf16[1024,16,64]{0,2,1:T(8,128)(2,1)}, u32[]{:S(2)}) copy-start(bf16[1024,16,64]{0,2,1:T(8,128)(2,1)} %copy-done) | copy-start | bytes 6291460
  610.0 16.0 %copy-start.10 = (f32[1,1024,16,32]{1,3,2,0:T(8,128)S(1)}, f32[1,1024,16,32]{1,3,2,0:T(8,128)}, u32[]{:S(2)}) copy-start(f32[1,1024,16,32]{1,3,2,0:T(8,128)} %copy-done.9) | copy-start | bytes 6291460
  659.4 149.6 %reduce-scatter.7.cloned.1.call-start = ((), (), s32[]{:S(2)}) async-start(), calls=%async_computation.8 | async-start | bytes 2228224 | tf_op jit(solution)/shard_map/reduce_scatter | solution.py:226
  666.2 250.5 %reduce-scatter.11.cloned.1.call-start = ((), (), s32[]{:S(2)}) async-start(), calls=%async_computation.10 | async-start | bytes 8912896 | tf_op jit(solution)/shard_map/reduce_scatter | solution.py:232
  682.3 417.0 %reduce-scatter.9.cloned.1.call-start = ((), (), s32[]{:S(2)}) async-start(), calls=%async_computation.9 | async-start | bytes 17825792 | tf_op jit(solution)/shard_map/reduce_scatter | solution.py:229
  707.8 392.8 %copy-start.66 = (bf16[1024]{0:T(1024)(128)(2,1)S(1)}, bf16[1024]{0:T(1024)(128)(2,1)}, u32[]{:S(2)}) copy-start(bf16[1024]{0:T(1024)(128)(2,1)} %copy-done.65) | copy-start | bytes 6148
  707.8 433.1 %copy-start.28 = (bf16[1024,1024]{0,1:T(8,128)(2,1)S(1)}, bf16[1024,1024]{0,1:T(8,128)(2,1)}, u32[]{:S(2)}) copy-start(bf16[1024,1024]{0,1:T(8,128)(2,1)} %get-tuple-element.94) | copy-start | bytes 6291460
  707.8 435.8 %copy-start.63 = (bf16[1024]{0:T(1024)(128)(2,1)S(1)}, bf16[1024]{0:T(1024)(128)(2,1)}, u32[]{:S(2)}) copy-start(bf16[1024]{0:T(1024)(128)(2,1)} %get-tuple-element.50) | copy-start | bytes 6148
  707.8 435.8 %copy-start.64 = (bf16[1024]{0:T(1024)(128)(2,1)S(1)}, bf16[1024]{0:T(1024)(128)(2,1)}, u32[]{:S(2)}) copy-start(bf16[1024]{0:T(1024)(128)(2,1)} %get-tuple-element.55) | copy-start | bytes 6148
  707.8 435.8 %copy-start.67 = (bf16[4096]{0:T(1024)(128)(2,1)S(1)}, bf16[4096]{0:T(1024)(128)(2,1)}, u32[]{:S(2)}) copy-start(bf16[4096]{0:T(1024)(128)(2,1)} %get-tuple-element.48) | copy-start | bytes 24580
  707.8 435.8 %copy-start.68 = (bf16[4096]{0:T(1024)(128)(2,1)S(1)}, bf16[4096]{0:T(1024)(128)(2,1)}, u32[]{:S(2)}) copy-start(bf16[4096]{0:T(1024)(128)(2,1)} %get-tuple-element.49) | copy-start | bytes 24580
  707.8 521.5 %all-reduce.14.cloned.1.call-start = ((), (), s32[]{:S(2)}) async-start(), calls=%async_computation.12 | async-start | bytes 4980736 | tf_op jit(solution)/shard_map/psum | solution.py:252
  (49 other events, 292.6 us)
Sparse Core Ops, SparseCore 0:
  10.3 65.4 all-gather.6
  78.0 40.3 all-gather.8
  120.5 125.6 all-gather.10
  248.3 73.1 all-gather.12
  659.5 84.0 reduce-scatter.12
  748.2 60.6 reduce-scatter.6
  813.0 103.7 reduce-scatter.10
  920.9 178.3 reduce-scatter.8
  1102.3 71.6 all-reduce.13
where the time goes:
time: 1260 us; the launch traced here: 1250 us
  waiting for transfers between devices  392 us (31%)
  matrix products  385 us (31%)
  blocking collectives  217 us (17%)
  other arithmetic  170 us (13%)
  local copies, waits for them, and re-layouts  61.2 us (5%)
  between operations  19.6 us (2%)
    reduce_scatter x1, waiting for transfers between devices, body(): lax.psum_scatter(grad_wug.astype(jnp.bfloat16), 'shard', scatter_dimensio...  182 us
    reduce_scatter x1, waiting for transfers between devices, body(): lax.psum_scatter(grad_wd.astype(jnp.bfloat16), 'shard', scatter_dimension...  108 us
    unnamed x2, blocking collectives  96.2 us
    psum x2, blocking collectives, body(): lax.psum((jnp.sum(mask_f), jnp.sum(mask_f[:, None] * diff * diff)), ('rep...  77.1 us
    reduce_scatter x1, waiting for transfers between devices, body(): lax.psum_scatter(grad_wo.astype(jnp.bfloat16), 'shard', scatter_dimension...  63.2 us
    convert_element_type x1, other arithmetic, body(): g_scores = (probs_f * (g_probs - spread)).astype(bf16)  54.9 us
    dot_general x2, matrix products, body(): jnp.einsum('sqhd,skhd->shqk', g_block, values, preferred_element_type=f32)  50.9 us
    unnamed x165, local copies, waits for them, and re-layouts  45.8 us
  transfers between devices with their start and end apart: 9, of which 4 were waited for; matrix products, arithmetic and copies ran while one was open for 22% of the time, Pallas kernels for 0%

commit v1 on v0

v1 whole, which is shorter than its diff:
```python
from functools import partial
import math

import jax
import jax.numpy as jnp
from jax import lax
from jax.experimental import pallas as pl
from jax.experimental.pallas import tpu as pltpu
from jax.sharding import PartitionSpec as P

EPS = 1e-06
AXES = ("rep", "shard")
NZ = 4
NC = 2


class Place:
    def __init__(self):
        self.reps = lax.axis_size("rep")
        self.shards = lax.axis_size("shard")
        self.nx = self.shards // (NZ * NC)
        self.pairs = self.reps % 2 == 0
        rep = lax.axis_index("rep")
        shard = lax.axis_index("shard")
        self.rep = rep
        self.shard = shard
        self.y = rep % 2
        self.core = shard % NC
        self.x = (shard // NC) % self.nx
        self.z = shard // (NC * self.nx)

    def moves(self, step):
        pairs = []
        for rep in range(self.reps):
            for z in range(NZ):
                for x in range(self.nx):
                    for core in range(NC):
                        to_rep, to_z, to_x, to_core = step(rep, z, x, core)
                        pairs.append(
                            (
                                rep * self.shards + (z * self.nx + x) * NC + core,
                                to_rep * self.shards + (to_z * self.nx + to_x) * NC + to_core,
                            )
                        )
        return pairs

    def near_z(self, value):
        return lax.ppermute(value, AXES, self.moves(lambda r, z, x, c: (r, z ^ 1, x, c)))

    def far_z(self, value):
        return lax.ppermute(value, AXES, self.moves(lambda r, z, x, c: (r, z ^ (2 + r % 2), x, c)))

    def along_x(self, value, j):
        return lax.ppermute(value, AXES, self.moves(lambda r, z, x, c: (r, z, x ^ j, c)))

    def along_y(self, value):
        return lax.ppermute(value, AXES, self.moves(lambda r, z, x, c: (r ^ 1, z, x, c)))

    def other_core(self, value):
        return lax.ppermute(value, AXES, self.moves(lambda r, z, x, c: (r, z, x, c ^ 1)))

    def flat(self, value, bit):
        count = self.reps * self.shards
        return lax.ppermute(value, AXES, [(i, i ^ bit) for i in range(count)])

    def slot(self, k, j):
        return (self.z ^ k) * self.nx + (self.x ^ j)


def tie(*values):
    return lax.optimization_barrier(values)


def place_kernel(count, slots, *refs):
    pieces, out = refs[:-1], refs[-1]
    for i in range(count):
        rows = pieces[i].shape[0]
        at = pl.multiple_of(slots[i] * rows, rows)
        out[pl.ds(at, rows), :] = pieces[i][...]


def assemble(pieces, slots, rows_out):
    cols = pieces[0].shape[1]
    size = rows_out * cols * pieces[0].dtype.itemsize
    return pl.pallas_call(
        partial(place_kernel, len(pieces)),
        out_shape=jax.ShapeDtypeStruct((rows_out, cols), pieces[0].dtype),
        in_specs=[pl.BlockSpec(memory_space=pltpu.SMEM)]
        + [pl.BlockSpec(memory_space=pltpu.VMEM)] * len(pieces),
        out_specs=pl.BlockSpec(memory_space=pltpu.VMEM),
        compiler_params=pltpu.CompilerParams(vmem_limit_bytes=2 * size + (4 << 20)),
        cost_estimate=pl.CostEstimate(flops=0, bytes_accessed=2 * size, transcendentals=0),
    )(slots, *pieces)


def weave_kernel(core, half, other, out, sems):
    at = core[0]
    first = pltpu.make_async_copy(half, out.at[:, at], sems.at[0])
    second = pltpu.make_async_copy(other, out.at[:, 1 - at], sems.at[1])
    first.start()
    second.start()
    first.wait()
    second.wait()


def weave(half, other, core, groups):
    rows, cols = half.shape
    each = rows // groups
    size = rows * cols * half.dtype.itemsize
    shape = (groups, each, cols)
    full = pl.pallas_call(
        weave_kernel,
        out_shape=jax.ShapeDtypeStruct((groups, 2, each, cols), half.dtype),
        in_specs=[
            pl.BlockSpec(memory_space=pltpu.SMEM),
            pl.BlockSpec(memory_space=pltpu.VMEM),
            pl.BlockSpec(memory_space=pltpu.VMEM),
        ],
        out_specs=pl.BlockSpec(memory_space=pl.ANY),
        scratch_shapes=[pltpu.SemaphoreType.DMA((2,))],
        compiler_params=pltpu.CompilerParams(vmem_limit_bytes=2 * size + (4 << 20)),
        cost_estimate=pl.CostEstimate(flops=0, bytes_accessed=4 * size, transcendentals=0),
    )(core, half.reshape(shape), other.reshape(shape))
    return full.reshape(2 * rows, cols)


class Gather:
    def __init__(self, at, chunks):
        self.at = at
        self.ready = list(chunks)
        self.near, self.far, self.over_x, self.over_y = {}, {}, {}, {}
        self.own, self.other = {}, {}
        self.groups = NZ * at.nx
        self.core = at.core.reshape(1).astype(jnp.int32)

    def tick(self, tick, gate):
        at = self.at
        count = len(self.ready)
        offsets = range(1, at.nx)
        y = at.y
        ended = []
        if tick < count:
            piece = after(self.ready[tick], gate)
            self.ready[tick] = piece
            self.near[tick] = at.near_z(piece)
            self.far[tick] = at.far_z(piece)
            ended += [self.near[tick], self.far[tick]]
        i = tick - 1
        if 0 <= i < count:
            piece = self.ready[i]
            rows = piece.shape[0]
            half = lax.dynamic_slice_in_dim(piece, y * (rows // 2), rows // 2, axis=0)
            send = after(jnp.concatenate([half, self.near[i], self.far[i]], axis=0), gate)
            self.over_x[i] = [at.along_x(send, j) for j in offsets]
            ended += self.over_x[i]
        i = tick - 2
        if 0 <= i < count:
            rows = self.ready[i].shape[0]
            sends = [self.far[i]]
            for got in self.over_x[i]:
                sends += [got[: rows // 2], got[rows // 2 + rows :]]
            self.over_y[i] = at.along_y(after(jnp.concatenate(sends, axis=0), gate))
            ended += [self.over_y[i]]
        i = tick - 3
        if 0 <= i < count:
            rows = self.ready[i].shape[0]
            half = rows // 2
            got = self.over_y[i]
            pieces = [self.ready[i], self.near[i], self.far[i], got[:rows]]
            slots = [at.slot(0, 0), at.slot(1, 0), at.slot(2 + y, 0), at.slot(3 - y, 0)]
            place = rows
            for mine, j in zip(self.over_x[i], offsets):
                pieces += [mine[:half], mine[half : half + rows], mine[half + rows :]]
                slots += [at.slot(0, j) * 2 + y, at.slot(1, j), at.slot(2 + y, j)]
                pieces += [got[place : place + half], got[place + half : place + half + rows]]
                slots += [at.slot(0, j) * 2 + (1 - y), at.slot(3 - y, j)]
                place += half + rows
            self.own[i] = assemble(pieces, jnp.stack(slots).astype(jnp.int32), self.groups * rows)
            self.other[i] = at.other_core(after(self.own[i], gate))
            ended += [self.other[i]]
        return ended

    def full(self, i):
        return weave(self.own[i], self.other[i], self.core, self.groups)


def after(value, gate):
    return tie(value, *gate)[0] if gate else value


class Reduce:
    def __init__(self, at, send, keep):
        self.at = at
        self.send = send
        self.keep = keep
        self.rows = keep.shape[0] // (NZ * at.nx)
        self.stage = 0

    def add(self, places, extras=()):
        slots = [self.at.slot(k, j) for k, j in places]
        return add_slots(self.keep, self.got, self.rows, slots, extras)

    def step(self, gate):
        at = self.at
        offsets = range(1, at.nx)
        y = at.y
        stage = self.stage
        self.stage += 1
        if stage == 0:
            self.got = at.other_core(after(self.send, gate))
            return [self.got]
        if stage == 1:
            send = self.add([(3 - y, j) for j in range(at.nx)])
            self.got_y = at.along_y(after(send, gate))
            return [self.got_y]
        if stage == 2:
            self.got_x = []
            for j in offsets:
                send = self.add([(0, j), (1, j), (2 + y, j)], [(self.got_y, [None, None, j])])
                self.got_x.append(at.along_x(after(send, gate), j))
            return self.got_x
        if stage == 3:
            near = self.add([(1, 0)], [(g, [1]) for g in self.got_x])
            far = self.add([(2 + y, 0)], [(self.got_y, [0])] + [(g, [2]) for g in self.got_x])
            self.near = at.near_z(after(near, gate))
            self.far = at.far_z(after(far, gate))
            return [self.near, self.far]
        if stage == 4:
            terms = [(self.near, [0]), (self.far, [0])] + [(g, [0]) for g in self.got_x]
            self.mine = after(self.add([(0, 0)], terms), gate)
            self.last = at.along_y(self.mine)
            return [self.last]
        return []

    def total(self):
        return over_copies(self.at, self.mine.astype(jnp.float32) + self.last.astype(jnp.float32), 2)


def over_copies(at, total, bit):
    while bit < at.reps:
        total = total + at.flat(total.astype(jnp.bfloat16), bit * at.shards).astype(jnp.float32)
        bit *= 2
    return total


def sum_everywhere(at, value):
    bit = 1
    while bit < at.reps * at.shards:
        value = value + at.flat(value, bit)
        bit *= 2
    return value


def gather_vectors(at, vectors):
    sizes = [v.shape[0] for v in vectors]
    flat = jnp.concatenate(vectors)
    length = -(-flat.shape[0] // 128) * 128
    flat = jnp.pad(flat, (0, length - flat.shape[0])).reshape(1, length)
    bit = 1
    while bit < at.shards:
        other = at.flat(flat, bit)
        low = (at.shard // bit) % 2 == 0
        flat = jnp.where(
            low, jnp.concatenate([flat, other], axis=0), jnp.concatenate([other, flat], axis=0)
        )
        bit *= 2
    out = []
    start = 0
    for size in sizes:
        out.append(flat[:, start : start + size].reshape(-1))
        start += size
    return out


LOG2E = 1.4426950408889634
HEAD = 64
PAIR = 128
ROWS_Q = 256
ROWS_K = 256


def lanes_of(shape):
    return lax.broadcasted_iota(jnp.int32, shape, len(shape) - 1)


def half_turn(value):
    low = lanes_of(value.shape) % HEAD < HEAD // 2
    return jnp.where(low, pltpu.roll(value, PAIR - HEAD // 2, 1), pltpu.roll(value, HEAD // 2, 1))


def swap_matrix():
    left = lax.broadcasted_iota(jnp.int32, (PAIR, PAIR), 0)
    right = lax.broadcasted_iota(jnp.int32, (PAIR, PAIR), 1)
    return (left == (right ^ (HEAD // 2))).astype(jnp.bfloat16)


def two_parts(value):
    high = value.astype(jnp.bfloat16)
    return high, (value - high.astype(jnp.float32)).astype(jnp.bfloat16)


def head_sum(value):
    left = lax.broadcasted_iota(jnp.int32, (2 * PAIR, PAIR), 0) // HEAD % 2
    right = lax.broadcasted_iota(jnp.int32, (2 * PAIR, PAIR), 1) // HEAD
    same = (left == right).astype(jnp.bfloat16)
    parts = jnp.concatenate(two_parts(value), axis=1)
    return jnp.dot(parts, same, preferred_element_type=jnp.float32)


def turned(raw, cosine, sine):
    swapped = jnp.dot(raw, swap_matrix(), preferred_element_type=jnp.float32)
    rot = raw.astype(jnp.float32) * cosine + swapped * sine
    factor = lax.rsqrt(head_sum(rot * rot) + EPS)
    return rot * factor, factor


def only(value, head):
    mine = lanes_of(value.shape) // HEAD == head
    return jnp.where(mine, value, jnp.zeros_like(value))


def dot_last(a, b):
    return lax.dot_general(a, b, (((1,), (1,)), ((), ())), preferred_element_type=jnp.float32)


def dot_first(a, b):
    return lax.dot_general(a, b, (((0,), (0,)), ((), ())), preferred_element_type=jnp.float32)


FAR = -16384.0


def spare_lane(shape, head):
    return lanes_of(shape) - (1 - head) * HEAD


def query_lanes(value, head, segs):
    spare = spare_lane(value.shape, head)
    own = lanes_of(value.shape) // HEAD == head
    marks = (spare >= 0) & (spare < 8) & (spare != segs)
    return jnp.where(own, value.astype(jnp.float32), jnp.where(marks, FAR, 0.0)).astype(value.dtype)


def key_lanes(value, head, segs):
    spare = spare_lane(value.shape, head)
    own = lanes_of(value.shape) // HEAD == head
    return jnp.where(own, value.astype(jnp.float32), (spare == segs).astype(jnp.float32)).astype(value.dtype)


def attend_kernel(temper, q_ref, k_ref, v_ref, cos_ref, sin_ref, scale_ref, seg_ref, out_ref, lse_ref,
                  q_sc, k_sc, v_sc, sum_sc):
    length = q_ref.shape[0]
    bf16 = jnp.bfloat16
    f32 = jnp.float32
    scale = scale_ref[...]
    cosine = cos_ref[...]
    sine = sin_ref[...]
    segs = seg_ref[...]
    q2 = (turned(q_ref[...], cosine, sine)[0] * scale).astype(bf16)
    k2 = (turned(k_ref[...], cosine, sine)[0] * scale).astype(bf16)
    v = v_ref[...]
    ones = jnp.ones_like(v)
    for head in range(2):
        q_sc[head] = query_lanes(q2, head, segs)
        k_sc[head] = key_lanes(k2, head, segs)
        v_sc[head, :, :PAIR] = only(v, head)
        v_sc[head, :, PAIR:] = only(ones, head)
    factor = temper * LOG2E
    size = min(ROWS_Q, length)
    blocks = length // size
    causal = lax.broadcasted_iota(jnp.int32, (size, size), 0) >= lax.broadcasted_iota(
        jnp.int32, (size, size), 1
    )
    for block in range(blocks):
        at = block * size
        for head in range(2):
            keys = k_sc[head, at : at + size, :]
            raw = dot_last(q_sc[head, at:, :], keys)
            expo = causal_top(jnp.exp2(raw * factor), causal).astype(bf16)
            part = jnp.dot(expo, v_sc[head, at : at + size, :], preferred_element_type=f32)
            if block == 0 and head == 0:
                sum_sc[...] = part
            else:
                sum_sc[at:, :] += part
    mass = sum_sc[:, PAIR:]
    out_ref[...] = (sum_sc[:, :PAIR] / mass).astype(bf16)
    lse_ref[...] = jnp.log2(mass)


def causal_top(value, causal):
    size = causal.shape[0]
    edge = jnp.where(causal, value[:size, :], 0.0)
    if value.shape[0] == size:
        return edge
    return jnp.concatenate([edge, value[size:, :]], axis=0)


def causal_bottom(value, causal):
    size = causal.shape[0]
    edge = jnp.where(causal, value[-size:, :], 0.0)
    if value.shape[0] == size:
        return edge
    return jnp.concatenate([value[:-size, :], edge], axis=0)


def pair_spec(length, offset):
    return pl.BlockSpec((length, PAIR), lambda p: (0, p + offset))


def attention(qkv, cosine, sine, scale, segs, offset):
    length, width = qkv.shape[0], qkv.shape[1] // 3
    pairs = width // PAIR
    whole = pl.BlockSpec((length, PAIR), lambda p: (0, 0))
    column = pl.BlockSpec((length, 1), lambda p: (0, 0))
    return pl.pallas_call(
        partial(attend_kernel, math.sqrt(HEAD)),
        grid=(pairs,),
        in_specs=[
            pair_spec(length, 0), pair_spec(length, pairs), pair_spec(length, 2 * pairs),
            whole, whole, pl.BlockSpec((1, PAIR), lambda p: (0, p + offset // PAIR)), column,
        ],
        out_specs=[pair_spec(length, 0), pair_spec(length, 0)],
        scratch_shapes=[
            pltpu.VMEM((2, length, PAIR), jnp.bfloat16),
            pltpu.VMEM((2, length, PAIR), jnp.bfloat16),
            pltpu.VMEM((2, length, 2 * PAIR), jnp.bfloat16),
            pltpu.VMEM((length, 2 * PAIR), jnp.float32),
        ],
        out_shape=[
            jax.ShapeDtypeStruct((length, width), jnp.bfloat16),
            jax.ShapeDtypeStruct((length, width), jnp.float32),
        ],
        compiler_params=pltpu.CompilerParams(vmem_limit_bytes=40 << 20),
        cost_estimate=pl.CostEstimate(
            flops=16 * length * length * width // 2, bytes_accessed=8 * length * width,
            transcendentals=length * length * width // HEAD // 2,
        ),
        name="attend",
    )(qkv, qkv, qkv, cosine, sine, scale, segs)


def three_parts(value):
    high = value.astype(jnp.bfloat16).astype(jnp.float32)
    rest = value - high
    mid = rest.astype(jnp.bfloat16).astype(jnp.float32)
    return high, mid, rest - mid


def attend_back_kernel(temper, q_ref, k_ref, v_ref, o_ref, g_ref, cos_ref, sin_ref, scale_ref, seg_ref, lse_ref,
                       g3_ref, gs_ref, q_sc, k_sc, v_sc, g_sc, dq_sc, dk_sc, dv_sc):
    length = q_ref.shape[0]
    bf16 = jnp.bfloat16
    f32 = jnp.float32
    scale = scale_ref[...]
    cosine = cos_ref[...]
    sine = sin_ref[...]
    segs = seg_ref[...]
    qn, q_factor = turned(q_ref[...], cosine, sine)
    kn, k_factor = turned(k_ref[...], cosine, sine)
    q2 = (qn * scale).astype(bf16)
    k2 = (kn * scale).astype(bf16)
    v = v_ref[...]
    grad = g_ref[...]
    spread = head_sum(grad.astype(f32) * o_ref[...].astype(f32))
    factor = temper * LOG2E
    lanes = lanes_of((length, PAIR))
    for head in range(2):
        spare = spare_lane((length, PAIR), head)
        own = lanes // HEAD == head
        parts = three_parts(lse_ref[:, head * HEAD : head * HEAD + 1] * (-1.0 / factor))
        marks = jnp.where((spare >= 0) & (spare < 8) & (spare != segs), FAR, 0.0)
        for n in range(3):
            marks = jnp.where(spare == 8 + n, parts[n], marks)
        q_sc[head] = jnp.where(own, q2.astype(f32), marks).astype(bf16)
        k_sc[head] = jnp.where(
            own, k2.astype(f32), ((spare == segs) | ((spare >= 8) & (spare < 11))).astype(f32)
        ).astype(bf16)
        parts = three_parts(-spread[:, head * HEAD : head * HEAD + 1])
        marks = jnp.zeros((length, PAIR), f32)
        for n in range(3):
            marks = jnp.where(spare == n, parts[n], marks)
        g_sc[head] = jnp.where(own, grad.astype(f32), marks).astype(bf16)
        v_sc[head] = jnp.where(own, v.astype(f32), ((spare >= 0) & (spare < 3)).astype(f32)).astype(bf16)
    size = min(ROWS_K, length)
    causal = lax.broadcasted_iota(jnp.int32, (size, size), 0) <= lax.broadcasted_iota(
        jnp.int32, (size, size), 1
    )
    blocks = length // size
    lanes = lanes_of((size, PAIR)) // HEAD
    for block in range(blocks - 1, -1, -1):
        at = block * size
        end = at + size
        dqs = []
        for head in range(2):
            queries = q_sc[head, at:end, :]
            grads = g_sc[head, at:end, :]
            keys = k_sc[head, :end, :]
            probs = causal_bottom(jnp.exp2(dot_last(keys, queries) * factor), causal)
            ds = (probs * dot_last(v_sc[head, :end, :], grads)).astype(bf16)
            dv = jnp.dot(probs.astype(bf16), grads, preferred_element_type=f32)
            dk = jnp.dot(ds, queries, preferred_element_type=f32)
            dqs.append(dot_first(ds, keys))
            if block == blocks - 1:
                dv_sc[head] = dv
                dk_sc[head] = dk
            else:
                dv_sc[head, :end, :] += dv
                dk_sc[head, :end, :] += dk
        dq_sc[at:end, :] = jnp.where(lanes == 0, dqs[0], dqs[1])
    lanes = lanes_of((length, PAIR)) // HEAD
    g3_ref[2] = jnp.where(lanes == 0, dv_sc[0], dv_sc[1]).astype(bf16)
    dq = dq_sc[...] * temper
    dk = jnp.where(lanes == 0, dk_sc[0], dk_sc[1]) * temper
    gs_ref[0] = jnp.broadcast_to(jnp.sum(dq * qn + dk * kn, axis=0, keepdims=True), (8, PAIR))

    def unturn(grad, unit, unit_factor):
        grad = grad * scale
        rot = unit_factor * (grad - unit * head_sum(grad * unit))
        return (rot * cosine + half_turn(rot * sine)).astype(bf16)

    g3_ref[0] = unturn(dq, qn, q_factor)
    g3_ref[1] = unturn(dk, kn, k_factor)


def attention_back(qkv, out, grad, lse, cosine, sine, scale, segs, offset, first, pairs):
    length, width = qkv.shape[0], qkv.shape[1] // 3
    every = width // PAIR
    base = offset // PAIR
    whole = pl.BlockSpec((length, PAIR), lambda p: (0, 0))
    column = pl.BlockSpec((length, 1), lambda p: (0, 0))
    return pl.pallas_call(
        partial(attend_back_kernel, math.sqrt(HEAD)),
        grid=(pairs,),
        in_specs=[
            pair_spec(length, first), pair_spec(length, first + every), pair_spec(length, first + 2 * every),
            pair_spec(length, first), pair_spec(length, first + base),
            whole, whole, pl.BlockSpec((1, PAIR), lambda p: (0, p + first + base)), column, pair_spec(length, first),
        ],
        out_specs=[
            pl.BlockSpec((3, length, PAIR), lambda p: (0, 0, p)),
            pl.BlockSpec((1, 8, PAIR), lambda p: (p, 0, 0)),
        ],
        scratch_shapes=[pltpu.VMEM((2, length, PAIR), jnp.bfloat16)] * 4
        + [pltpu.VMEM((length, PAIR), jnp.float32)]
        + [pltpu.VMEM((2, length, PAIR), jnp.float32)] * 2,
        out_shape=[
            jax.ShapeDtypeStruct((3, length, pairs * PAIR), jnp.bfloat16),
            jax.ShapeDtypeStruct((pairs, 8, PAIR), jnp.float32),
        ],
        compiler_params=pltpu.CompilerParams(vmem_limit_bytes=48 << 20),
        cost_estimate=pl.CostEstimate(
            flops=60 * length * length * pairs * PAIR, bytes_accessed=18 * length * pairs * PAIR,
            transcendentals=length * length * pairs * 2,
        ),
        name="attend_back",
    )(qkv, qkv, qkv, out, grad, cosine, sine, scale, segs, lse)


def rotary_wide(positions):
    half = HEAD // 2
    freq = jnp.power(10000.0, -2.0 * jnp.arange(half, dtype=jnp.float32) / HEAD)
    angle = positions.astype(jnp.float32)[:, None] * freq
    cosine = jnp.cos(angle)
    sine = jnp.sin(angle)
    return (
        jnp.concatenate([cosine] * 4, axis=1),
        jnp.concatenate([-sine, sine, -sine, sine], axis=1),
    )


def mean_last(value):
    return jnp.mean(value, axis=-1, keepdims=True)


def sort_matrix(core, each):
    left = lax.broadcasted_iota(jnp.int32, (256, 256), 0)
    right = lax.broadcasted_iota(jnp.int32, (256, 256), 1)
    place = right % 128
    source = (place // each * 2 + (core + 1 + right // 128) % 2) * each + place % each
    return (left == source).astype(jnp.bfloat16)


def sort_cores(value, matrix, out_ref, start):
    half = out_ref.shape[1] // 2
    for n in range(value.shape[1] // 256):
        both = jnp.dot(value[:, 256 * n : 256 * (n + 1)], matrix, preferred_element_type=jnp.float32)
        at = start + 128 * n
        out_ref[:, at : at + 128] = both[:, :128].astype(jnp.bfloat16)
        out_ref[:, half + at : half + at + 128] = both[:, 128:].astype(jnp.bfloat16)


def sort_kernel(each, core_ref, value_ref, out_ref):
    sort_cores(value_ref[...], sort_matrix(core_ref[0], each), out_ref, 0)


def sorted_cores(value, core, each):
    rows, width = value.shape
    tile = min(512, rows)
    spec = pl.BlockSpec((tile, width), lambda i: (i, 0))
    return pl.pallas_call(
        partial(sort_kernel, each),
        grid=(rows // tile,),
        in_specs=[pl.BlockSpec(memory_space=pltpu.SMEM), spec],
        out_specs=spec,
        out_shape=jax.ShapeDtypeStruct((rows, width), value.dtype),
        cost_estimate=pl.CostEstimate(flops=512 * rows * width, bytes_accessed=4 * rows * width, transcendentals=0),
        name="sort_cores",
    )(core, value)


def after_attention_kernel(each, core_ref, a0_ref, a1_ref, w_ref, x_ref, alpha_ref,
                           branch_ref, h_ref, low_ref, hs_ref, as_ref):
    f32 = jnp.float32
    half = a0_ref.shape[1]
    matrix = sort_matrix(core_ref[0], each)
    branch = jnp.dot(a0_ref[...], w_ref[:half, :], preferred_element_type=f32)
    branch = branch + jnp.dot(a1_ref[...], w_ref[half:, :], preferred_element_type=f32)
    branch_ref[...] = branch
    unit = branch * lax.rsqrt(mean_last(branch * branch) + EPS)
    x = x_ref[...].astype(f32)
    z = x + alpha_ref[...] * (unit - x)
    h = z * lax.rsqrt(mean_last(z * z) + EPS)
    low = h.astype(jnp.bfloat16)
    h_ref[...] = h
    low_ref[...] = low
    sort_cores(low, matrix, hs_ref, 0)
    sort_cores(a0_ref[...], matrix, as_ref, 0)
    sort_cores(a1_ref[...], matrix, as_ref, half // 2)


def after_attention(core, each, att, w_out, tokens, alpha):
    rows, width = tokens.shape
    tile = min(512, rows)
    full = pl.BlockSpec((tile, width), lambda i: (i, 0))
    half = pl.BlockSpec((tile, width // 2), lambda i: (i, 0))
    shape = lambda cols, kind: jax.ShapeDtypeStruct((rows, cols), kind)
    return pl.pallas_call(
        partial(after_attention_kernel, each),
        grid=(rows // tile,),
        in_specs=[
            pl.BlockSpec(memory_space=pltpu.SMEM), half, half,
            pl.BlockSpec((width, width), lambda i: (0, 0)), full, pl.BlockSpec((1, width), lambda i: (0, 0)),
        ],
        out_specs=[full] * 5,
        out_shape=[shape(width, jnp.float32)] * 2 + [shape(width, jnp.bfloat16)] * 3,
        compiler_params=pltpu.CompilerParams(vmem_limit_bytes=40 << 20),
        cost_estimate=pl.CostEstimate(flops=2 * rows * width * width, bytes_accessed=20 * rows * width, transcendentals=0),
        name="after_attention",
    )(core, *att, w_out, tokens, alpha)


def sigmoid(value):
    return 0.5 * jnp.tanh(0.5 * value) + 0.5


def up_kernel(h_ref, wu_ref, wg_ref, su_ref, sg_ref, up_ref, gate_ref, hid_ref):
    f32 = jnp.float32
    bf16 = jnp.bfloat16
    up = jnp.dot(h_ref[...], wu_ref[...], preferred_element_type=f32)
    gate = jnp.dot(h_ref[...], wg_ref[...], preferred_element_type=f32)
    value = gate * sg_ref[...]
    up_ref[...] = up.astype(bf16)
    gate_ref[...] = gate.astype(bf16)
    hid_ref[...] = (up * su_ref[...] * (value * sigmoid(value))).astype(bf16)


def feed_up(h_low, w, scale_up, scale_gate):
    rows, width = h_low.shape
    total = scale_up.shape[1]
    block = min(512, total)
    steps = total // block
    shape = jax.ShapeDtypeStruct((rows, total), jnp.bfloat16)
    out = pl.BlockSpec((rows, block), lambda j: (0, j))
    scale = pl.BlockSpec((1, block), lambda j: (0, j))
    return pl.pallas_call(
        up_kernel,
        grid=(steps,),
        in_specs=[
            pl.BlockSpec((rows, width), lambda j: (0, 0)),
            pl.BlockSpec((width, block), lambda j: (0, j)),
            pl.BlockSpec((width, block), lambda j: (0, steps + j)),
            scale, scale,
        ],
        out_specs=[out] * 3,
        out_shape=[shape] * 3,
        compiler_params=pltpu.CompilerParams(vmem_limit_bytes=48 << 20),
        cost_estimate=pl.CostEstimate(flops=4 * rows * width * total, bytes_accessed=2 * (rows * width + 2 * width * total + 3 * rows * total), transcendentals=rows * total),
        name="feed_up",
    )(h_low, w, w, scale_up, scale_gate)


def finish_kernel(scale_ref, hid_ref, wd_ref, m0_ref, h_ref, t_ref, mask_ref, alpha_ref,
                  out_ref, gm_ref, gz_ref, ga_ref, loss_ref):
    f32 = jnp.float32
    m1 = jnp.dot(hid_ref[...], wd_ref[...], preferred_element_type=f32)
    branch = jnp.concatenate([m0_ref[...], m1], axis=1)
    factor = lax.rsqrt(mean_last(branch * branch) + EPS)
    unit = branch * factor
    h1 = h_ref[...]
    alpha = alpha_ref[...]
    z = h1 + alpha * (unit - h1)
    z_factor = lax.rsqrt(mean_last(z * z) + EPS)
    h2 = z * z_factor
    out_ref[...] = h2.astype(jnp.bfloat16)
    diff = h2 - t_ref[...].astype(f32)
    masked = mask_ref[...] * diff
    grad = scale_ref[0] * masked
    gz = z_factor * (grad - h2 * mean_last(grad * h2))
    gz_ref[...] = (1.0 - alpha) * gz
    back = alpha * gz
    gm_ref[...] = (factor * (back - unit * mean_last(back * unit))).astype(jnp.bfloat16)

    @pl.when(pl.program_id(0) == 0)
    def _():
        ga_ref[...] = jnp.zeros_like(ga_ref)
        loss_ref[...] = jnp.zeros_like(loss_ref)

    ga_ref[...] += jnp.sum(gz * (unit - h1), axis=0, keepdims=True)
    loss_ref[...] += jnp.sum(masked * diff, axis=0, keepdims=True)


def finish(scale, hidden, wd, m0, h1, teacher, mask, alpha):
    rows, ff = hidden.shape
    width = h1.shape[1]
    tile = min(512, rows)
    full = pl.BlockSpec((tile, width), lambda i: (i, 0))
    row = pl.BlockSpec((1, width), lambda i: (0, 0))
    line = jax.ShapeDtypeStruct((1, width), jnp.float32)
    return pl.pallas_call(
        finish_kernel,
        grid=(rows // tile,),
        in_specs=[
            pl.BlockSpec(memory_space=pltpu.SMEM),
            pl.BlockSpec((tile, ff), lambda i: (i, 0)),
            pl.BlockSpec((ff, wd.shape[1]), lambda i: (0, 0)),
            pl.BlockSpec((tile, width - wd.shape[1]), lambda i: (i, 0)),
            full, full, pl.BlockSpec((tile, 1), lambda i: (i, 0)), row,
        ],
        out_specs=[full, full, full, row, row],
        out_shape=[
            jax.ShapeDtypeStruct((rows, width), jnp.bfloat16),
            jax.ShapeDtypeStruct((rows, width), jnp.bfloat16),
            jax.ShapeDtypeStruct((rows, width), jnp.float32),
            line, line,
        ],
        compiler_params=pltpu.CompilerParams(vmem_limit_bytes=56 << 20),
        cost_estimate=pl.CostEstimate(flops=2 * rows * ff * wd.shape[1], bytes_accessed=2 * rows * ff + 2 * ff * wd.shape[1] + 16 * rows * width, transcendentals=0),
        name="finish",
    )(scale, hidden, wd, m0, h1, teacher, mask, alpha)


def down_back_kernel(g_ref, w0_ref, w1_ref, up_ref, gate_ref, su_ref, sg_ref, gu_ref, gg_ref, gsu_ref, gsg_ref):
    f32 = jnp.float32
    bf16 = jnp.bfloat16
    half = w0_ref.shape[1]
    su = su_ref[...]
    sg = sg_ref[...]
    back = dot_last(g_ref[:, :half], w0_ref[...]) + dot_last(g_ref[:, half:], w1_ref[...])
    up = up_ref[...].astype(f32)
    gate = gate_ref[...].astype(f32)
    value = gate * sg
    sig = sigmoid(value)
    active = value * sig
    with_active = back * active
    g_value = back * up * su * (sig + active * (1.0 - sig))
    gu_ref[...] = (with_active * su).astype(bf16)
    gg_ref[...] = (g_value * sg).astype(bf16)
    gsu_ref[...] = jnp.sum(with_active * up, axis=0, keepdims=True)
    gsg_ref[...] = jnp.sum(g_value * gate, axis=0, keepdims=True)


def down_back(g, wd, up, gate, scale_up, scale_gate):
    rows, width = g.shape
    ff = up.shape[1]
    block = min(512, ff)
    col = pl.BlockSpec((rows, block), lambda j: (0, j))
    line = pl.BlockSpec((1, block), lambda j: (0, j))
    weight = pl.BlockSpec((block, width // 2), lambda j: (j, 0))
    big = jax.ShapeDtypeStruct((rows, ff), jnp.bfloat16)
    small = jax.ShapeDtypeStruct((1, ff), jnp.float32)
    return pl.pallas_call(
        down_back_kernel,
        grid=(ff // block,),
        in_specs=[pl.BlockSpec((rows, width), lambda j: (0, 0)), weight, weight, col, col, line, line],
        out_specs=[col, col, line, line],
        out_shape=[big, big, small, small],
        compiler_params=pltpu.CompilerParams(vmem_limit_bytes=48 << 20),
        cost_estimate=pl.CostEstimate(flops=2 * rows * ff * width, bytes_accessed=8 * rows * ff + 2 * ff * width, transcendentals=rows * ff),
        name="down_back",
    )(g, *wd, up, gate, scale_up, scale_gate)


def up_back_kernel(steps, gu_ref, gg_ref, wu_ref, wg_ref, gz_ref, branch_ref, x_ref, alpha_ref, gb_ref, gx_ref, ga_ref, acc):
    f32 = jnp.float32
    step = pl.program_id(0)

    @pl.when(step == 0)
    def _():
        acc[...] = gz_ref[...]

    acc[...] += dot_last(gu_ref[...], wu_ref[...]) + dot_last(gg_ref[...], wg_ref[...])

    @pl.when(step == steps - 1)
    def _():
        alpha = alpha_ref[...]
        tile = min(256, acc.shape[0])
        total = jnp.zeros(ga_ref.shape, f32)
        for at in range(0, acc.shape[0], tile):
            branch = branch_ref[at : at + tile, :]
            a_factor = lax.rsqrt(mean_last(branch * branch) + EPS)
            unit = branch * a_factor
            x = x_ref[at : at + tile, :].astype(f32)
            z = x + alpha * (unit - x)
            z_factor = lax.rsqrt(mean_last(z * z) + EPS)
            h = z * z_factor
            grad = acc[at : at + tile, :]
            gz = z_factor * (grad - h * mean_last(grad * h))
            total = total + jnp.sum(gz * (unit - x), axis=0, keepdims=True)
            back = alpha * gz
            gb_ref[at : at + tile, :] = (a_factor * (back - unit * mean_last(back * unit))).astype(jnp.bfloat16)
            gx_ref[at : at + tile, :] = (1.0 - alpha) * gz
        ga_ref[...] = total


def up_back(g_up, g_gate, w, gz, branch, tokens, alpha):
    rows, width = tokens.shape
    ff = g_up.shape[1]
    block = min(1024, ff)
    steps = ff // block
    once = pl.Buffered(1)
    whole = lambda: pl.BlockSpec((rows, width), lambda s: (0, 0), pipeline_mode=once)
    col = pl.BlockSpec((rows, block), lambda s: (0, s))
    line = pl.BlockSpec((1, width), lambda s: (0, 0))
    return pl.pallas_call(
        partial(up_back_kernel, steps),
        grid=(steps,),
        in_specs=[
            col, col, pl.BlockSpec((width, block), lambda s: (0, s)),
            pl.BlockSpec((width, block), lambda s: (0, s + steps)),
            whole(), whole(), whole(), line,
        ],
        out_specs=[whole(), whole(), line],
        out_shape=[
            jax.ShapeDtypeStruct((rows, width), jnp.bfloat16),
            jax.ShapeDtypeStruct((rows, width), jnp.float32),
            jax.ShapeDtypeStruct((1, width), jnp.float32),
        ],
        scratch_shapes=[pltpu.VMEM((rows, width), jnp.float32)],
        compiler_params=pltpu.CompilerParams(vmem_limit_bytes=60 << 20),
        cost_estimate=pl.CostEstimate(flops=4 * rows * width * ff, bytes_accessed=4 * ff * (rows + width) + 14 * rows * width, transcendentals=0),
        name="up_back",
    )(g_up, g_gate, w, w, gz, branch, tokens, alpha)


def down_grad_kernel(each, core_ref, h_ref, g_ref, other_ref, own_ref, whole_ref):
    whole_ref[...] = dot_first(h_ref[...], g_ref[...])
    core = core_ref[0]
    for n in range(h_ref.shape[1] // (2 * each)):
        for out_ref, which in ((other_ref, 1 - core), (own_ref, core)):
            start = pl.multiple_of((2 * n + which) * each, each)
            out_ref[n * each : (n + 1) * each, :] = whole_ref[pl.ds(start, each), :].astype(jnp.bfloat16)


def down_grad(core, hidden, g, groups):
    rows, ff = hidden.shape
    width = g.shape[1]
    each = ff // (2 * groups)
    block = min(1024, ff)
    out = pl.BlockSpec((block // 2, width), lambda i: (i, 0))
    shape = jax.ShapeDtypeStruct((ff // 2, width), jnp.bfloat16)
    return pl.pallas_call(
        partial(down_grad_kernel, each),
        grid=(ff // block,),
        in_specs=[
            pl.BlockSpec(memory_space=pltpu.SMEM),
            pl.BlockSpec((rows, block), lambda i: (0, i)),
            pl.BlockSpec((rows, width), lambda i: (0, 0)),
        ],
        out_specs=[out, out],
        out_shape=[shape, shape],
        scratch_shapes=[pltpu.VMEM((block, width), jnp.float32)],
        compiler_params=pltpu.CompilerParams(vmem_limit_bytes=40 << 20),
        cost_estimate=pl.CostEstimate(flops=2 * rows * ff * width, bytes_accessed=2 * rows * ff + 2 * ff * width + 2 * rows * width, transcendentals=0),
        name="down_grad",
    )(core, hidden, g)


def row_grad_kernel(left_ref, *refs):
    rights, (other_ref, own_ref) = refs[:-2], refs[-2:]
    half = other_ref.shape[0]
    at = 0
    for right in rights:
        cols = right.shape[1]
        both = dot_first(left_ref[...], right[...])
        other_ref[:, at : at + cols] = both[:half, :].astype(jnp.bfloat16)
        own_ref[:, at : at + cols] = both[half:, :].astype(jnp.bfloat16)
        at += cols


def row_grad(left, right):
    rows, width = left.shape
    cols = right.shape[1]
    block = min(512, cols)
    out = pl.BlockSpec((width // 2, block), lambda j: (0, j))
    shape = jax.ShapeDtypeStruct((width // 2, cols), jnp.bfloat16)
    return pl.pallas_call(
        row_grad_kernel,
        grid=(cols // block,),
        in_specs=[
            pl.BlockSpec((rows, width), lambda j: (0, 0)),
            pl.BlockSpec((rows, block), lambda j: (0, j)),
        ],
        out_specs=[out, out],
        out_shape=[shape, shape],
        compiler_params=pltpu.CompilerParams(vmem_limit_bytes=40 << 20),
        cost_estimate=pl.CostEstimate(flops=2 * rows * width * cols, bytes_accessed=2 * (rows * width + width * cols + rows * cols), transcendentals=0),
        name="row_grad",
    )(left, right)


def heads_grad(left, parts):
    rows, width = left.shape
    cols = parts[0].shape[2]
    count = len(parts)
    out = pl.BlockSpec((width // 2, cols * count), lambda j: (0, j))
    shape = jax.ShapeDtypeStruct((width // 2, 3 * cols * count), jnp.bfloat16)
    return pl.pallas_call(
        row_grad_kernel,
        grid=(3,),
        in_specs=[pl.BlockSpec((rows, width), lambda j: (0, 0))]
        + [pl.BlockSpec((pl.Squeezed(), rows, cols), lambda j: (j, 0, 0))] * count,
        out_specs=[out, out],
        out_shape=[shape, shape],
        compiler_params=pltpu.CompilerParams(vmem_limit_bytes=40 << 20),
        cost_estimate=pl.CostEstimate(flops=6 * rows * width * cols * count, bytes_accessed=2 * (rows * width + 3 * (width + rows) * cols * count), transcendentals=0),
        name="heads_grad",
    )(left, *parts)


def input_grad_kernel(base_ref, *refs):
    out_ref = refs[-1]
    count = len(refs) // 3
    total = base_ref[...]
    for n in range(count):
        first, second, w = refs[n * 3 : n * 3 + 3]
        cols = first.shape[2]
        for p in range(3):
            at = 2 * p * cols
            total = total + dot_last(first[p], w[:, at : at + cols])
            total = total + dot_last(second[p], w[:, at + cols : at + 2 * cols])
    out_ref[...] = total


def input_grad(base, parts, weights):
    rows, width = base.shape
    tile = min(256, width)
    out = pl.BlockSpec((rows, tile), lambda j: (0, j))
    specs, operands = [], []
    for n, w in enumerate(weights):
        for part in parts[2 * n : 2 * n + 2]:
            specs.append(pl.BlockSpec(part.shape, lambda j: (0, 0, 0), pipeline_mode=pl.Buffered(1)))
            operands.append(part)
        specs.append(pl.BlockSpec((tile, w.shape[1]), lambda j: (j, 0)))
        operands.append(w)
    flops = 2 * rows * width * sum(w.shape[1] for w in weights)
    return pl.pallas_call(
        input_grad_kernel,
        grid=(width // tile,),
        in_specs=[out] + specs,
        out_specs=out,
        out_shape=jax.ShapeDtypeStruct((rows, width), jnp.float32),
        compiler_params=pltpu.CompilerParams(vmem_limit_bytes=48 << 20),
        cost_estimate=pl.CostEstimate(flops=flops, bytes_accessed=20 * rows * width, transcendentals=0),
        name="input_grad",
    )(base, *operands)


def slots_kernel(count, uses, slots_ref, keep_ref, got_ref, *refs):
    extras, out_ref, acc = refs[:-2], refs[-2], refs[-1]
    f32 = jnp.float32
    acc[...] = keep_ref[...].astype(f32) + got_ref[...].astype(f32)
    for n, extra in enumerate(extras):
        takers = [i for i in range(count) if uses[n][i] is not None]
        if len(takers) == count:
            acc[...] += extra[...].astype(f32)
            continue
        for i in takers:

            @pl.when(pl.program_id(0) == i)
            def _(extra=extra):
                acc[...] += extra[...].astype(f32)

    out_ref[...] = acc[...].astype(out_ref.dtype)


def add_slots(keep, got, rows, slots, extras=()):
    count = len(slots)
    cols = keep.shape[1]
    uses = [use for _, use in extras]
    specs = [pl.BlockSpec((rows, cols), lambda i, s: (s[i], 0))] * 2
    for _, use in extras:
        first = next(u for u in use if u is not None)
        if all(u is None or u == first for u in use):
            specs.append(pl.BlockSpec((rows, cols), lambda i, s, first=first: (first, 0)))
        else:
            assert use == list(range(count))
            specs.append(pl.BlockSpec((rows, cols), lambda i, s: (i, 0)))
    grid = pltpu.PrefetchScalarGridSpec(
        num_scalar_prefetch=1,
        grid=(count,),
        in_specs=specs,
        out_specs=pl.BlockSpec((rows, cols), lambda i, s: (i, 0)),
        scratch_shapes=[pltpu.VMEM((rows, cols), jnp.float32)],
    )
    return pl.pallas_call(
        partial(slots_kernel, count, uses),
        grid_spec=grid,
        out_shape=jax.ShapeDtypeStruct((count * rows, cols), keep.dtype),
        compiler_params=pltpu.CompilerParams(vmem_limit_bytes=40 << 20),
        cost_estimate=pl.CostEstimate(flops=0, bytes_accessed=8 * count * rows * cols, transcendentals=0),
        name="add_slots",
    )(jnp.stack(slots).astype(jnp.int32), keep, got, *[e for e, _ in extras])


def body(
    tokens,
    teacher,
    valid,
    segments,
    positions,
    w_qkv,
    w_out,
    w_upgate,
    w_down,
    s_qk,
    alpha_attn,
    s_up,
    s_gate,
    alpha_mlp,
):
    f32 = jnp.float32
    bf16 = jnp.bfloat16
    at = Place()
    rows, width = tokens.shape
    ff = w_upgate.shape[1] // 2
    each = w_out.shape[0]
    groups = at.shards // NC
    core = at.core.reshape(1).astype(jnp.int32)
    half = width // 2
    pairs = half // PAIR
    segs = segments.reshape(rows, 1)

    def columns(w, starts, size):
        return jnp.concatenate([w[:, s : s + size] for s in starts], axis=1)

    chunks = [columns(w_qkv, [p * width + n * half for p in range(3)], half) for n in range(2)]
    chunks.append(w_out)
    full_up = lax.all_gather(w_upgate, "shard", axis=0, tiled=True)
    chunks += [w_down[:, :half], w_down[:, half:]]

    gather = Gather(at, chunks)
    gate = []
    for tick in range(4):
        gate = gather.tick(tick, gate)
    vectors = gather_vectors(at, (s_qk, alpha_attn, s_up, s_gate, alpha_mlp))
    f_sqk, f_aa, f_su, f_sg, f_am = (v.astype(f32).reshape(1, -1) for v in vectors)
    mask = valid.astype(f32)
    count = jnp.maximum(sum_everywhere(at, jnp.full((8, 128), jnp.sum(mask)))[0, 0], 1.0)
    scale = (2.0 * rows * at.reps * at.shards / count).reshape(1)
    cosine, sine = rotary_wide(positions.reshape(rows))
    x_sorted = sorted_cores(tokens, core, each)
    gate += [x_sorted, cosine, f_sqk, scale]

    def dot(left, right):
        return jnp.dot(left, right, preferred_element_type=f32).astype(bf16)

    weights, qkv, att, lse = {}, [], [], []
    for n in range(2):
        moved = gather.tick(4 + n, gate)
        weights[n] = gather.full(n)
        qkv.append(dot(after(tokens, gate), weights[n]))
        out, sums = attention(qkv[n], cosine, sine, f_sqk, segs, n * half)
        att.append(out)
        lse.append(sums)
        gate = moved + [out]
    moved = gather.tick(6, gate)
    weights[2] = gather.full(2)
    att = [after(a, gate) for a in att]
    branch_a, h_one, h_low, h_sorted, att_sorted = after_attention(core, each, att, weights[2], tokens, f_aa)
    gate = moved + [h_low]
    moved = gather.tick(7, gate)
    up, gate_part, hidden = feed_up(after(h_low, moved), full_up, f_su, f_sg)
    down = [gather.full(3), gather.full(4)]
    m_first = jnp.dot(hidden, down[0], preferred_element_type=f32)
    output, g_bm, gz, grad_am, loss_rows = finish(
        scale, hidden, down[1], m_first, h_one, teacher, mask.reshape(rows, 1), f_am
    )

    lanes = []
    waiting = {}

    def window(gate, enter):
        moved = []
        for name in enter:
            lanes.append(waiting[name])
        for chunk in lanes:
            if chunk.stage < 5:
                moved += chunk.step(gate)
        return moved

    def start(name, left, right, gate):
        waiting[name] = Reduce(at, *row_grad(left, after(right, gate)))
        return [waiting[name].send, waiting[name].keep]

    def dot_rows(left, right):
        return lax.dot_general(left, right, (((0,), (0,)), ((), ())), preferred_element_type=f32).astype(bf16)

    sides = down_grad(core, hidden, g_bm, groups)
    waiting["down"] = Reduce(at, *sides)
    gate = list(sides)
    moved = window(gate, ["down"])
    g_up, g_gate, grad_su, grad_sg = down_back(after(g_bm, gate), down, up, gate_part, f_su, f_sg)
    gate = moved + [g_up]
    moved = window(gate, [])
    own_up = lax.psum_scatter(dot_rows(after(h_low, gate), g_up), "shard", scatter_dimension=0, tiled=True)
    done = start("gate", h_sorted, g_gate, gate)
    gate = moved + done
    moved = window(gate, ["gate"])
    g_ba, gx_base, grad_aa = up_back(after(g_up, gate), g_gate, full_up, gz, branch_a, tokens, f_aa)
    gate = moved + [g_ba]

    g3, g_scale = {}, []

    def back(n, gate):
        part = pairs // 2
        out, sums = attention_back(
            qkv[n // 2], att[n // 2], after(g_att, gate), lse[n // 2], cosine, sine, f_sqk, segs,
            n // 2 * half, n % 2 * part, part,
        )
        g3[n] = out
        g_scale.append(sums[:, 0, :].reshape(-1))
        return [out]

    def start_qkv(n, gate):
        sides = heads_grad(after(x_sorted, gate), [g3[2 * n], g3[2 * n + 1]])
        waiting[f"qkv{n}"] = Reduce(at, *sides)
        return list(sides)

    moved = window(gate, [])
    g_att = lax.dot_general(
        after(g_ba, gate), weights[2], (((1,), (1,)), ((), ())), preferred_element_type=f32
    ).astype(bf16)
    done = start("out", att_sorted, g_ba, gate)
    gate = moved + done + back(0, gate)
    moved = window(gate, ["out"])
    gate = moved + back(1, gate)
    moved = window(gate, [])
    done = start_qkv(0, gate)
    gate = moved + done + back(2, gate)
    moved = window(gate, ["qkv0"])
    gate = moved + back(3, gate)
    moved = window(gate, [])
    gate = moved + start_qkv(1, gate)
    moved = window(gate, ["qkv1"])
    grad_x = input_grad(after(gx_base, gate), [g3[n] for n in range(4)], [weights[0], weights[1]])
    parts = [
        jnp.concatenate(g_scale), grad_aa.reshape(-1), grad_su.reshape(-1), grad_sg.reshape(-1),
        grad_am.reshape(-1), jnp.sum(loss_rows).reshape(1),
    ]
    sizes = [p.shape[0] for p in parts]
    flat = jnp.concatenate(parts)
    tall = -(-flat.shape[0] // 1024) * 8
    flat = jnp.pad(flat, (0, tall * 128 - flat.shape[0])).reshape(tall, 128)
    flat = sum_everywhere(at, flat).reshape(-1)
    gate = moved + [grad_x]
    while any(chunk.stage < 5 for chunk in lanes):
        gate = window(gate, [])
    owned = []
    place = 0
    for size in sizes[:-1]:
        mine = size // at.shards
        owned.append(lax.dynamic_slice_in_dim(flat, place + at.shard * mine, mine))
        place += size
    loss = flat[place] / count
    total = {name: chunk.total() for name, chunk in waiting.items()}
    own_up = after(own_up, gate)
    own_up = over_copies(at, own_up.astype(f32), 1)
    halves = lambda value: [value[:, p * half : (p + 1) * half] for p in range(3)]
    q0, q1 = halves(total["qkv0"]), halves(total["qkv1"])
    own_qkv = jnp.concatenate([part for pair in zip(q0, q1) for part in pair], axis=1)
    own_up = jnp.concatenate([own_up, total["gate"]], axis=1)
    return (output, loss, grad_x, own_qkv, total["out"], own_up, total["down"], *owned)


def solution(mesh):
    return jax.shard_map(
        body,
        mesh=mesh,
        in_specs=(
            P(("rep", "shard"), None),
            P(("rep", "shard"), None),
            P(("rep", "shard")),
            P(("rep", "shard"), None),
            P(("rep", "shard"), None),
            P("shard", None),
            P("shard", None),
            P("shard", None),
            P("shard", None),
            P("shard"),
            P("shard"),
            P("shard"),
            P("shard"),
            P("shard"),
        ),
        out_specs=(
            P(("rep", "shard"), None),
            P(),
            P(("rep", "shard"), None),
            P("shard", None),
            P("shard", None),
            P("shard", None),
            P("shard", None),
            P("shard"),
            P("shard"),
            P("shard"),
            P("shard"),
            P("shard"),
        ),
        check_vma=False,
    )
```

time: 1260 us -> 661 us (0.52)
  matrix products: 385 us -> 33.7 us
  Pallas kernels: 0 us -> 278 us
  waiting for transfers between devices: 392 us -> 152 us
  blocking collectives: 217 us -> 0 us
  other arithmetic: 170 us -> 18.2 us
  starting transfers between devices: 0.36 us -> 68.5 us
  local copies, waits for them, and re-layouts: 61.2 us -> 86.9 us
    reduce_scatter x3 -> x1, waiting for transfers between devices: 354 us -> 0.01 us  [body(): lax.psum_scatter(dot_rows(after(h_low, gate), g_up), 'shard', scatter_dim...]
    dot_general x24 -> x5, matrix products: 385 us -> 33.7 us  [the longest x1 14.6 us: dot_rows(): lax.dot_general(left, right, (((0,), (0,)), ((), ())), preferred_element_...]
    pallas_call x0 -> x53, Pallas kernels: none -> 278 us  [the longest x4 56.6 us: attention_back(): pl.pallas_call(partial(attend_back_kernel, math.sqrt(HEAD)), grid=(pairs,...]
    ppermute x0 -> x70, waiting for transfers between devices: none -> 152 us  [the longest x10 54 us: along_x(): lax.ppermute(value, AXES, self.moves(lambda r, z, x, c: (r, z, x ^ j, c)))]
    unnamed x2 -> x0, blocking collectives: 96.2 us -> none
    convert_element_type x20 -> x3, other arithmetic: 88.3 us -> 0.67 us  [the longest x1 0.67 us: body(): v.astype(f32).reshape(1, -1)]
    psum x3 -> x0, blocking collectives: 82 us -> none  [the longest x2 77.1 us: body(): lax.psum((jnp.sum(mask_f), jnp.sum(mask_f[:, None] * diff * diff)), ('rep...]
    ppermute x0 -> x70, starting transfers between devices: none -> 68.4 us  [the longest x15 20.2 us: along_y(): lax.ppermute(value, AXES, self.moves(lambda r, z, x, c: (r ^ 1, z, x, c)))]
  transfers between devices with their start and end apart: 9 -> 72, of which waited for: 4 -> 29; matrix products, arithmetic and copies ran while one was open for 22% -> 10% of each run, Pallas kernels for 0% -> 34%
where the time goes in v1:
time: 661 us; the launch traced here: 656 us
  Pallas kernels  278 us (42%)
  waiting for transfers between devices  152 us (23%)
  local copies, waits for them, and re-layouts  86.9 us (13%)
  starting transfers between devices  68.5 us (10%)
  matrix products  33.7 us (5%)
  between operations  18.5 us (3%)
  other arithmetic  18.2 us (3%)
    unnamed x293, local copies, waits for them, and re-layouts  70.4 us
    pallas_call x4, Pallas kernels, attention_back(): pl.pallas_call(partial(attend_back_kernel, math.sqrt(HEAD)), grid=(pairs,...  56.6 us
    ppermute x10, waiting for transfers between devices, along_x(): lax.ppermute(value, AXES, self.moves(lambda r, z, x, c: (r, z, x ^ j, c)))  54 us
    ppermute x10, waiting for transfers between devices, far_z(): lax.ppermute(value, AXES, self.moves(lambda r, z, x, c: (r, z ^ 2 + r % 2...  43.3 us
    pallas_call x1, Pallas kernels, up_back(): pl.pallas_call(partial(up_back_kernel, steps), grid=(steps,), in_specs=[c...  34.5 us
    pallas_call x25, Pallas kernels, add_slots(): pl.pallas_call(partial(slots_kernel, count, uses), grid_spec=grid, out_sh...  27.8 us
    pallas_call x1, Pallas kernels, down_back(): pl.pallas_call(down_back_kernel, grid=(ff // block,), in_specs=[pl.BlockS...  25.4 us
    pallas_call x1, Pallas kernels, feed_up(): pl.pallas_call(up_kernel, grid=(steps,), in_specs=[pl.BlockSpec((rows, wi...  24.9 us
  transfers between devices with their start and end apart: 72, of which 29 were waited for; matrix products, arithmetic and copies ran while one was open for 10% of the time, Pallas kernels for 34%

profile of v1, /device:TPU:0, one launch (start us, length us, event | category | flops | bytes accessed | tf_op | source)
XLA Modules:
  0.0 656.4 jit_solution(9270474530868278403)
XLA Ops:
  9.1 4.1 collective-permute-start.6
  45.0 17.5 %collective-permute-done.8.refs_2_ = bf16[64,1536]{1,0:T(8,128)(2,1)S(1)} collective-permute-done((bf16[64,1536]{1,0:T(8,128)(2,1)S(1)}, bf16[64,1536]{1,0:T(8,128)(2,1)S(1)}, u32[]{:S(2)}, u32[]{:S(2)}) %collective-permute-start.8) | collective-permute-done | bytes 196640 | tf_op jit(solution)/shard_map/ppermute | solution.py:51
  83.8 17.0 %collective-permute-done.15.refs_2_ = bf16[256,512]{1,0:T(8,128)(2,1)S(1)} collective-permute-done((bf16[256,512]{1,0:T(8,128)(2,1)S(1)}, bf16[256,512]{1,0:T(8,128)(2,1)S(1)}, u32[]{:S(2)}, u32[]{:S(2)}) %collective-permute-start.15) | collective-permute-done | bytes 262176 | tf_op jit(solution)/shard_map/ppermute | solution.py:51
  105.8 5.8 collective-permute-start.26
  117.7 11.2 %attend.2 = (bf16[1024,512]{1,0:T(8,128)(2,1)S(1)}, f32[1024,512]{1,0:T(8,128)S(1)}) custom-call(bf16[1024,1536]{1,0:T(8,128)(2,1)S(1)} %convolution_convert_fusion.2.q_ref.k_ref.v_ref, bf16[1024,1536]{1,0:T(8,128)(2,1)S(1)} %convolution_convert_fusion.2.q_ref.k_ref.v_ref, bf16[1024,1536]{1,0:T(8,128)(2,1)S(1)} %convolution_convert_fusion.2.q_ref.k_ref.v_ref, ...), custom_call_target="tpu_custom_call" | custom-call | flops 4294967296 | bytes 4194304 | tf_op jit(solution)/shard_map/attend/pallas_call | solution.py:415
  133.8 8.4 %collective-permute-done.25 = bf16[640,512]{1,0:T(8,128)(2,1)S(1)} collective-permute-done((bf16[640,512]{1,0:T(8,128)(2,1)S(1)}, bf16[640,512]{1,0:T(8,128)(2,1)S(1)}, u32[]{:S(2)}, u32[]{:S(2)}) %collective-permute-start.25) | collective-permute-done | bytes 655392 | tf_op jit(solution)/shard_map/ppermute | solution.py:54
  146.5 11.7 %attend.3 = (bf16[1024,512]{1,0:T(8,128)(2,1)S(1)}, f32[1024,512]{1,0:T(8,128)S(1)}) custom-call(bf16[1024,1536]{1,0:T(8,128)(2,1)S(1)} %convolution_convert_fusion.1.q_ref.k_ref.v_ref, bf16[1024,1536]{1,0:T(8,128)(2,1)S(1)} %convolution_convert_fusion.1.q_ref.k_ref.v_ref, bf16[1024,1536]{1,0:T(8,128)(2,1)S(1)} %convolution_convert_fusion.1.q_ref.k_ref.v_ref, ...), custom_call_target="tpu_custom_call" | custom-call | flops 4294967296 | bytes 4194304 | tf_op jit(solution)/shard_map/attend/pallas_call | solution.py:415
  171.3 7.1 %after_attention.1 = (f32[1024,1024]{1,0:T(8,128)}, f32[1024,1024]{1,0:T(8,128)}, bf16[1024,1024]{1,0:T(8,128)(2,1)S(1)}, bf16[1024,1024]{1,0:T(8,128)(2,1)S(1)}, bf16[1024,1024]{1,0:T(8,128)(2,1)S(1)}) custom-call(s32[1]{0:T(128)} %bitcast.2.core_ref.core, bf16[1024,512]{1,0:T(8,128)(2,1)S(1)} %copy-done.98, bf16[1024,512]{1,0:T(8,128)(2,1)S(1)} %copy-done.94, ...), custom_call_target="tpu_custom_call" | custom-call | flops 2147483648 | bytes 20971520 | tf_op jit(solution)/shard_map/after_attention/pallas_call | solution.py:637
  195.9 24.9 %feed_up.1 = (bf16[1024,4096]{1,0:T(8,128)(2,1)}, bf16[1024,4096]{1,0:T(8,128)(2,1)}, bf16[1024,4096]{1,0:T(8,128)(2,1)}) custom-call(bf16[1024,1024]{1,0:T(8,128)(2,1)S(1)} %copy-done.90, bf16[1024,8192]{1,0:T(8,128)(2,1)} %all-gather.2.cloned.1.call-done.wu_ref.wg_ref, bf16[1024,8192]{1,0:T(8,128)(2,1)} %all-gather.2.cloned.1.call-done.wu_ref.wg_ref, ...), custom_call_target="tpu_custom_call" | custom-call | flops 17179869184 | bytes 44040192 | tf_op jit(solution)/shard_map/feed_up/pallas_call | solution.py:675
  220.7 8.2 %fusion.16.m0_ref = f32[1024,512]{1,0:T(8,128)} fusion(bf16[1024,4096]{1,0:T(8,128)(2,1)} %get-tuple-element.148.hid_ref.h_ref, bf16[4096,512]{1,0:T(8,128)(2,1)S(1)} %bitcast.74), kind=kOutput, calls=%fused_computation.79 | convolution fusion | flops 4294967296 | bytes 14680064 | tf_op jit(solution)/shard_map/dot_general | solution.py:1094
  229.0 16.8 %finish.1 = (bf16[1024,1024]{1,0:T(8,128)(2,1)}, bf16[1024,1024]{1,0:T(8,128)(2,1)}, f32[1024,1024]{1,0:T(8,128)}, f32[1,1024]{1,0:T(1,128)}, f32[1,1024]{1,0:T(1,128)}) custom-call(f32[1]{0:T(128)} %bitcast.1.scale_ref, bf16[1024,4096]{1,0:T(8,128)(2,1)} %get-tuple-element.148.hid_ref.h_ref, bf16[4096,512]{1,0:T(8,128)(2,1)} %bitcast.67, ...), custom_call_target="tpu_custom_call" | custom-call | flops 4294967296 | bytes 29360128 | tf_op jit(solution)/shard_map/finish/pallas_call | solution.py:729
  247.3 13.0 %down_grad.1 = (bf16[2048,1024]{1,0:T(8,128)(2,1)}, bf16[2048,1024]{1,0:T(8,128)(2,1)S(1)}) custom-call(s32[1]{0:T(128)} %bitcast.2.core_ref.core, bf16[1024,4096]{1,0:T(8,128)(2,1)} %get-tuple-element.148.hid_ref.h_ref, bf16[1024,1024]{1,0:T(8,128)(2,1)S(1)} %copy-done.85), custom_call_target="tpu_custom_call" | custom-call | flops 8589934592 | bytes 18874368 | tf_op jit(solution)/shard_map/down_grad/pallas_call | solution.py:871
  260.9 25.4 %down_back.1 = (bf16[1024,4096]{1,0:T(8,128)(2,1)}, bf16[1024,4096]{1,0:T(8,128)(2,1)}, f32[1,4096]{1,0:T(1,128)S(1)}, f32[1,4096]{1,0:T(1,128)S(1)}) custom-call(bf16[1024,1024]{1,0:T(8,128)(2,1)S(1)} %copy-done.86, bf16[4096,512]{1,0:T(8,128)(2,1)} %bitcast.73, bf16[4096,512]{1,0:T(8,128)(2,1)} %bitcast.68, bf16[1024,4096]{1,0:T(8,128)(2,1)} %get-tuple-element.155.up_ref, ...), custom_call_target="tpu_custom_call" | custom-call | flops 8589934592 | bytes 41943040 | tf_op jit(solution)/shard_map/down_back/pallas_call | solution.py:781
  290.2 12.5 %row_grad.2 = (bf16[512,4096]{1,0:T(8,128)(2,1)}, bf16[512,4096]{1,0:T(8,128)(2,1)S(1)}) custom-call(bf16[1024,1024]{1,0:T(8,128)(2,1)S(1)} %copy-done.92, bf16[1024,4096]{1,0:T(8,128)(2,1)} %get-tuple-element.162.refs_0_.gg_ref), custom_call_target="tpu_custom_call" | custom-call | flops 8589934592 | bytes 18874368 | tf_op jit(solution)/shard_map/row_grad/pallas_call | solution.py:906
  304.7 9.4 %collective-permute-done.35.refs_0_ = bf16[512,1024]{1,0:T(8,128)(2,1)S(1)} collective-permute-done((bf16[512,1024]{1,0:T(8,128)(2,1)S(1)}, bf16[512,1024]{1,0:T(8,128)(2,1)S(1)}, u32[]{:S(2)}, u32[]{:S(2)}) %collective-permute-start.35) | collective-permute-done | bytes 1048608 | tf_op jit(solution)/shard_map/ppermute | solution.py:57
  314.8 14.6 %convolution_convert_fusion = bf16[1024,4096]{1,0:T(8,128)(2,1)} fusion(bf16[1024,1024]{1,0:T(8,128)(2,1)S(1)} %copy-done.90, bf16[1024,4096]{1,0:T(8,128)(2,1)} %get-tuple-element.165.gu_ref), kind=kOutput, calls=%fused_computation | convolution fusion | flops 8594128896 | bytes 18874368 | tf_op jit(solution)/shard_map/dot_general | solution.py:1116
  338.3 34.5 %up_back.1 = (bf16[1024,1024]{1,0:T(8,128)(2,1)}, f32[1024,1024]{1,0:T(8,128)}, f32[1,1024]{1,0:T(1,128)}) custom-call(bf16[1024,4096]{1,0:T(8,128)(2,1)} %get-tuple-element.165.gu_ref, bf16[1024,4096]{1,0:T(8,128)(2,1)} %get-tuple-element.162.refs_0_.gg_ref, bf16[1024,8192]{1,0:T(8,128)(2,1)} %all-gather.2.cloned.1.call-done.wu_ref.wg_ref, ...), custom_call_target="tpu_custom_call" | custom-call | flops 17179869184 | bytes 48234496 | tf_op jit(solution)/shard_map/up_back/pallas_call | solution.py:834
  372.7 11.4 %collective-permute-done.36.refs_0_.refs_1_.refs_2_ = bf16[768,1024]{1,0:T(8,128)(2,1)S(1)} collective-permute-done((bf16[768,1024]{1,0:T(8,128)(2,1)}, bf16[768,1024]{1,0:T(8,128)(2,1)S(1)}, u32[]{:S(2)}, u32[]{:S(2)}) %collective-permute-start.36) | collective-permute-done | bytes 1572896 | tf_op jit(solution)/shard_map/ppermute | solution.py:54
  401.0 14.5 %attend_back.4 = (bf16[3,1024,256]{2,1,0:T(8,128)(2,1)S(1)}, f32[2,8,128]{2,1,0:T(8,128)S(1)}) custom-call(bf16[1024,1536]{1,0:T(8,128)(2,1)} %copy-done.114, bf16[1024,1536]{1,0:T(8,128)(2,1)} %copy-done.114, bf16[1024,1536]{1,0:T(8,128)(2,1)} %copy-done.114, bf16[1024,512]{1,0:T(8,128)(2,1)S(1)} %copy-done.99, ...), custom_call_target="tpu_custom_call" | custom-call | flops 16106127360 | bytes 4718592 | tf_op jit(solution)/shard_map/attend_back/pallas_call | solution.py:531
  434.2 14.0 %attend_back.5 = (bf16[3,1024,256]{2,1,0:T(8,128)(2,1)S(1)}, f32[2,8,128]{2,1,0:T(8,128)S(1)}) custom-call(bf16[1024,1536]{1,0:T(8,128)(2,1)} %copy-done.114, bf16[1024,1536]{1,0:T(8,128)(2,1)} %copy-done.114, bf16[1024,1536]{1,0:T(8,128)(2,1)} %copy-done.114, bf16[1024,512]{1,0:T(8,128)(2,1)S(1)} %copy-done.100, ...), custom_call_target="tpu_custom_call" | custom-call | flops 16106127360 | bytes 4718592 | tf_op jit(solution)/shard_map/attend_back/pallas_call | solution.py:531
  451.9 17.8 %collective-permute-done.42.refs_0_.refs_1_.refs_2_ = bf16[192,4096]{1,0:T(8,128)(2,1)S(1)} collective-permute-done((bf16[192,4096]{1,0:T(8,128)(2,1)S(1)}, bf16[192,4096]{1,0:T(8,128)(2,1)S(1)}, u32[]{:S(2)}, u32[]{:S(2)}) %collective-permute-start.42) | collective-permute-done | bytes 1572896 | tf_op jit(solution)/shard_map/ppermute | solution.py:54
  481.6 14.2 %attend_back.6 = (bf16[3,1024,256]{2,1,0:T(8,128)(2,1)S(1)}, f32[2,8,128]{2,1,0:T(8,128)S(1)}) custom-call(bf16[1024,1536]{1,0:T(8,128)(2,1)} %copy-done.113, bf16[1024,1536]{1,0:T(8,128)(2,1)} %copy-done.113, bf16[1024,1536]{1,0:T(8,128)(2,1)} %copy-done.113, bf16[1024,512]{1,0:T(8,128)(2,1)S(1)} %copy-done.95, ...), custom_call_target="tpu_custom_call" | custom-call | flops 16106127360 | bytes 4718592 | tf_op jit(solution)/shard_map/attend_back/pallas_call | solution.py:531
  501.0 4.7 heads_grad.2
  517.3 13.9 %attend_back.7 = (bf16[3,1024,256]{2,1,0:T(8,128)(2,1)S(1)}, f32[2,8,128]{2,1,0:T(8,128)S(1)}) custom-call(bf16[1024,1536]{1,0:T(8,128)(2,1)} %copy-done.113, bf16[1024,1536]{1,0:T(8,128)(2,1)} %copy-done.113, bf16[1024,1536]{1,0:T(8,128)(2,1)} %copy-done.113, bf16[1024,512]{1,0:T(8,128)(2,1)S(1)} %copy-done.96, ...), custom_call_target="tpu_custom_call" | custom-call | flops 16106127360 | bytes 4718592 | tf_op jit(solution)/shard_map/attend_back/pallas_call | solution.py:531
  532.7 10.2 %collective-permute-done.52.refs_0_.refs_1_.refs_2_ = bf16[192,1024]{1,0:T(8,128)(2,1)S(1)} collective-permute-done((bf16[192,1024]{1,0:T(8,128)(2,1)S(1)}, bf16[192,1024]{1,0:T(8,128)(2,1)S(1)}, u32[]{:S(2)}, u32[]{:S(2)}) %collective-permute-start.52) | collective-permute-done | bytes 393248 | tf_op jit(solution)/shard_map/ppermute | solution.py:54
  546.4 4.7 heads_grad.3
  563.3 4.4 collective-permute-done.49
  577.4 11.1 %input_grad.1 = f32[1024,1024]{1,0:T(8,128)} custom-call(f32[1024,1024]{1,0:T(8,128)} %get-tuple-element.216.base_ref, bf16[3,1024,256]{2,1,0:T(8,128)(2,1)S(1)} %copy-done.105, bf16[3,1024,256]{2,1,0:T(8,128)(2,1)S(1)} %copy-done.108, bf16[1024,1536]{1,0:T(8,128)(2,1)} %bitcast.76, bf16[3,1024,256]{2,1,0:T(8,128)(2,1)S(1)} %copy-done.111, ...), custom_call_target="tpu_custom_call" | custom-call | flops 6442450944 | bytes 20971520 | tf_op jit(solution)/shard_map/input_grad/pallas_call | solution.py:966
  610.8 6.3 collective-permute-done.65.refs_0_.refs_1_.refs_2_
  622.2 4.1 collective-permute-done.66.refs_0_
  630.3 6.9 %collective-permute-done.68 = bf16[64,1536]{1,0:T(8,128)(2,1)S(1)} collective-permute-done((bf16[64,1536]{1,0:T(8,128)(2,1)S(1)}, bf16[64,1536]{1,0:T(8,128)(2,1)S(1)}, u32[]{:S(2)}, u32[]{:S(2)}) %collective-permute-start.68) | collective-permute-done | bytes 196640 | tf_op jit(solution)/shard_map/ppermute | solution.py:57
  640.8 5.8 collective-permute-done.69
  (559 shorter events, 252.2 us)
Async XLA Ops:
  7.2 188.6 %all-gather.2.cloned.1.call-start = ((), (), s32[]{:S(2)}) async-start(), calls=%async_computation.1 | async-start | bytes 17825792 | tf_op jit(solution)/shard_map/all_gather | solution.py:1058
  8.0 622.3 %reduce-scatter.2.cloned.1.call-start = ((), (), s32[]{:S(2)}) async-start(), calls=%async_computation.2 | async-start | bytes 8912896 | tf_op jit(solution)/shard_map/reduce_scatter | solution.py:1125
  9.1 29.4 %collective-permute-start.6 = (bf16[64,1536]{1,0:T(8,128)(2,1)S(1)}, bf16[64,1536]{1,0:T(8,128)(2,1)S(1)}, u32[]{:S(2)}, u32[]{:S(2)}) collective-permute-start(bf16[64,1536]{1,0:T(8,128)(2,1)S(1)} %pad_maximum_fusion.14.refs_0_), channel_id=1, source_target_pairs={{0,8},{1,9},{2,10},{3,11},{4,12},{5,13},{6,14},{7,15},{8,0},{9,1},... | collective-permute-start | bytes 589832 | tf_op jit(solution)/shard_map/ppermute | solution.py:51
  13.2 25.3 %collective-permute-start.5 = (bf16[64,1536]{1,0:T(8,128)(2,1)S(1)}, bf16[64,1536]{1,0:T(8,128)(2,1)S(1)}, u32[]{:S(2)}, u32[]{:S(2)}) collective-permute-start(bf16[64,1536]{1,0:T(8,128)(2,1)S(1)} %pad_maximum_fusion.14.refs_0_), channel_id=1, source_target_pairs={{0,4},{1,5},{2,6},{3,7},{4,0},{5,1},{6,2},{7,3},{8,12},{9,13},{10,... | collective-permute-start | bytes 589832 | tf_op jit(solution)/shard_map/ppermute | solution.py:48
  38.5 26.6 %collective-permute-start.9 = (bf16[160,1536]{1,0:T(8,128)(2,1)S(1)}, bf16[160,1536]{1,0:T(8,128)(2,1)S(1)}, u32[]{:S(2)}, u32[]{:S(2)}) collective-permute-start(bf16[160,1536]{1,0:T(8,128)(2,1)S(1)} %pad_maximum_fusion.7), channel_id=1, source_target_pairs={{0,2},{1,3},{2,0},{3,1},{4,6},{5,7},{6,4},{7,5},{8,10},{9,11},{10,... | collective-permute-start | bytes 1474568 | tf_op jit(solution)/shard_map/ppermute | solution.py:54
  39.9 27.5 %collective-permute-start.22 = (bf16[8,768]{1,0:T(8,128)(2,1)S(1)}, bf16[8,768]{1,0:T(8,128)(2,1)S(1)}, u32[]{:S(2)}, u32[]{:S(2)}) collective-permute-start(bf16[8,768]{1,0:T(8,128)(2,1)S(1)} %maximum_select_fusion.1), channel_id=1, source_target_pairs={{0,8},{1,9},{2,10},{3,11},{4,12},{5,13},{6,14},{7,15},{8,0},{9,1},... | collective-permute-start | bytes 36872 | tf_op jit(solution)/shard_map/ppermute | solution.py:64
  42.0 20.6 %collective-permute-start.8 = (bf16[64,1536]{1,0:T(8,128)(2,1)S(1)}, bf16[64,1536]{1,0:T(8,128)(2,1)S(1)}, u32[]{:S(2)}, u32[]{:S(2)}) collective-permute-start(bf16[64,1536]{1,0:T(8,128)(2,1)S(1)} %pad_maximum_fusion.13.refs_0_), channel_id=1, source_target_pairs={{0,8},{1,9},{2,10},{3,11},{4,12},{5,13},{6,14},{7,15},{8,0},{9,1},... | collective-permute-start | bytes 589832 | tf_op jit(solution)/shard_map/ppermute | solution.py:51
  44.2 20.1 %collective-permute-start.7 = (bf16[64,1536]{1,0:T(8,128)(2,1)S(1)}, bf16[64,1536]{1,0:T(8,128)(2,1)S(1)}, u32[]{:S(2)}, u32[]{:S(2)}) collective-permute-start(bf16[64,1536]{1,0:T(8,128)(2,1)S(1)} %pad_maximum_fusion.13.refs_0_), channel_id=1, source_target_pairs={{0,4},{1,5},{2,6},{3,7},{4,0},{5,1},{6,2},{7,3},{8,12},{9,13},{10,... | collective-permute-start | bytes 589832 | tf_op jit(solution)/shard_map/ppermute | solution.py:48
  77.4 23.3 %collective-permute-start.15 = (bf16[256,512]{1,0:T(8,128)(2,1)S(1)}, bf16[256,512]{1,0:T(8,128)(2,1)S(1)}, u32[]{:S(2)}, u32[]{:S(2)}) collective-permute-start(bf16[256,512]{1,0:T(8,128)(2,1)S(1)} %get-tuple-element.126.refs_0_), channel_id=1, source_target_pairs={{0,8},{1,9},{2,10},{3,11},{4,12},{5,13},{6,14},{7,15},{8,0},{9,1},... | collective-permute-start | bytes 786440 | tf_op jit(solution)/shard_map/ppermute | solution.py:51
  78.2 24.5 %collective-permute-start.14 = (bf16[256,512]{1,0:T(8,128)(2,1)S(1)}, bf16[256,512]{1,0:T(8,128)(2,1)S(1)}, u32[]{:S(2)}, u32[]{:S(2)}) collective-permute-start(bf16[256,512]{1,0:T(8,128)(2,1)S(1)} %get-tuple-element.126.refs_0_), channel_id=1, source_target_pairs={{0,4},{1,5},{2,6},{3,7},{4,0},{5,1},{6,2},{7,3},{8,12},{9,13},{10,... | collective-permute-start | bytes 786440 | tf_op jit(solution)/shard_map/ppermute | solution.py:48
  82.6 20.1 %collective-permute-start.16 = (bf16[160,1024]{1,0:T(8,128)(2,1)S(1)}, bf16[160,1024]{1,0:T(8,128)(2,1)S(1)}, u32[]{:S(2)}, u32[]{:S(2)}) collective-permute-start(bf16[160,1024]{1,0:T(8,128)(2,1)S(1)} %pad_maximum_fusion.11), channel_id=1, source_target_pairs={{0,2},{1,3},{2,0},{3,1},{4,6},{5,7},{6,4},{7,5},{8,10},{9,11},{10,... | collective-permute-start | bytes 983048 | tf_op jit(solution)/shard_map/ppermute | solution.py:54
  83.0 20.5 %collective-permute-start.18 = (bf16[512,1536]{1,0:T(8,128)(2,1)S(1)}, bf16[512,1536]{1,0:T(8,128)(2,1)S(1)}, u32[]{:S(2)}, u32[]{:S(2)}) collective-permute-start(bf16[512,1536]{1,0:T(8,128)(2,1)S(1)} %shard_map.229), channel_id=1, source_target_pairs={{0,1},{1,0},{2,3},{3,2},{4,5},{5,4},{6,7},{7,6},{8,9},{9,8},{10,11... | collective-permute-start | bytes 4718600 | tf_op jit(solution)/shard_map/ppermute | solution.py:60
  103.5 28.4 %collective-permute-start.24 = (bf16[256,512]{1,0:T(8,128)(2,1)S(1)}, bf16[256,512]{1,0:T(8,128)(2,1)S(1)}, u32[]{:S(2)}, u32[]{:S(2)}) collective-permute-start(bf16[256,512]{1,0:T(8,128)(2,1)S(1)} %get-tuple-element.132.refs_0_), channel_id=1, source_target_pairs={{0,8},{1,9},{2,10},{3,11},{4,12},{5,13},{6,14},{7,15},{8,0},{9,1},... | collective-permute-start | bytes 786440 | tf_op jit(solution)/shard_map/ppermute | solution.py:51
  103.6 28.3 %collective-permute-start.23 = (bf16[256,512]{1,0:T(8,128)(2,1)S(1)}, bf16[256,512]{1,0:T(8,128)(2,1)S(1)}, u32[]{:S(2)}, u32[]{:S(2)}) collective-permute-start(bf16[256,512]{1,0:T(8,128)(2,1)S(1)} %get-tuple-element.132.refs_0_), channel_id=1, source_target_pairs={{0,4},{1,5},{2,6},{3,7},{4,0},{5,1},{6,2},{7,3},{8,12},{9,13},{10,... | collective-permute-start | bytes 786440 | tf_op jit(solution)/shard_map/ppermute | solution.py:48
  105.8 26.2 %collective-permute-start.26 = (bf16[160,1024]{1,0:T(8,128)(2,1)S(1)}, bf16[160,1024]{1,0:T(8,128)(2,1)S(1)}, u32[]{:S(2)}, u32[]{:S(2)}) collective-permute-start(bf16[160,1024]{1,0:T(8,128)(2,1)S(1)} %pad_maximum_fusion.12), channel_id=1, source_target_pairs={{0,16},{1,17},{2,18},{3,19},{4,20},{5,21},{6,22},{7,23},{8,24},{9,... | collective-permute-start | bytes 983048 | tf_op jit(solution)/shard_map/ppermute | solution.py:57
  111.5 30.6 %collective-permute-start.25 = (bf16[640,512]{1,0:T(8,128)(2,1)S(1)}, bf16[640,512]{1,0:T(8,128)(2,1)S(1)}, u32[]{:S(2)}, u32[]{:S(2)}) collective-permute-start(bf16[640,512]{1,0:T(8,128)(2,1)S(1)} %pad_maximum_fusion.2), channel_id=1, source_target_pairs={{0,2},{1,3},{2,0},{3,1},{4,6},{5,7},{6,4},{7,5},{8,10},{9,11},{10,... | collective-permute-start | bytes 1966088 | tf_op jit(solution)/shard_map/ppermute | solution.py:54
  111.5 30.7 %collective-permute-start.27 = (bf16[512,1536]{1,0:T(8,128)(2,1)S(1)}, bf16[512,1536]{1,0:T(8,128)(2,1)S(1)}, u32[]{:S(2)}, u32[]{:S(2)}) collective-permute-start(bf16[512,1536]{1,0:T(8,128)(2,1)S(1)} %shard_map.231), channel_id=1, source_target_pairs={{0,1},{1,0},{2,3},{3,2},{4,5},{5,4},{6,7},{7,6},{8,9},{9,8},{10,11... | collective-permute-start | bytes 4718600 | tf_op jit(solution)/shard_map/ppermute | solution.py:60
  161.3 24.3 %collective-permute-start.32 = (bf16[2048,512]{1,0:T(8,128)(2,1)S(1)}, bf16[2048,512]{1,0:T(8,128)(2,1)}, u32[]{:S(2)}, u32[]{:S(2)}) collective-permute-start(bf16[2048,512]{1,0:T(8,128)(2,1)S(1)} %shard_map.236), channel_id=1, source_target_pairs={{0,1},{1,0},{2,3},{3,2},{4,5},{5,4},{6,7},{7,6},{8,9},{9,8},{10,11... | collective-permute-start | bytes 6291464 | tf_op jit(solution)/shard_map/ppermute | solution.py:60
  260.4 26.0 %collective-permute-start.34 = (bf16[2048,1024]{1,0:T(8,128)(2,1)}, bf16[2048,1024]{1,0:T(8,128)(2,1)S(1)}, u32[]{:S(2)}, u32[]{:S(2)}) collective-permute-start(bf16[2048,1024]{1,0:T(8,128)(2,1)} %get-tuple-element.158), channel_id=1, source_target_pairs={{0,1},{1,0},{2,3},{3,2},{4,5},{5,4},{6,7},{7,6},{8,9},{9,8},{10,11... | collective-permute-start | bytes 12582920 | tf_op jit(solution)/shard_map/ppermute | solution.py:60
  288.5 25.6 %collective-permute-start.35 = (bf16[512,1024]{1,0:T(8,128)(2,1)S(1)}, bf16[512,1024]{1,0:T(8,128)(2,1)S(1)}, u32[]{:S(2)}, u32[]{:S(2)}) collective-permute-start(bf16[512,1024]{1,0:T(8,128)(2,1)S(1)} %add_slots.25), channel_id=1, source_target_pairs={{0,16},{1,17},{2,18},{3,19},{4,20},{5,21},{6,22},{7,23},{8,24},{9,... | collective-permute-start | bytes 3145736 | tf_op jit(solution)/shard_map/ppermute | solution.py:57
  314.1 75.1 %collective-permute-start.37 = (bf16[512,4096]{1,0:T(8,128)(2,1)}, bf16[512,4096]{1,0:T(8,128)(2,1)}, u32[]{:S(2)}, u32[]{:S(2)}) collective-permute-start(bf16[512,4096]{1,0:T(8,128)(2,1)} %get-tuple-element.170), channel_id=1, source_target_pairs={{0,1},{1,0},{2,3},{3,2},{4,5},{5,4},{6,7},{7,6},{8,9},{9,8},{10,11... | collective-permute-start | bytes 12582920 | tf_op jit(solution)/shard_map/ppermute | solution.py:60
  336.3 47.8 %collective-permute-start.36 = (bf16[768,1024]{1,0:T(8,128)(2,1)}, bf16[768,1024]{1,0:T(8,128)(2,1)S(1)}, u32[]{:S(2)}, u32[]{:S(2)}) collective-permute-start(bf16[768,1024]{1,0:T(8,128)(2,1)} %add_slots.26), channel_id=1, source_target_pairs={{0,2},{1,3},{2,0},{3,1},{4,6},{5,7},{6,4},{7,5},{8,10},{9,11},{10,... | collective-permute-start | bytes 4718600 | tf_op jit(solution)/shard_map/ppermute | solution.py:54
  395.0 29.6 %collective-permute-start.38 = (bf16[256,1024]{1,0:T(8,128)(2,1)S(1)}, bf16[256,1024]{1,0:T(8,128)(2,1)S(1)}, u32[]{:S(2)}, u32[]{:S(2)}) collective-permute-start(bf16[256,1024]{1,0:T(8,128)(2,1)S(1)} %add_slots.27), channel_id=1, source_target_pairs={{0,4},{1,5},{2,6},{3,7},{4,0},{5,1},{6,2},{7,3},{8,12},{9,13},{10,... | collective-permute-start | bytes 1572872 | tf_op jit(solution)/shard_map/ppermute | solution.py:48
  397.0 27.6 %collective-permute-start.39 = (bf16[256,1024]{1,0:T(8,128)(2,1)S(1)}, bf16[256,1024]{1,0:T(8,128)(2,1)S(1)}, u32[]{:S(2)}, u32[]{:S(2)}) collective-permute-start(bf16[256,1024]{1,0:T(8,128)(2,1)S(1)} %add_slots.28), channel_id=1, source_target_pairs={{0,8},{1,9},{2,10},{3,11},{4,12},{5,13},{6,14},{7,15},{8,0},{9,1},... | collective-permute-start | bytes 1572872 | tf_op jit(solution)/shard_map/ppermute | solution.py:51
  398.9 28.3 %collective-permute-start.40 = (bf16[128,4096]{1,0:T(8,128)(2,1)S(1)}, bf16[128,4096]{1,0:T(8,128)(2,1)}, u32[]{:S(2)}, u32[]{:S(2)}) collective-permute-start(bf16[128,4096]{1,0:T(8,128)(2,1)S(1)} %add_slots.29), channel_id=1, source_target_pairs={{0,16},{1,17},{2,18},{3,19},{4,20},{5,21},{6,22},{7,23},{8,24},{9,... | collective-permute-start | bytes 3145736 | tf_op jit(solution)/shard_map/ppermute | solution.py:57
  431.0 41.0 %collective-permute-start.41 = (bf16[256,1024]{1,0:T(8,128)(2,1)S(1)}, bf16[256,1024]{1,0:T(8,128)(2,1)}, u32[]{:S(2)}, u32[]{:S(2)}) collective-permute-start(bf16[256,1024]{1,0:T(8,128)(2,1)S(1)} %add_slots.30), channel_id=1, source_target_pairs={{0,16},{1,17},{2,18},{3,19},{4,20},{5,21},{6,22},{7,23},{8,24},{9,... | collective-permute-start | bytes 1572872 | tf_op jit(solution)/shard_map/ppermute | solution.py:57
  432.9 36.8 %collective-permute-start.42 = (bf16[192,4096]{1,0:T(8,128)(2,1)S(1)}, bf16[192,4096]{1,0:T(8,128)(2,1)S(1)}, u32[]{:S(2)}, u32[]{:S(2)}) collective-permute-start(bf16[192,4096]{1,0:T(8,128)(2,1)S(1)} %add_slots.31), channel_id=1, source_target_pairs={{0,2},{1,3},{2,0},{3,1},{4,6},{5,7},{6,4},{7,5},{8,10},{9,11},{10,... | collective-permute-start | bytes 4718600 | tf_op jit(solution)/shard_map/ppermute | solution.py:54
  471.9 33.8 %collective-permute-start.46 = (bf16[128,1024]{1,0:T(8,128)(2,1)}, bf16[128,1024]{1,0:T(8,128)(2,1)S(1)}, u32[]{:S(2)}, u32[]{:S(2)}) collective-permute-start(bf16[128,1024]{1,0:T(8,128)(2,1)} %add_slots.34), channel_id=1, source_target_pairs={{0,16},{1,17},{2,18},{3,19},{4,20},{5,21},{6,22},{7,23},{8,24},{9,... | collective-permute-start | bytes 786440 | tf_op jit(solution)/shard_map/ppermute | solution.py:57
  475.4 31.8 %collective-permute-start.44 = (bf16[64,4096]{1,0:T(8,128)(2,1)}, bf16[64,4096]{1,0:T(8,128)(2,1)S(1)}, u32[]{:S(2)}, u32[]{:S(2)}) collective-permute-start(bf16[64,4096]{1,0:T(8,128)(2,1)} %add_slots.32), channel_id=1, source_target_pairs={{0,4},{1,5},{2,6},{3,7},{4,0},{5,1},{6,2},{7,3},{8,12},{9,13},{10,... | collective-permute-start | bytes 1572872 | tf_op jit(solution)/shard_map/ppermute | solution.py:48
  476.9 31.2 %collective-permute-start.45 = (bf16[64,4096]{1,0:T(8,128)(2,1)}, bf16[64,4096]{1,0:T(8,128)(2,1)S(1)}, u32[]{:S(2)}, u32[]{:S(2)}) collective-permute-start(bf16[64,4096]{1,0:T(8,128)(2,1)} %add_slots.33), channel_id=1, source_target_pairs={{0,8},{1,9},{2,10},{3,11},{4,12},{5,13},{6,14},{7,15},{8,0},{9,1},... | collective-permute-start | bytes 1572872 | tf_op jit(solution)/shard_map/ppermute | solution.py:51
  512.3 30.5 %collective-permute-start.53 = (bf16[64,4096]{1,0:T(8,128)(2,1)S(1)}, bf16[64,4096]{1,0:T(8,128)(2,1)S(1)}, u32[]{:S(2)}, u32[]{:S(2)}) collective-permute-start(bf16[64,4096]{1,0:T(8,128)(2,1)S(1)} %add_slots.37), channel_id=1, source_target_pairs={{0,16},{1,17},{2,18},{3,19},{4,20},{5,21},{6,22},{7,23},{8,24},{9,... | collective-permute-start | bytes 1572872 | tf_op jit(solution)/shard_map/ppermute | solution.py:57
  555.5 33.0 %collective-permute-start.60 = (bf16[512,1536]{1,0:T(8,128)(2,1)}, bf16[512,1536]{1,0:T(8,128)(2,1)}, u32[]{:S(2)}, u32[]{:S(2)}) collective-permute-start(bf16[512,1536]{1,0:T(8,128)(2,1)} %get-tuple-element.219), channel_id=1, source_target_pairs={{0,1},{1,0},{2,3},{3,2},{4,5},{5,4},{6,7},{7,6},{8,9},{9,8},{10,11... | collective-permute-start | bytes 4718600 | tf_op jit(solution)/shard_map/ppermute | solution.py:60
  (179 other events, 1615.2 us)
Sparse Core Ops, SparseCore 0:
  10.2 164.9 all-gather.1
  329.5 119.5 reduce-scatter.1

commit v2 on v1

--- a/solution.py
+++ b/solution.py
@@ -93,35 +93,42 @@
     )(slots, *pieces)
 
 
-def weave_kernel(core, half, other, out, sems):
+def weave_kernel(columns, core, half, other, *refs):
+    out, sems = refs[-2], refs[-1]
     at = core[0]
-    first = pltpu.make_async_copy(half, out.at[:, at], sems.at[0])
-    second = pltpu.make_async_copy(other, out.at[:, 1 - at], sems.at[1])
-    first.start()
-    second.start()
-    first.wait()
-    second.wait()
-
-
-def weave(half, other, core, groups):
+    copies = []
+    for n, (source, target, size) in enumerate(columns):
+        cols = pl.ds(target, size)
+        copies.append(pltpu.make_async_copy(half.at[:, :, source : source + size], out.at[:, at, :, cols], sems.at[0, n]))
+        copies.append(pltpu.make_async_copy(other.at[:, :, source : source + size], out.at[:, 1 - at, :, cols], sems.at[1, n]))
+    for copy in copies:
+        copy.start()
+    for copy in copies:
+        copy.wait()
+
+
+def weave(half, other, core, groups, columns, total, before):
     rows, cols = half.shape
     each = rows // groups
     size = rows * cols * half.dtype.itemsize
     shape = (groups, each, cols)
-    full = pl.pallas_call(
-        weave_kernel,
-        out_shape=jax.ShapeDtypeStruct((groups, 2, each, cols), half.dtype),
+    full = (groups, 2, each, total)
+    return pl.pallas_call(
+        partial(weave_kernel, columns),
+        out_shape=jax.ShapeDtypeStruct(full, half.dtype),
         in_specs=[
             pl.BlockSpec(memory_space=pltpu.SMEM),
             pl.BlockSpec(memory_space=pltpu.VMEM),
             pl.BlockSpec(memory_space=pltpu.VMEM),
-        ],
+        ]
+        + [pl.BlockSpec(memory_space=pl.ANY)] * len(before),
         out_specs=pl.BlockSpec(memory_space=pl.ANY),
-        scratch_shapes=[pltpu.SemaphoreType.DMA((2,))],
+        scratch_shapes=[pltpu.SemaphoreType.DMA((2, len(columns)))],
+        input_output_aliases={3: 0} if before else {},
         compiler_params=pltpu.CompilerParams(vmem_limit_bytes=2 * size + (4 << 20)),
         cost_estimate=pl.CostEstimate(flops=0, bytes_accessed=4 * size, transcendentals=0),
-    )(core, half.reshape(shape), other.reshape(shape))
-    return full.reshape(2 * rows, cols)
+        name="weave",
+    )(core, half.reshape(shape), other.reshape(shape), *[b.reshape(full) for b in before]).reshape(2 * rows, total)
 
 
 class Gather:
@@ -139,6 +146,7 @@
         offsets = range(1, at.nx)
         y = at.y
         ended = []
+        self.sends = []
         if tick < count:
             piece = after(self.ready[tick], gate)
             self.ready[tick] = piece
@@ -149,17 +157,21 @@
         if 0 <= i < count:
             piece = self.ready[i]
             rows = piece.shape[0]
-            half = lax.dynamic_slice_in_dim(piece, y * (rows // 2), rows // 2, axis=0)
-            send = after(jnp.concatenate([half, self.near[i], self.far[i]], axis=0), gate)
+            halves = [
+                lax.dynamic_slice_in_dim(part, y * (rows // 2), rows // 2, axis=0) for part in (piece, self.near[i])
+            ]
+            send = after(jnp.concatenate(halves + [self.far[i]], axis=0), gate)
+            self.sends.append(send)
             self.over_x[i] = [at.along_x(send, j) for j in offsets]
             ended += self.over_x[i]
         i = tick - 2
         if 0 <= i < count:
             rows = self.ready[i].shape[0]
             sends = [self.far[i]]
-            for got in self.over_x[i]:
-                sends += [got[: rows // 2], got[rows // 2 + rows :]]
-            self.over_y[i] = at.along_y(after(jnp.concatenate(sends, axis=0), gate))
+            sends += self.over_x[i]
+            send = after(jnp.concatenate(sends, axis=0), gate)
+            self.sends.append(send)
+            self.over_y[i] = at.along_y(send)
             ended += [self.over_y[i]]
         i = tick - 3
         if 0 <= i < count:
@@ -170,18 +182,20 @@
             slots = [at.slot(0, 0), at.slot(1, 0), at.slot(2 + y, 0), at.slot(3 - y, 0)]
             place = rows
             for mine, j in zip(self.over_x[i], offsets):
-                pieces += [mine[:half], mine[half : half + rows], mine[half + rows :]]
-                slots += [at.slot(0, j) * 2 + y, at.slot(1, j), at.slot(2 + y, j)]
-                pieces += [got[place : place + half], got[place + half : place + half + rows]]
-                slots += [at.slot(0, j) * 2 + (1 - y), at.slot(3 - y, j)]
-                place += half + rows
+                for got_here, side in ((mine, y), (got[place : place + 2 * rows], 1 - y)):
+                    pieces += [got_here[:half], got_here[half:rows], got_here[rows:]]
+                    slots += [at.slot(0, j) * 2 + side, at.slot(1, j) * 2 + side, at.slot(2 + side, j)]
+                place += 2 * rows
             self.own[i] = assemble(pieces, jnp.stack(slots).astype(jnp.int32), self.groups * rows)
+            self.sends.append(self.own[i])
             self.other[i] = at.other_core(after(self.own[i], gate))
             ended += [self.other[i]]
         return ended
 
-    def full(self, i):
-        return weave(self.own[i], self.other[i], self.core, self.groups)
+    def full(self, i, columns=None, total=None, before=()):
+        cols = self.own[i].shape[1]
+        columns = columns or [(0, 0, cols)]
+        return weave(self.own[i], self.other[i], self.core, self.groups, columns, total or cols, before)
 
 
 def after(value, gate):
@@ -196,9 +210,10 @@
         self.rows = keep.shape[0] // (NZ * at.nx)
         self.stage = 0
 
-    def add(self, places, extras=()):
+    def add(self, gate, places, plan, terms=()):
         slots = [self.at.slot(k, j) for k, j in places]
-        return add_slots(self.keep, self.got, self.rows, slots, extras)
+        self.sends = list(add_slots(after(self.keep, gate), self.got, self.rows, slots, plan, terms))
+        return self.sends
 
     def step(self, gate):
         at = self.at
@@ -207,27 +222,35 @@
         stage = self.stage
         self.stage += 1
         if stage == 0:
+            self.sends = []
             self.got = at.other_core(after(self.send, gate))
             return [self.got]
         if stage == 1:
-            send = self.add([(3 - y, j) for j in range(at.nx)])
-            self.got_y = at.along_y(after(send, gate))
+            (send,) = self.add(gate, [(3 - y, j) for j in range(at.nx)], [[[]] * at.nx])
+            self.got_y = at.along_y(send)
             return [self.got_y]
         if stage == 2:
-            self.got_x = []
+            places, plan = [], []
             for j in offsets:
-                send = self.add([(0, j), (1, j), (2 + y, j)], [(self.got_y, [None, None, j])])
-                self.got_x.append(at.along_x(after(send, gate), j))
+                places += [(0, j), (1, j), (2 + y, j)]
+                plan.append([[], [], [(0, j)]])
+            sends = self.add(gate, places, plan, [self.got_y])
+            self.got_x = [at.along_x(send, j) for send, j in zip(sends, offsets)]
             return self.got_x
         if stage == 3:
-            near = self.add([(1, 0)], [(g, [1]) for g in self.got_x])
-            far = self.add([(2 + y, 0)], [(self.got_y, [0])] + [(g, [2]) for g in self.got_x])
-            self.near = at.near_z(after(near, gate))
-            self.far = at.far_z(after(far, gate))
+            count = len(self.got_x)
+            near, far = self.add(
+                gate,
+                [(1, 0), (2 + y, 0)],
+                [[[(1 + n, 1) for n in range(count)]], [[(0, 0)] + [(1 + n, 2) for n in range(count)]]],
+                [self.got_y] + self.got_x,
+            )
+            self.near = at.near_z(near)
+            self.far = at.far_z(far)
             return [self.near, self.far]
         if stage == 4:
-            terms = [(self.near, [0]), (self.far, [0])] + [(g, [0]) for g in self.got_x]
-            self.mine = after(self.add([(0, 0)], terms), gate)
+            terms = [self.near, self.far] + self.got_x
+            (self.mine,) = self.add(gate, [(0, 0)], [[[(n, 0) for n in range(len(terms))]]], terms)
             self.last = at.along_y(self.mine)
             return [self.last]
         return []
@@ -243,33 +266,24 @@
     return total
 
 
-def sum_everywhere(at, value):
-    bit = 1
-    while bit < at.reps * at.shards:
-        value = value + at.flat(value, bit)
-        bit *= 2
-    return value
-
-
-def gather_vectors(at, vectors):
-    sizes = [v.shape[0] for v in vectors]
-    flat = jnp.concatenate(vectors)
-    length = -(-flat.shape[0] // 128) * 128
-    flat = jnp.pad(flat, (0, length - flat.shape[0])).reshape(1, length)
-    bit = 1
-    while bit < at.shards:
-        other = at.flat(flat, bit)
-        low = (at.shard // bit) % 2 == 0
-        flat = jnp.where(
-            low, jnp.concatenate([flat, other], axis=0), jnp.concatenate([other, flat], axis=0)
-        )
-        bit *= 2
-    out = []
-    start = 0
-    for size in sizes:
-        out.append(flat[:, start : start + size].reshape(-1))
-        start += size
-    return out
+class Sum:
+    def __init__(self, at, value):
+        self.at = at
+        self.value = value
+        self.bit = 1
+
+    def step(self, gate):
+        if self.bit >= self.at.reps * self.at.shards:
+            return []
+        value = after(self.value, gate)
+        self.value = value + self.at.flat(value, self.bit)
+        self.bit *= 2
+        return [self.value]
+
+    def total(self):
+        while self.step([]):
+            pass
+        return self.value
 
 
 LOG2E = 1.4426950408889634
@@ -427,8 +441,8 @@
             pltpu.VMEM((length, 2 * PAIR), jnp.float32),
         ],
         out_shape=[
-            jax.ShapeDtypeStruct((length, width), jnp.bfloat16),
-            jax.ShapeDtypeStruct((length, width), jnp.float32),
+            far_array((length, width), jnp.bfloat16),
+            far_array((length, width), jnp.float32),
         ],
         compiler_params=pltpu.CompilerParams(vmem_limit_bytes=40 << 20),
         cost_estimate=pl.CostEstimate(
@@ -544,7 +558,7 @@
         + [pltpu.VMEM((length, PAIR), jnp.float32)]
         + [pltpu.VMEM((2, length, PAIR), jnp.float32)] * 2,
         out_shape=[
-            jax.ShapeDtypeStruct((3, length, pairs * PAIR), jnp.bfloat16),
+            far_array((3, length, pairs * PAIR), jnp.bfloat16),
             jax.ShapeDtypeStruct((pairs, 8, PAIR), jnp.float32),
         ],
         compiler_params=pltpu.CompilerParams(vmem_limit_bytes=48 << 20),
@@ -553,7 +567,7 @@
             transcendentals=length * length * pairs * 2,
         ),
         name="attend_back",
-    )(qkv, qkv, qkv, out, grad, cosine, sine, scale, segs, lse)
+    )(far(qkv), far(qkv), far(qkv), far(out), far(grad), far(cosine), far(sine), scale, far(segs), far(lse))
 
 
 def rotary_wide(positions):
@@ -566,6 +580,14 @@
         jnp.concatenate([cosine] * 4, axis=1),
         jnp.concatenate([-sine, sine, -sine, sine], axis=1),
     )
+
+
+def far_array(shape, kind):
+    return pltpu.HBM(shape, kind)
+
+
+def far(value):
+    return pltpu.with_memory_space_constraint(value, pltpu.HBM)
 
 
 def mean_last(value):
@@ -609,7 +631,7 @@
 
 
 def after_attention_kernel(each, core_ref, a0_ref, a1_ref, w_ref, x_ref, alpha_ref,
-                           branch_ref, h_ref, low_ref, hs_ref, as_ref):
+                           branch_ref, h_ref, low_ref, hs_ref):
     f32 = jnp.float32
     half = a0_ref.shape[1]
     matrix = sort_matrix(core_ref[0], each)
@@ -624,8 +646,6 @@
     h_ref[...] = h
     low_ref[...] = low
     sort_cores(low, matrix, hs_ref, 0)
-    sort_cores(a0_ref[...], matrix, as_ref, 0)
-    sort_cores(a1_ref[...], matrix, as_ref, half // 2)
 
 
 def after_attention(core, each, att, w_out, tokens, alpha):
@@ -641,8 +661,8 @@
             pl.BlockSpec(memory_space=pltpu.SMEM), half, half,
             pl.BlockSpec((width, width), lambda i: (0, 0)), full, pl.BlockSpec((1, width), lambda i: (0, 0)),
         ],
-        out_specs=[full] * 5,
-        out_shape=[shape(width, jnp.float32)] * 2 + [shape(width, jnp.bfloat16)] * 3,
+        out_specs=[full] * 4,
+        out_shape=[shape(width, jnp.float32)] * 2 + [shape(width, jnp.bfloat16)] * 2,
         compiler_params=pltpu.CompilerParams(vmem_limit_bytes=40 << 20),
         cost_estimate=pl.CostEstimate(flops=2 * rows * width * width, bytes_accessed=20 * rows * width, transcendentals=0),
         name="after_attention",
@@ -653,9 +673,10 @@
     return 0.5 * jnp.tanh(0.5 * value) + 0.5
 
 
-def up_kernel(h_ref, wu_ref, wg_ref, su_ref, sg_ref, up_ref, gate_ref, hid_ref):
+def up_kernel(h_ref, wu_ref, wg_ref, su_ref, sg_ref, *refs):
     f32 = jnp.float32
     bf16 = jnp.bfloat16
+    up_ref, gate_ref, hid_ref = refs[-3:]
     up = jnp.dot(h_ref[...], wu_ref[...], preferred_element_type=f32)
     gate = jnp.dot(h_ref[...], wg_ref[...], preferred_element_type=f32)
     value = gate * sg_ref[...]
@@ -664,14 +685,16 @@
     hid_ref[...] = (up * su_ref[...] * (value * sigmoid(value))).astype(bf16)
 
 
-def feed_up(h_low, w, scale_up, scale_gate):
+def feed_up(part, parts, h_low, w, scale_up, scale_gate, before):
     rows, width = h_low.shape
-    total = scale_up.shape[1]
-    block = min(512, total)
-    steps = total // block
-    shape = jax.ShapeDtypeStruct((rows, total), jnp.bfloat16)
-    out = pl.BlockSpec((rows, block), lambda j: (0, j))
-    scale = pl.BlockSpec((1, block), lambda j: (0, j))
+    ff = scale_up.shape[1]
+    q = w.shape[1] // 2
+    block = min(512, q)
+    steps = q // block
+    first = part * steps
+    out = pl.BlockSpec((rows, block), lambda j: (0, first + j))
+    line = pl.BlockSpec((1, block), lambda j: (0, first + j))
+    shape = far_array((rows, ff), jnp.bfloat16)
     return pl.pallas_call(
         up_kernel,
         grid=(steps,),
@@ -679,80 +702,105 @@
             pl.BlockSpec((rows, width), lambda j: (0, 0)),
             pl.BlockSpec((width, block), lambda j: (0, j)),
             pl.BlockSpec((width, block), lambda j: (0, steps + j)),
-            scale, scale,
-        ],
+            line, line,
+        ] + [pl.BlockSpec(memory_space=pl.ANY)] * len(before),
         out_specs=[out] * 3,
         out_shape=[shape] * 3,
+        input_output_aliases={5 + n: n for n in range(len(before))},
         compiler_params=pltpu.CompilerParams(vmem_limit_bytes=48 << 20),
-        cost_estimate=pl.CostEstimate(flops=4 * rows * width * total, bytes_accessed=2 * (rows * width + 2 * width * total + 3 * rows * total), transcendentals=rows * total),
+        cost_estimate=pl.CostEstimate(flops=4 * rows * width * q, bytes_accessed=2 * (rows * width + 2 * width * q + 3 * rows * q), transcendentals=rows * q),
         name="feed_up",
-    )(h_low, w, w, scale_up, scale_gate)
-
-
-def finish_kernel(scale_ref, hid_ref, wd_ref, m0_ref, h_ref, t_ref, mask_ref, alpha_ref,
-                  out_ref, gm_ref, gz_ref, ga_ref, loss_ref):
+    )(h_low, w, w, scale_up, scale_gate, *before)
+
+
+def finish_kernel(steps, hid_ref, w0_ref, w1_ref, h1_ref, t_ref, mask_ref, alpha_ref,
+                  out_ref, gm_ref, gz_ref, ga_ref, loss_ref, acc):
     f32 = jnp.float32
-    m1 = jnp.dot(hid_ref[...], wd_ref[...], preferred_element_type=f32)
-    branch = jnp.concatenate([m0_ref[...], m1], axis=1)
-    factor = lax.rsqrt(mean_last(branch * branch) + EPS)
-    unit = branch * factor
-    h1 = h_ref[...]
-    alpha = alpha_ref[...]
-    z = h1 + alpha * (unit - h1)
-    z_factor = lax.rsqrt(mean_last(z * z) + EPS)
-    h2 = z * z_factor
-    out_ref[...] = h2.astype(jnp.bfloat16)
-    diff = h2 - t_ref[...].astype(f32)
-    masked = mask_ref[...] * diff
-    grad = scale_ref[0] * masked
-    gz = z_factor * (grad - h2 * mean_last(grad * h2))
-    gz_ref[...] = (1.0 - alpha) * gz
-    back = alpha * gz
-    gm_ref[...] = (factor * (back - unit * mean_last(back * unit))).astype(jnp.bfloat16)
-
-    @pl.when(pl.program_id(0) == 0)
+    bf16 = jnp.bfloat16
+    step = pl.program_id(0)
+    half = w0_ref.shape[1]
+
+    @pl.when(step == 0)
     def _():
-        ga_ref[...] = jnp.zeros_like(ga_ref)
-        loss_ref[...] = jnp.zeros_like(loss_ref)
-
-    ga_ref[...] += jnp.sum(gz * (unit - h1), axis=0, keepdims=True)
-    loss_ref[...] += jnp.sum(masked * diff, axis=0, keepdims=True)
-
-
-def finish(scale, hidden, wd, m0, h1, teacher, mask, alpha):
+        acc[...] = jnp.zeros_like(acc)
+
+    acc[:, :half] += jnp.dot(hid_ref[...], w0_ref[...], preferred_element_type=f32)
+    acc[:, half:] += jnp.dot(hid_ref[...], w1_ref[...], preferred_element_type=f32)
+
+    @pl.when(step == steps - 1)
+    def _():
+        alpha = alpha_ref[...]
+        grads = jnp.zeros(ga_ref.shape, f32)
+        losses = jnp.zeros(loss_ref.shape, f32)
+        tile = min(256, acc.shape[0])
+        for at in range(0, acc.shape[0], tile):
+            rows = pl.ds(at, tile)
+            branch = acc[rows, :]
+            factor = lax.rsqrt(mean_last(branch * branch) + EPS)
+            unit = branch * factor
+            h1 = h1_ref[rows, :]
+            z = h1 + alpha * (unit - h1)
+            z_factor = lax.rsqrt(mean_last(z * z) + EPS)
+            h2 = z * z_factor
+            out_ref[rows, :] = h2.astype(bf16)
+            diff = h2 - t_ref[rows, :].astype(f32)
+            masked = mask_ref[rows, :] * diff
+            grad = 2.0 * masked
+            gz = z_factor * (grad - h2 * mean_last(grad * h2))
+            gz_ref[rows, :] = (1.0 - alpha) * gz
+            back = alpha * gz
+            gm_ref[rows, :] = (factor * (back - unit * mean_last(back * unit))).astype(bf16)
+            grads = grads + jnp.sum(gz * (unit - h1), axis=0, keepdims=True)
+            losses = losses + jnp.sum(masked * diff, axis=0, keepdims=True)
+        ga_ref[...] = grads
+        loss_ref[...] = losses
+
+
+def finish(hidden, down, h1, teacher, mask, alpha):
     rows, ff = hidden.shape
     width = h1.shape[1]
-    tile = min(512, rows)
-    full = pl.BlockSpec((tile, width), lambda i: (i, 0))
-    row = pl.BlockSpec((1, width), lambda i: (0, 0))
+    block = min(1024, ff)
+    steps = ff // block
+    once = pl.Buffered(1)
+    whole = lambda cols=width: pl.BlockSpec((rows, cols), lambda j: (0, 0), pipeline_mode=once)
+    row = pl.BlockSpec((1, width), lambda j: (0, 0))
+    deep = pl.BlockSpec((block, width // 2), lambda j: (j, 0))
     line = jax.ShapeDtypeStruct((1, width), jnp.float32)
     return pl.pallas_call(
-        finish_kernel,
-        grid=(rows // tile,),
+        partial(finish_kernel, steps),
+        grid=(steps,),
         in_specs=[
-            pl.BlockSpec(memory_space=pltpu.SMEM),
-            pl.BlockSpec((tile, ff), lambda i: (i, 0)),
-            pl.BlockSpec((ff, wd.shape[1]), lambda i: (0, 0)),
-            pl.BlockSpec((tile, width - wd.shape[1]), lambda i: (i, 0)),
-            full, full, pl.BlockSpec((tile, 1), lambda i: (i, 0)), row,
+            pl.BlockSpec((rows, block), lambda j: (0, j)),
+            deep, deep, whole(), whole(), whole(1), row,
         ],
-        out_specs=[full, full, full, row, row],
+        out_specs=[whole(), whole(), whole(), row, row],
         out_shape=[
-            jax.ShapeDtypeStruct((rows, width), jnp.bfloat16),
-            jax.ShapeDtypeStruct((rows, width), jnp.bfloat16),
-            jax.ShapeDtypeStruct((rows, width), jnp.float32),
-            line, line,
+            far_array((rows, width), jnp.bfloat16), jax.ShapeDtypeStruct((rows, width), jnp.bfloat16),
+            far_array((rows, width), jnp.float32), line, line,
         ],
-        compiler_params=pltpu.CompilerParams(vmem_limit_bytes=56 << 20),
-        cost_estimate=pl.CostEstimate(flops=2 * rows * ff * wd.shape[1], bytes_accessed=2 * rows * ff + 2 * ff * wd.shape[1] + 16 * rows * width, transcendentals=0),
+        scratch_shapes=[pltpu.VMEM((rows, width), jnp.float32)],
+        compiler_params=pltpu.CompilerParams(vmem_limit_bytes=48 << 20),
+        cost_estimate=pl.CostEstimate(flops=2 * rows * width * ff, bytes_accessed=2 * (rows + width) * ff + 16 * rows * width, transcendentals=0),
         name="finish",
-    )(scale, hidden, wd, m0, h1, teacher, mask, alpha)
-
-
-def down_back_kernel(g_ref, w0_ref, w1_ref, up_ref, gate_ref, su_ref, sg_ref, gu_ref, gg_ref, gsu_ref, gsg_ref):
+    )(hidden, *down, h1, teacher, mask, alpha)
+
+
+def feed_back_kernel(steps, each, last, g_ref, left_ref, w0_ref, w1_ref, up_ref, gate_ref, su_ref, sg_ref, wu_ref, wg_ref, start_ref, *refs):
     f32 = jnp.float32
     bf16 = jnp.bfloat16
+    step = pl.program_id(0)
     half = w0_ref.shape[1]
+    if last:
+        branch_ref, x_ref, alpha_ref, gsu_ref, gsg_ref, other_ref, own_ref, gb_ref, gx_ref, ga_ref, acc = refs
+        parts = (other_ref, own_ref)
+    else:
+        gsu_ref, gsg_ref, all_ref, acc = refs
+        parts = (all_ref,)
+
+    @pl.when(step == 0)
+    def _():
+        acc[...] = start_ref[...]
+
     su = su_ref[...]
     sg = sg_ref[...]
     back = dot_last(g_ref[:, :half], w0_ref[...]) + dot_last(g_ref[:, half:], w1_ref[...])
@@ -763,42 +811,21 @@
     active = value * sig
     with_active = back * active
     g_value = back * up * su * (sig + active * (1.0 - sig))
-    gu_ref[...] = (with_active * su).astype(bf16)
-    gg_ref[...] = (g_value * sg).astype(bf16)
+    g_up = (with_active * su).astype(bf16)
+    g_gate = (g_value * sg).astype(bf16)
     gsu_ref[...] = jnp.sum(with_active * up, axis=0, keepdims=True)
     gsg_ref[...] = jnp.sum(g_value * gate, axis=0, keepdims=True)
-
-
-def down_back(g, wd, up, gate, scale_up, scale_gate):
-    rows, width = g.shape
-    ff = up.shape[1]
-    block = min(512, ff)
-    col = pl.BlockSpec((rows, block), lambda j: (0, j))
-    line = pl.BlockSpec((1, block), lambda j: (0, j))
-    weight = pl.BlockSpec((block, width // 2), lambda j: (j, 0))
-    big = jax.ShapeDtypeStruct((rows, ff), jnp.bfloat16)
-    small = jax.ShapeDtypeStruct((1, ff), jnp.float32)
-    return pl.pallas_call(
-        down_back_kernel,
-        grid=(ff // block,),
-        in_specs=[pl.BlockSpec((rows, width), lambda j: (0, 0)), weight, weight, col, col, line, line],
-        out_specs=[col, col, line, line],
-        out_shape=[big, big, small, small],
-        compiler_params=pltpu.CompilerParams(vmem_limit_bytes=48 << 20),
-        cost_estimate=pl.CostEstimate(flops=2 * rows * ff * width, bytes_accessed=8 * rows * ff + 2 * ff * width, transcendentals=rows * ff),
-        name="down_back",
-    )(g, *wd, up, gate, scale_up, scale_gate)
-
-
-def up_back_kernel(steps, gu_ref, gg_ref, wu_ref, wg_ref, gz_ref, branch_ref, x_ref, alpha_ref, gb_ref, gx_ref, ga_ref, acc):
-    f32 = jnp.float32
-    step = pl.program_id(0)
-
-    @pl.when(step == 0)
-    def _():
-        acc[...] = gz_ref[...]
-
-    acc[...] += dot_last(gu_ref[...], wu_ref[...]) + dot_last(gg_ref[...], wg_ref[...])
+    acc[...] += dot_last(g_up, wu_ref[...])
+    acc[...] += dot_last(g_gate, wg_ref[...])
+    for n, grad in enumerate((g_up, g_gate)):
+        rows = dot_first(left_ref[...], grad).astype(bf16)
+        at = 0
+        for part in parts:
+            for group in range(part.shape[0]):
+                part[group, n] = rows[at : at + each, :]
+                at += each
+    if not last:
+        return
 
     @pl.when(step == steps - 1)
     def _():
@@ -817,39 +844,60 @@
             gz = z_factor * (grad - h * mean_last(grad * h))
             total = total + jnp.sum(gz * (unit - x), axis=0, keepdims=True)
             back = alpha * gz
-            gb_ref[at : at + tile, :] = (a_factor * (back - unit * mean_last(back * unit))).astype(jnp.bfloat16)
+            gb_ref[at : at + tile, :] = (a_factor * (back - unit * mean_last(back * unit))).astype(bf16)
             gx_ref[at : at + tile, :] = (1.0 - alpha) * gz
         ga_ref[...] = total
 
 
-def up_back(g_up, g_gate, w, gz, branch, tokens, alpha):
-    rows, width = tokens.shape
-    ff = g_up.shape[1]
-    block = min(1024, ff)
-    steps = ff // block
+def feed_back(part, parts, shards, g, left, down, up, gate, scale_up, scale_gate, w, start, rest=None):
+    rows, width = g.shape
+    ff = up.shape[1]
+    block = min(512, ff // parts)
+    steps = ff // parts // block
+    first = part * steps
+    each = width // shards
+    last = rest is not None
     once = pl.Buffered(1)
-    whole = lambda: pl.BlockSpec((rows, width), lambda s: (0, 0), pipeline_mode=once)
-    col = pl.BlockSpec((rows, block), lambda s: (0, s))
-    line = pl.BlockSpec((1, width), lambda s: (0, 0))
+    whole = lambda: pl.BlockSpec((rows, width), lambda j: (0, 0), pipeline_mode=once)
+    col = pl.BlockSpec((rows, block), lambda j: (0, first + j))
+    line = pl.BlockSpec((1, block), lambda j: (0, first + j))
+    sums = pl.BlockSpec((1, block), lambda j: (0, j))
+    row = pl.BlockSpec((1, width), lambda j: (0, 0))
+    deep = pl.BlockSpec((block, width // 2), lambda j: (first + j, 0))
+    small = jax.ShapeDtypeStruct((1, ff // parts), jnp.float32)
+    specs = [
+        whole(), whole(), deep, deep, col, col, line, line,
+        pl.BlockSpec((width, block), lambda j: (0, j)),
+        pl.BlockSpec((width, block), lambda j: (0, steps + j)),
+        whole(),
+    ]
+    operands = [g, left, *down, up, gate, scale_up, scale_gate, w, w, start]
+    groups = shards // 2 if last else shards
+    grads = pl.BlockSpec((groups, 2, each, block), lambda j: (0, 0, 0, j))
+    shape = far_array((groups, 2, each, ff // parts), jnp.bfloat16)
+    full = jax.ShapeDtypeStruct((rows, width), jnp.float32)
+    scratch = []
+    if last:
+        specs += [whole(), whole(), row]
+        operands += rest
+        out_specs = [sums, sums, grads, grads, whole(), whole(), row]
+        out_shape = [small, small, shape, shape, jax.ShapeDtypeStruct((rows, width), jnp.bfloat16), far_array((rows, width), jnp.float32),
+                     jax.ShapeDtypeStruct((1, width), jnp.float32)]
+        scratch = [pltpu.VMEM((rows, width), jnp.float32)]
+    else:
+        out_specs = [sums, sums, grads, pl.BlockSpec((rows, width), lambda j: (0, 0), pipeline_mode=once)]
+        out_shape = [small, small, shape, full]
     return pl.pallas_call(
-        partial(up_back_kernel, steps),
+        partial(feed_back_kernel, steps, each, last),
         grid=(steps,),
-        in_specs=[
-            col, col, pl.BlockSpec((width, block), lambda s: (0, s)),
-            pl.BlockSpec((width, block), lambda s: (0, s + steps)),
-            whole(), whole(), whole(), line,
-        ],
-        out_specs=[whole(), whole(), line],
-        out_shape=[
-            jax.ShapeDtypeStruct((rows, width), jnp.bfloat16),
-            jax.ShapeDtypeStruct((rows, width), jnp.float32),
-            jax.ShapeDtypeStruct((1, width), jnp.float32),
-        ],
-        scratch_shapes=[pltpu.VMEM((rows, width), jnp.float32)],
-        compiler_params=pltpu.CompilerParams(vmem_limit_bytes=60 << 20),
-        cost_estimate=pl.CostEstimate(flops=4 * rows * width * ff, bytes_accessed=4 * ff * (rows + width) + 14 * rows * width, transcendentals=0),
-        name="up_back",
-    )(g_up, g_gate, w, w, gz, branch, tokens, alpha)
+        in_specs=specs,
+        out_specs=out_specs,
+        out_shape=out_shape,
+        scratch_shapes=scratch,
+        compiler_params=pltpu.CompilerParams(vmem_limit_bytes=61 << 20),
+        cost_estimate=pl.CostEstimate(flops=10 * rows * width * ff // parts, bytes_accessed=10 * (rows + width) * ff // parts + 16 * rows * width, transcendentals=rows * ff // parts),
+        name="feed_back",
+    )(*operands)
 
 
 def down_grad_kernel(each, core_ref, h_ref, g_ref, other_ref, own_ref, whole_ref):
@@ -867,7 +915,7 @@
     each = ff // (2 * groups)
     block = min(1024, ff)
     out = pl.BlockSpec((block // 2, width), lambda i: (i, 0))
-    shape = jax.ShapeDtypeStruct((ff // 2, width), jnp.bfloat16)
+    shape = far_array((ff // 2, width), jnp.bfloat16)
     return pl.pallas_call(
         partial(down_grad_kernel, each),
         grid=(ff // block,),
@@ -897,47 +945,71 @@
         at += cols
 
 
-def row_grad(left, right):
-    rows, width = left.shape
-    cols = right.shape[1]
-    block = min(512, cols)
-    out = pl.BlockSpec((width // 2, block), lambda j: (0, j))
-    shape = jax.ShapeDtypeStruct((width // 2, cols), jnp.bfloat16)
+def rows_kernel(count, *refs):
+    lefts, rights, out_ref = refs[:count], refs[count:-1], refs[-1]
+    at = 0
+    for left in lefts:
+        row = left.shape[1]
+        col = 0
+        for right in rights:
+            cols = right.shape[1]
+            out_ref[at : at + row, col : col + cols] = dot_first(left[...], right[...]).astype(jnp.bfloat16)
+            col += cols
+        at += row
+
+
+def out_grad(lefts, right, total):
+    rows, width = right.shape
+    every = sum(left.shape[1] for left in lefts)
+    block = min(512, width)
     return pl.pallas_call(
-        row_grad_kernel,
-        grid=(cols // block,),
-        in_specs=[
-            pl.BlockSpec((rows, width), lambda j: (0, 0)),
-            pl.BlockSpec((rows, block), lambda j: (0, j)),
-        ],
-        out_specs=[out, out],
-        out_shape=[shape, shape],
+        partial(rows_kernel, len(lefts)),
+        grid=(width // block,),
+        in_specs=[pl.BlockSpec(left.shape, lambda j: (0, 0)) for left in lefts]
+        + [pl.BlockSpec((rows, block), lambda j: (0, j))],
+        out_specs=pl.BlockSpec((every, block), lambda j: (0, j)),
+        out_shape=far_array((every, total), jnp.bfloat16),
         compiler_params=pltpu.CompilerParams(vmem_limit_bytes=40 << 20),
-        cost_estimate=pl.CostEstimate(flops=2 * rows * width * cols, bytes_accessed=2 * (rows * width + width * cols + rows * cols), transcendentals=0),
-        name="row_grad",
-    )(left, right)
-
-
-def heads_grad(left, parts):
+        cost_estimate=pl.CostEstimate(flops=2 * rows * width * every, bytes_accessed=2 * (rows * (width + every) + width * every), transcendentals=0),
+        name="out_grad",
+    )(*lefts, right)
+
+
+def heads_grad(left, parts, before=None, wide=0):
     rows, width = left.shape
     cols = parts[0].shape[2]
     count = len(parts)
-    out = pl.BlockSpec((width // 2, cols * count), lambda j: (0, j))
-    shape = jax.ShapeDtypeStruct((width // 2, 3 * cols * count), jnp.bfloat16)
+    each = cols * count
+    lefts = pl.BlockSpec((rows, width), lambda j: (0, 0))
+    rights = [pl.BlockSpec((pl.Squeezed(), rows, cols), lambda j: (j, 0, 0))] * count
+    params = dict(
+        compiler_params=pltpu.CompilerParams(vmem_limit_bytes=40 << 20),
+        cost_estimate=pl.CostEstimate(flops=6 * rows * width * each, bytes_accessed=2 * (rows * width + 3 * (width + rows) * each), transcendentals=0),
+        name="heads_grad",
+    )
+    if before is None:
+        out = pl.BlockSpec((width // 2, each), lambda j: (0, j))
+        shape = far_array((width // 2, 3 * each + wide), jnp.bfloat16)
+        return pl.pallas_call(
+            row_grad_kernel, grid=(3,), in_specs=[lefts] + rights, out_specs=[out, out], out_shape=[shape, shape], **params
+        )(left, *parts)
+    first = before.shape[1] // each - 3
     return pl.pallas_call(
-        row_grad_kernel,
+        rows_under_kernel,
         grid=(3,),
-        in_specs=[pl.BlockSpec((rows, width), lambda j: (0, 0))]
-        + [pl.BlockSpec((pl.Squeezed(), rows, cols), lambda j: (j, 0, 0))] * count,
-        out_specs=[out, out],
-        out_shape=[shape, shape],
-        compiler_params=pltpu.CompilerParams(vmem_limit_bytes=40 << 20),
-        cost_estimate=pl.CostEstimate(flops=6 * rows * width * cols * count, bytes_accessed=2 * (rows * width + 3 * (width + rows) * cols * count), transcendentals=0),
-        name="heads_grad",
-    )(left, *parts)
-
-
-def input_grad_kernel(base_ref, *refs):
+        in_specs=[lefts] + rights + [pl.BlockSpec(memory_space=pl.ANY)],
+        out_specs=pl.BlockSpec((width, each), lambda j: (0, first + j)),
+        out_shape=far_array(before.shape, jnp.bfloat16),
+        input_output_aliases={1 + count: 0},
+        **params,
+    )(left, *parts, before)
+
+
+def rows_under_kernel(left_ref, *refs):
+    rows_kernel(1, left_ref, *refs[:-2], refs[-1])
+
+
+def input_grad_kernel(scale_ref, base_ref, *refs):
     out_ref = refs[-1]
     count = len(refs) // 3
     total = base_ref[...]
@@ -948,10 +1020,10 @@
             at = 2 * p * cols
             total = total + dot_last(first[p], w[:, at : at + cols])
             total = total + dot_last(second[p], w[:, at + cols : at + 2 * cols])
-    out_ref[...] = total
-
-
-def input_grad(base, parts, weights):
+    out_ref[...] = total * scale_ref[0]
+
+
+def input_grad(scale, base, parts, weights):
     rows, width = base.shape
     tile = min(256, width)
     out = pl.BlockSpec((rows, tile), lambda j: (0, j))
@@ -966,60 +1038,62 @@
     return pl.pallas_call(
         input_grad_kernel,
         grid=(width // tile,),
-        in_specs=[out] + specs,
+        in_specs=[pl.BlockSpec(memory_space=pltpu.SMEM), out] + specs,
         out_specs=out,
         out_shape=jax.ShapeDtypeStruct((rows, width), jnp.float32),
         compiler_params=pltpu.CompilerParams(vmem_limit_bytes=48 << 20),
         cost_estimate=pl.CostEstimate(flops=flops, bytes_accessed=20 * rows * width, transcendentals=0),
         name="input_grad",
-    )(base, *operands)
-
-
-def slots_kernel(count, uses, slots_ref, keep_ref, got_ref, *refs):
-    extras, out_ref, acc = refs[:-2], refs[-2], refs[-1]
+    )(scale, base, *operands)
+
+
+def slots_kernel(plan, rows, extras, slots, keep, got, *refs):
     f32 = jnp.float32
-    acc[...] = keep_ref[...].astype(f32) + got_ref[...].astype(f32)
-    for n, extra in enumerate(extras):
-        takers = [i for i in range(count) if uses[n][i] is not None]
-        if len(takers) == count:
-            acc[...] += extra[...].astype(f32)
-            continue
-        for i in takers:
-
-            @pl.when(pl.program_id(0) == i)
-            def _(extra=extra):
-                acc[...] += extra[...].astype(f32)
-
-    out_ref[...] = acc[...].astype(out_ref.dtype)
-
-
-def add_slots(keep, got, rows, slots, extras=()):
-    count = len(slots)
+    terms = refs[:extras]
+    outs = refs[extras : extras + len(plan)]
+    kept, gotten, sems = refs[extras + len(plan) :]
+    total = sum(len(blocks) for blocks in plan)
+    copies = []
+    for b in range(total):
+        place = pl.ds(pl.multiple_of(slots[b] * rows, rows), rows)
+        pair = (
+            pltpu.make_async_copy(keep.at[place], kept.at[b], sems.at[0, b]),
+            pltpu.make_async_copy(got.at[place], gotten.at[b], sems.at[1, b]),
+        )
+        for copy in pair:
+            copy.start()
+        copies.append(pair)
+    b = 0
+    for out, blocks in zip(outs, plan):
+        for n, uses in enumerate(blocks):
+            for copy in copies[b]:
+                copy.wait()
+            value = kept[b].astype(f32) + gotten[b].astype(f32)
+            for term, at in uses:
+                value = value + terms[term][at * rows : (at + 1) * rows, :].astype(f32)
+            out[n * rows : (n + 1) * rows, :] = value.astype(out.dtype)
+            b += 1
+
+
+def add_slots(keep, got, rows, slots, plan, terms=()):
     cols = keep.shape[1]
-    uses = [use for _, use in extras]
-    specs = [pl.BlockSpec((rows, cols), lambda i, s: (s[i], 0))] * 2
-    for _, use in extras:
-        first = next(u for u in use if u is not None)
-        if all(u is None or u == first for u in use):
-            specs.append(pl.BlockSpec((rows, cols), lambda i, s, first=first: (first, 0)))
-        else:
-            assert use == list(range(count))
-            specs.append(pl.BlockSpec((rows, cols), lambda i, s: (i, 0)))
-    grid = pltpu.PrefetchScalarGridSpec(
-        num_scalar_prefetch=1,
-        grid=(count,),
-        in_specs=specs,
-        out_specs=pl.BlockSpec((rows, cols), lambda i, s: (i, 0)),
-        scratch_shapes=[pltpu.VMEM((rows, cols), jnp.float32)],
-    )
+    total = len(slots)
+    vmem = pl.BlockSpec(memory_space=pltpu.VMEM)
+    block = rows * cols
     return pl.pallas_call(
-        partial(slots_kernel, count, uses),
-        grid_spec=grid,
-        out_shape=jax.ShapeDtypeStruct((count * rows, cols), keep.dtype),
-        compiler_params=pltpu.CompilerParams(vmem_limit_bytes=40 << 20),
-        cost_estimate=pl.CostEstimate(flops=0, bytes_accessed=8 * count * rows * cols, transcendentals=0),
+        partial(slots_kernel, plan, rows, len(terms)),
+        in_specs=[pl.BlockSpec(memory_space=pltpu.SMEM)] + [pl.BlockSpec(memory_space=pl.ANY)] * 2 + [vmem] * len(terms),
+        out_specs=[vmem] * len(plan),
+        out_shape=[jax.ShapeDtypeStruct((len(blocks) * rows, cols), keep.dtype) for blocks in plan],
+        scratch_shapes=[
+            pltpu.VMEM((total, rows, cols), keep.dtype),
+            pltpu.VMEM((total, rows, cols), keep.dtype),
+            pltpu.SemaphoreType.DMA((2, total)),
+        ],
+        compiler_params=pltpu.CompilerParams(vmem_limit_bytes=8 * total * block + 8 * block + (4 << 20)),
+        cost_estimate=pl.CostEstimate(flops=0, bytes_accessed=8 * total * block, transcendentals=0),
         name="add_slots",
-    )(jnp.stack(slots).astype(jnp.int32), keep, got, *[e for e, _ in extras])
+    )(jnp.stack(slots).astype(jnp.int32), far(keep), far(got), *terms)
 
 
 def body(
@@ -1054,79 +1128,100 @@
         return jnp.concatenate([w[:, s : s + size] for s in starts], axis=1)
 
     chunks = [columns(w_qkv, [p * width + n * half for p in range(3)], half) for n in range(2)]
+    vectors = (s_qk, alpha_attn, s_up, s_gate, alpha_mlp)
+    short = jnp.concatenate(vectors).reshape(each, -1)
+    per_row = short.shape[1]
+    chunks[0] = jnp.concatenate([chunks[0], jnp.pad(short, ((0, 0), (0, PAIR - per_row)))], axis=1)
     chunks.append(w_out)
-    full_up = lax.all_gather(w_upgate, "shard", axis=0, tiled=True)
     chunks += [w_down[:, :half], w_down[:, half:]]
 
-    gather = Gather(at, chunks)
+    gather = Gather(at, chunks[:3])
+    late = Gather(at, chunks[3:])
+    mask = valid.astype(f32)
+    upgate = [
+        lax.all_gather(columns(w_upgate, [n * ff // 2, ff + n * ff // 2], ff // 2), "shard", axis=0, tiled=True)
+        for n in range(2)
+    ]
     gate = []
     for tick in range(4):
-        gate = gather.tick(tick, gate)
-    vectors = gather_vectors(at, (s_qk, alpha_attn, s_up, s_gate, alpha_mlp))
-    f_sqk, f_aa, f_su, f_sg, f_am = (v.astype(f32).reshape(1, -1) for v in vectors)
-    mask = valid.astype(f32)
-    count = jnp.maximum(sum_everywhere(at, jnp.full((8, 128), jnp.sum(mask)))[0, 0], 1.0)
-    scale = (2.0 * rows * at.reps * at.shards / count).reshape(1)
-    cosine, sine = rotary_wide(positions.reshape(rows))
-    x_sorted = sorted_cores(tokens, core, each)
-    gate += [x_sorted, cosine, f_sqk, scale]
-
+        moved = gather.tick(tick, gate)
+        if tick == 3:
+            late.tick(0, gate)
+        if tick == 0:
+            cosine, sine = rotary_wide(positions.reshape(rows))
+            moved += [cosine, sine]
+        if tick == 1:
+            x_sorted = sorted_cores(after(tokens, gate + gather.sends), core, each)
+            moved += [x_sorted]
+        gate = moved
     def dot(left, right):
         return jnp.dot(left, right, preferred_element_type=f32).astype(bf16)
 
     weights, qkv, att, lse = {}, [], [], []
     for n in range(2):
         moved = gather.tick(4 + n, gate)
+        late.tick(1 + n, gate)
+        gate = gate + gather.sends
         weights[n] = gather.full(n)
-        qkv.append(dot(after(tokens, gate), weights[n]))
+        if n == 0:
+            found = weights[0][:, 3 * half : 3 * half + per_row].astype(f32).reshape(at.shards, -1)
+            shorts, place = [], 0
+            for vector in vectors:
+                size = vector.shape[0]
+                shorts.append(found[:, place : place + size].reshape(1, -1))
+                place += size
+            f_sqk, f_aa, f_su, f_sg, f_am = shorts
+        qkv.append(dot(after(tokens, gate), weights[n][:, : 3 * half]))
         out, sums = attention(qkv[n], cosine, sine, f_sqk, segs, n * half)
         att.append(out)
         lse.append(sums)
         gate = moved + [out]
-    moved = gather.tick(6, gate)
+    late.tick(3, gate)
     weights[2] = gather.full(2)
     att = [after(a, gate) for a in att]
-    branch_a, h_one, h_low, h_sorted, att_sorted = after_attention(core, each, att, weights[2], tokens, f_aa)
-    gate = moved + [h_low]
-    moved = gather.tick(7, gate)
-    up, gate_part, hidden = feed_up(after(h_low, moved), full_up, f_su, f_sg)
-    down = [gather.full(3), gather.full(4)]
-    m_first = jnp.dot(hidden, down[0], preferred_element_type=f32)
+    branch_a, h_one, h_low, h_sorted = after_attention(
+        core, each, [far(a) for a in att], weights[2], tokens, f_aa
+    )
+    before = feed_up(0, 2, h_low, upgate[0], f_su, f_sg, [])
+    late.tick(4, [before[2]])
+    before = feed_up(1, 2, after(h_low, [before[2]]), upgate[1], f_su, f_sg, before)
+    down = [late.full(0), late.full(1)]
+    up, gate_part, hidden = before
     output, g_bm, gz, grad_am, loss_rows = finish(
-        scale, hidden, down[1], m_first, h_one, teacher, mask.reshape(rows, 1), f_am
+        hidden, down, h_one, teacher, mask.reshape(rows, 1), f_am
     )
 
-    lanes = []
     waiting = {}
 
-    def window(gate, enter):
+    def window(gate, names, late=()):
         moved = []
-        for name in enter:
-            lanes.append(waiting[name])
-        for chunk in lanes:
-            if chunk.stage < 5:
-                moved += chunk.step(gate)
-        return moved
-
-    def start(name, left, right, gate):
-        waiting[name] = Reduce(at, *row_grad(left, after(right, gate)))
-        return [waiting[name].send, waiting[name].keep]
-
-    def dot_rows(left, right):
-        return lax.dot_general(left, right, (((0,), (0,)), ((), ())), preferred_element_type=f32).astype(bf16)
-
-    sides = down_grad(core, hidden, g_bm, groups)
-    waiting["down"] = Reduce(at, *sides)
-    gate = list(sides)
-    moved = window(gate, ["down"])
-    g_up, g_gate, grad_su, grad_sg = down_back(after(g_bm, gate), down, up, gate_part, f_su, f_sg)
-    gate = moved + [g_up]
-    moved = window(gate, [])
-    own_up = lax.psum_scatter(dot_rows(after(h_low, gate), g_up), "shard", scatter_dimension=0, tiled=True)
-    done = start("gate", h_sorted, g_gate, gate)
-    gate = moved + done
-    moved = window(gate, ["gate"])
-    g_ba, gx_base, grad_aa = up_back(after(g_up, gate), g_gate, full_up, gz, branch_a, tokens, f_aa)
+        sends = list(gate)
+        for name in names:
+            moved += waiting[name].step(gate)
+            sends += waiting[name].sends
+        for name in late:
+            waiting[name].step(gate)
+            sends += waiting[name].sends
+        return moved, sends
+
+    upper = lax.broadcasted_iota(jnp.int32, (8, 128), 0) < 4
+    counted = Sum(at, jnp.where(upper, jnp.sum(loss_rows), jnp.sum(mask)))
+    waiting["down"] = Reduce(at, *down_grad(core, hidden, g_bm, groups))
+    gate = [waiting["down"].send, waiting["down"].keep]
+    moved, gate = window(gate, ["down"])
+    moved += counted.step(gate)
+    su0, sg0, first_up, acc = feed_back(
+        0, 2, at.shards, after(g_bm, gate), h_low, down, up, gate_part, f_su, f_sg, upgate[0], gz
+    )
+    gate = moved + [acc]
+    moved, gate = window(gate, ["down"])
+    moved += counted.step(gate)
+    first_up = lax.psum_scatter(after(first_up, gate), "shard", scatter_dimension=0, tiled=True)
+    su1, sg1, up_other, up_own, g_ba, gx_base, grad_aa = feed_back(
+        1, 2, at.shards, after(g_bm, gate), h_sorted, down, up, gate_part, f_su, f_sg, upgate[1], acc,
+        [branch_a, tokens, f_aa],
+    )
+    waiting["up"] = Reduce(at, up_other.reshape(width, ff // 2), up_own.reshape(width, ff // 2))
     gate = moved + [g_ba]
 
     g3, g_scale = {}, []
@@ -1141,55 +1236,76 @@
         g_scale.append(sums[:, 0, :].reshape(-1))
         return [out]
 
-    def start_qkv(n, gate):
-        sides = heads_grad(after(x_sorted, gate), [g3[2 * n], g3[2 * n + 1]])
-        waiting[f"qkv{n}"] = Reduce(at, *sides)
-        return list(sides)
-
-    moved = window(gate, [])
+    moved, gate = window(gate, ["up"], ["down"])
+    moved += counted.step(gate)
     g_att = lax.dot_general(
         after(g_ba, gate), weights[2], (((1,), (1,)), ((), ())), preferred_element_type=f32
     ).astype(bf16)
-    done = start("out", att_sorted, g_ba, gate)
-    gate = moved + done + back(0, gate)
-    moved = window(gate, ["out"])
-    gate = moved + back(1, gate)
-    moved = window(gate, [])
-    done = start_qkv(0, gate)
-    gate = moved + done + back(2, gate)
-    moved = window(gate, ["qkv0"])
-    gate = moved + back(3, gate)
-    moved = window(gate, [])
-    gate = moved + start_qkv(1, gate)
-    moved = window(gate, ["qkv1"])
-    grad_x = input_grad(after(gx_base, gate), [g3[n] for n in range(4)], [weights[0], weights[1]])
-    parts = [
-        jnp.concatenate(g_scale), grad_aa.reshape(-1), grad_su.reshape(-1), grad_sg.reshape(-1),
-        grad_am.reshape(-1), jnp.sum(loss_rows).reshape(1),
+    attended = out_grad(att, after(g_ba, gate), width + 3 * half)
+    gate = moved + [g_att]
+    moved, gate = window(gate, ["up"])
+    moved += counted.step(gate)
+    back(0, gate)
+    gate = moved + back(1, [g3[0]])
+    over_x, gate = window(gate, ["up"])
+    over_x += counted.step(gate)
+    attended = heads_grad(after(tokens, gate), [g3[0], g3[1]], attended)
+    own_att = lax.psum_scatter(attended, "shard", scatter_dimension=0, tiled=True)
+    moved, gate = window([attended], ["down"])
+    back(2, gate)
+    first_up = after(first_up.reshape(2 * each, ff // 2), [g3[2]])
+    last_up = at.along_y(first_up)
+    gate = moved + over_x + back(3, [g3[2]])
+    counts = counted.total()
+    count = jnp.maximum(counts[4, 0], 1.0)
+    loss = counts[0, 0] / count
+    scale = rows * at.reps * at.shards / count
+    over_z, gate = window(gate, ["up"])
+    sides = heads_grad(after(x_sorted, gate), [g3[2], g3[3]], wide=PAIR)
+    shorts = [
+        jnp.concatenate(g_scale), grad_aa.reshape(-1), jnp.concatenate([su0, su1], axis=1).reshape(-1),
+        jnp.concatenate([sg0, sg1], axis=1).reshape(-1), grad_am.reshape(-1),
     ]
-    sizes = [p.shape[0] for p in parts]
-    flat = jnp.concatenate(parts)
-    tall = -(-flat.shape[0] // 1024) * 8
-    flat = jnp.pad(flat, (0, tall * 128 - flat.shape[0])).reshape(tall, 128)
-    flat = sum_everywhere(at, flat).reshape(-1)
-    gate = moved + [grad_x]
-    while any(chunk.stage < 5 for chunk in lanes):
-        gate = window(gate, [])
-    owned = []
-    place = 0
-    for size in sizes[:-1]:
-        mine = size // at.shards
-        owned.append(lax.dynamic_slice_in_dim(flat, place + at.shard * mine, mine))
-        place += size
-    loss = flat[place] / count
-    total = {name: chunk.total() for name, chunk in waiting.items()}
-    own_up = after(own_up, gate)
-    own_up = over_copies(at, own_up.astype(f32), 1)
-    halves = lambda value: [value[:, p * half : (p + 1) * half] for p in range(3)]
-    q0, q1 = halves(total["qkv0"]), halves(total["qkv1"])
-    own_qkv = jnp.concatenate([part for pair in zip(q0, q1) for part in pair], axis=1)
-    own_up = jnp.concatenate([own_up, total["gate"]], axis=1)
-    return (output, loss, grad_x, own_qkv, total["out"], own_up, total["down"], *owned)
+    shorts = jnp.concatenate([s.reshape(at.shards, -1) for s in shorts], axis=1).astype(bf16)
+    shorts = jnp.pad(shorts.reshape(groups, NC, each, per_row), ((0, 0), (0, 0), (0, 0), (0, PAIR - per_row)))
+    sides = [
+        lax.dynamic_update_slice(
+            side, lax.dynamic_index_in_dim(shorts, which, axis=1, keepdims=False).reshape(-1, PAIR), (0, 3 * half)
+        )
+        for side, which in zip(sides, (1 - at.core, at.core))
+    ]
+    waiting["qkv1"] = Reduce(at, *sides)
+    gate = list(sides) + [last_up]
+    gate, _ = window(gate, ["qkv1"])
+    gate, _ = window(gate, ["qkv1"])
+    moved, sends = window(gate, ["qkv1"])
+    last_down, _ = window(gate, ["down"])
+    moved += last_down
+    grad_x = input_grad(
+        scale.reshape(1), after(gx_base, sends), [g3[n] for n in range(4)], [weights[0], weights[1]]
+    )
+    gate = moved + over_z + [grad_x]
+    gate, _ = window(gate, ["qkv1", "up"])
+    own_att = after(own_att, gate)
+    last_att = at.along_y(own_att)
+    window(gate, ["qkv1"])
+    total = {name: chunk.total() * scale for name, chunk in waiting.items()}
+
+    def whole(mine, other):
+        return over_copies(at, mine.astype(f32) + other.astype(f32), 2) * scale
+
+    attended = whole(own_att, last_att)
+    q0, q1 = (jnp.split(v, 3, axis=1) for v in (attended[:, width:], total["qkv1"][:, : 3 * half]))
+    shorts = total["qkv1"][:, 3 * half : 3 * half + per_row].reshape(-1)
+    owned, place = [], 0
+    for vector in vectors:
+        owned.append(shorts[place : place + vector.shape[0]])
+        place += vector.shape[0]
+    own_qkv = jnp.concatenate([part for two in zip(q0, q1) for part in two], axis=1)
+    first_up = whole(first_up, last_up)
+    ups = [first_up[:each], total["up"][:each], first_up[each:], total["up"][each:]]
+    own_up = jnp.concatenate(ups, axis=1)
+    return (output, loss, grad_x, own_qkv, attended[:, :width], own_up, total["down"], *owned)
 
 
 def solution(mesh):

time: 661 us -> 565 us (0.85)
  waiting for transfers between devices: 152 us -> 80.5 us
  Pallas kernels: 278 us -> 317 us
  local copies, waits for them, and re-layouts: 86.9 us -> 53 us
  matrix products: 33.7 us -> 13 us
    ppermute x10 -> x8, waiting for transfers between devices: 54 us -> 15.5 us  [along_x(): lax.ppermute(value, AXES, self.moves(lambda r, z, x, c: (r, z, x ^ j, c)))]
    unnamed x293 -> x168, local copies, waits for them, and re-layouts: 70.4 us -> 32.6 us
    pallas_call x38 -> x24, Pallas kernels: 146 us -> 175 us  [the longest x2 79.6 us: feed_back(): pl.pallas_call(partial(feed_back_kernel, steps, each, last), grid=(steps,...]
    ppermute x10 -> x8, waiting for transfers between devices: 43.3 us -> 19 us  [far_z(): lax.ppermute(value, AXES, self.moves(lambda r, z, x, c: (r, z ^ 2 + r % 2...]
    ppermute x15 -> x5, waiting for transfers between devices: 23.1 us -> 0.01 us  [flat(): return lax.ppermute(value, AXES, [(i, i ^ bit) for i in range(count)])]
    dot_general x2 -> x0, matrix products: 22.8 us -> none  [the longest x1 14.6 us: dot_rows(): lax.dot_general(left, right, (((0,), (0,)), ((), ())), preferred_element_...]
    ppermute x10 -> x8, waiting for transfers between devices: 10.3 us -> 30.7 us  [near_z(): lax.ppermute(value, AXES, self.moves(lambda r, z, x, c: (r, z ^ 1, x, c)))]
    ppermute x15 -> x13, waiting for transfers between devices: 20.8 us -> 11.2 us  [along_y(): lax.ppermute(value, AXES, self.moves(lambda r, z, x, c: (r ^ 1, z, x, c)))]
  transfers between devices with their start and end apart: 72 -> 54, of which waited for: 29 -> 18; matrix products, arithmetic and copies ran while one was open for 10% -> 9% of each run, Pallas kernels for 34% -> 49%
where the time goes in v2:
time: 565 us; the launch traced here: 564 us
  Pallas kernels  317 us (56%)
  waiting for transfers between devices  80.5 us (14%)
  starting transfers between devices  63.1 us (11%)
  local copies, waits for them, and re-layouts  53 us (9%)
  other arithmetic  19.1 us (3%)
  between operations  17.9 us (3%)
  matrix products  13 us (2%)
    pallas_call x2, Pallas kernels, feed_back(): pl.pallas_call(partial(feed_back_kernel, steps, each, last), grid=(steps,...  79.6 us
    pallas_call x4, Pallas kernels, attention_back(): pl.pallas_call(partial(attend_back_kernel, math.sqrt(HEAD)), grid=(pairs,...  61.6 us
    unnamed x168, local copies, waits for them, and re-layouts  32.6 us
    pallas_call x12, Pallas kernels, add_slots(): pl.pallas_call(partial(slots_kernel, plan, rows, len(terms)), in_specs=[p...  31.5 us
    ppermute x8, waiting for transfers between devices, near_z(): lax.ppermute(value, AXES, self.moves(lambda r, z, x, c: (r, z ^ 1, x, c)))  30.7 us
    pallas_call x2, Pallas kernels, feed_up(): pl.pallas_call(up_kernel, grid=(steps,), in_specs=[pl.BlockSpec((rows, wi...  27.6 us
    ppermute x13, starting transfers between devices, along_y(): lax.ppermute(value, AXES, self.moves(lambda r, z, x, c: (r ^ 1, z, x, c)))  23.7 us
    pallas_call x2, Pallas kernels, attention(): pl.pallas_call(partial(attend_kernel, math.sqrt(HEAD)), grid=(pairs,), in...  23.1 us
  transfers between devices with their start and end apart: 54, of which 18 were waited for; matrix products, arithmetic and copies ran while one was open for 9% of the time, Pallas kernels for 49%

profile of v2, /device:TPU:0, one launch (start us, length us, event | category | flops | bytes accessed | tf_op | source)
XLA Modules:
  0.0 563.7 jit_solution(3375470668639809516)
XLA Ops:
  10.8 4.1 collective-permute-start.1
  27.9 5.8 %collective-permute-start.2 = (bf16[64,1536]{1,0:T(8,128)(2,1)S(1)}, bf16[64,1536]{1,0:T(8,128)(2,1)S(1)}, u32[]{:S(2)}, u32[]{:S(2)}) collective-permute-start(bf16[64,1536]{1,0:T(8,128)(2,1)S(1)} %pad_maximum_fusion.15.refs_0_), channel_id=1, source_target_pairs={{0,4},{1,5},{2,6},{3,7},{4,0},{5,1},{6,2},{7,3},{8,12},{9,13},{10,... | collective-permute-start | bytes 589832 | tf_op jit(solution)/shard_map/ppermute | solution.py:48
  38.8 11.0 %collective-permute-done.2.refs_1_ = bf16[64,1536]{1,0:T(8,128)(2,1)S(1)} collective-permute-done((bf16[64,1536]{1,0:T(8,128)(2,1)S(1)}, bf16[64,1536]{1,0:T(8,128)(2,1)S(1)}, u32[]{:S(2)}, u32[]{:S(2)}) %collective-permute-start.2) | collective-permute-done | bytes 196640 | tf_op jit(solution)/shard_map/ppermute | solution.py:48
  58.9 10.9 %collective-permute-done.7 = bf16[128,1536]{1,0:T(8,128)(2,1)S(1)} collective-permute-done((bf16[128,1536]{1,0:T(8,128)(2,1)S(1)}, bf16[128,1536]{1,0:T(8,128)(2,1)S(1)}, u32[]{:S(2)}, u32[]{:S(2)}) %collective-permute-start.7) | collective-permute-done | bytes 393248 | tf_op jit(solution)/shard_map/ppermute | solution.py:54
  73.3 5.9 %collective-permute-start.10 = (bf16[192,1536]{1,0:T(8,128)(2,1)S(1)}, bf16[192,1536]{1,0:T(8,128)(2,1)S(1)}, u32[]{:S(2)}, u32[]{:S(2)}) collective-permute-start(bf16[192,1536]{1,0:T(8,128)(2,1)S(1)} %pad_maximum_fusion.4), channel_id=1, source_target_pairs={{0,16},{1,17},{2,18},{3,19},{4,20},{5,21},{6,22},{7,23},{8,24},{9,... | collective-permute-start | bytes 1769480 | tf_op jit(solution)/shard_map/ppermute | solution.py:57
  79.3 4.6 collective-permute-done.9
  87.7 11.8 %collective-permute-done.16.refs_2_ = bf16[256,512]{1,0:T(8,128)(2,1)S(1)} collective-permute-done((bf16[256,512]{1,0:T(8,128)(2,1)S(1)}, bf16[256,512]{1,0:T(8,128)(2,1)S(1)}, u32[]{:S(2)}, u32[]{:S(2)}) %collective-permute-start.16) | collective-permute-done | bytes 262176 | tf_op jit(solution)/shard_map/ppermute | solution.py:51
  102.8 6.8 %collective-permute-start.12 = (bf16[192,1024]{1,0:T(8,128)(2,1)}, bf16[192,1024]{1,0:T(8,128)(2,1)}, u32[]{:S(2)}, u32[]{:S(2)}) collective-permute-start(bf16[192,1024]{1,0:T(8,128)(2,1)} %pad_maximum_fusion.13), channel_id=1, source_target_pairs={{0,16},{1,17},{2,18},{3,19},{4,20},{5,21},{6,22},{7,23},{8,24},{9,... | collective-permute-start | bytes 1179656 | tf_op jit(solution)/shard_map/ppermute | solution.py:57
  116.0 5.6 convolution_convert_fusion.1.q_ref.k_ref.v_ref
  121.7 11.5 %attend.2 = (bf16[1024,512]{1,0:T(8,128)(2,1)}, f32[1024,512]{1,0:T(8,128)}) custom-call(bf16[1024,1536]{1,0:T(8,128)(2,1)S(1)} %convolution_convert_fusion.1.q_ref.k_ref.v_ref, bf16[1024,1536]{1,0:T(8,128)(2,1)S(1)} %convolution_convert_fusion.1.q_ref.k_ref.v_ref, bf16[1024,1536]{1,0:T(8,128)(2,1)S(1)} %convolution_convert_fusion.1.q_ref.k_ref.v_ref, ...), custom_call_target="tpu_custom_call" | custom-call | flops 4294967296 | bytes 4194304 | tf_op jit(solution)/shard_map/attend/pallas_call | solution.py:429
  153.2 11.6 %attend.3 = (bf16[1024,512]{1,0:T(8,128)(2,1)}, f32[1024,512]{1,0:T(8,128)}) custom-call(bf16[1024,1536]{1,0:T(8,128)(2,1)S(1)} %convolution_convert_fusion.q_ref.k_ref.v_ref, bf16[1024,1536]{1,0:T(8,128)(2,1)S(1)} %convolution_convert_fusion.q_ref.k_ref.v_ref, bf16[1024,1536]{1,0:T(8,128)(2,1)S(1)} %convolution_convert_fusion.q_ref.k_ref.v_ref, ...), custom_call_target="tpu_custom_call" | custom-call | flops 4294967296 | bytes 4194304 | tf_op jit(solution)/shard_map/attend/pallas_call | solution.py:429
  169.1 11.0 %weave.7 = bf16[8,2,64,1024]{3,2,1,0:T(8,128)(2,1)S(1)} custom-call(s32[1]{0:T(128)} %bitcast.core_ref.core, bf16[8,64,1024]{2,1,0:T(8,128)(2,1)S(1)} %bitcast.56, bf16[8,64,1024]{2,1,0:T(8,128)(2,1)S(1)} %bitcast.71), custom_call_target="tpu_custom_call" | custom-call | bytes 4194304 | tf_op jit(solution)/shard_map/weave/pallas_call | solution.py:116
  180.1 7.8 %after_attention.1 = (f32[1024,1024]{1,0:T(8,128)S(1)}, f32[1024,1024]{1,0:T(8,128)}, bf16[1024,1024]{1,0:T(8,128)(2,1)S(1)}, bf16[1024,1024]{1,0:T(8,128)(2,1)S(1)}) custom-call(s32[1]{0:T(128)} %bitcast.core_ref.core, bf16[1024,512]{1,0:T(8,128)(2,1)} %get-tuple-element.134.a0_ref.o_ref.refs_0_, bf16[1024,512]{1,0:T(8,128)(2,1)} %get-tuple-element.135.a1_ref.refs_1_.o_ref, ...), custom_call_target="tpu_custom_call" | custom-call | flops 2147483648 | bytes 20971520 | tf_op jit(solution)/shard_map/after_attention/pallas_call | solution.py:657
  195.6 13.8 %feed_up.2 = (bf16[1024,4096]{1,0:T(8,128)(2,1)}, bf16[1024,4096]{1,0:T(8,128)(2,1)}, bf16[1024,4096]{1,0:T(8,128)(2,1)}) custom-call(bf16[1024,1024]{1,0:T(8,128)(2,1)S(1)} %copy-done.13, bf16[1024,4096]{1,0:T(8,128)(2,1)} %all-gather.3.cloned.1.call-done.wu_ref.wg_ref, bf16[1024,4096]{1,0:T(8,128)(2,1)} %all-gather.3.cloned.1.call-done.wu_ref.wg_ref, ...), custom_call_target="tpu_custom_call" | custom-call | flops 8589934592 | bytes 23068672 | tf_op jit(solution)/shard_map/feed_up/pallas_call | solution.py:698
  216.1 13.7 %feed_up.3 = (bf16[1024,4096]{1,0:T(8,128)(2,1)}, bf16[1024,4096]{1,0:T(8,128)(2,1)}, bf16[1024,4096]{1,0:T(8,128)(2,1)}) custom-call(bf16[1024,1024]{1,0:T(8,128)(2,1)S(1)} %copy-done.14, bf16[1024,4096]{1,0:T(8,128)(2,1)} %all-gather.5.cloned.1.call-done.wu_ref.wg_ref, ...), custom_call_target="tpu_custom_call", output_to_operand_aliasing={{0}: (5, {}), {1}: (6, {}), {2}: (7, {})} | custom-call | flops 8589934592 | bytes 23068672 | tf_op jit(solution)/shard_map/feed_up/pallas_call | solution.py:698
  235.5 21.2 %finish.1 = (bf16[1024,1024]{1,0:T(8,128)(2,1)}, bf16[1024,1024]{1,0:T(8,128)(2,1)S(1)}, f32[1024,1024]{1,0:T(8,128)}, f32[1,1024]{1,0:T(1,128)S(1)}, f32[1,1024]{1,0:T(1,128)S(1)}) custom-call(bf16[1024,4096]{1,0:T(8,128)(2,1)} %get-tuple-element.141.hid_ref.h_ref, bf16[4096,512]{1,0:T(8,128)(2,1)} %bitcast.57, bf16[4096,512]{1,0:T(8,128)(2,1)} %bitcast.60, ...), custom_call_target="tpu_custom_call" | custom-call | flops 8589934592 | bytes 33554432 | tf_op jit(solution)/shard_map/finish/pallas_call | solution.py:769
  256.8 12.1 %down_grad.1 = (bf16[2048,1024]{1,0:T(8,128)(2,1)}, bf16[2048,1024]{1,0:T(8,128)(2,1)}) custom-call(s32[1]{0:T(128)} %bitcast.core_ref.core, bf16[1024,4096]{1,0:T(8,128)(2,1)S(1)} %bitcast.54, bf16[1024,1024]{1,0:T(8,128)(2,1)S(1)} %get-tuple-element.165.g_ref), custom_call_target="tpu_custom_call" | custom-call | flops 8589934592 | bytes 18874368 | tf_op jit(solution)/shard_map/down_grad/pallas_call | solution.py:919
  272.1 35.1 %feed_back.2 = (f32[1,2048]{1,0:T(1,128)}, f32[1,2048]{1,0:T(1,128)}, bf16[16,2,64,2048]{3,2,1,0:T(8,128)(2,1)}, f32[1024,1024]{1,0:T(8,128)}) custom-call(bf16[1024,1024]{1,0:T(8,128)(2,1)} %copy-done.58, bf16[1024,1024]{1,0:T(8,128)(2,1)} %copy-done.12, bf16[4096,512]{1,0:T(8,128)(2,1)} %bitcast.58, bf16[4096,512]{1,0:T(8,128)(2,1)} %bitcast.61, ...), custom_call_target="tpu_custom_call" | custom-call | flops 21474836480 | bytes 58720256 | tf_op jit(solution)/shard_map/feed_back/pallas_call | solution.py:890
  310.2 44.6 %feed_back.3 = (f32[1,2048]{1,0:T(1,128)}, f32[1,2048]{1,0:T(1,128)}, bf16[8,2,64,2048]{3,2,1,0:T(8,128)(2,1)}, bf16[8,2,64,2048]{3,2,1,0:T(8,128)(2,1)}, bf16[1...) custom-call(bf16[1024,1024]{1,0:T(8,128)(2,1)} %copy-done.58, bf16[1024,1024]{1,0:T(8,128)(2,1)} %copy-done.52, ...), custom_call_target="tpu_custom_call" | custom-call | flops 21474836480 | bytes 58720256 | tf_op jit(solution)/shard_map/feed_back/pallas_call | solution.py:890
  357.6 4.1 add_slots.13
  380.2 15.1 %attend_back.4 = (bf16[3,1024,256]{2,1,0:T(8,128)(2,1)}, f32[2,8,128]{2,1,0:T(8,128)S(1)}) custom-call(bf16[1024,1536]{1,0:T(8,128)(2,1)} %copy-done.53, bf16[1024,1536]{1,0:T(8,128)(2,1)} %copy-done.53, bf16[1024,1536]{1,0:T(8,128)(2,1)} %copy-done.53, bf16[1024,512]{1,0:T(8,128)(2,1)} %get-tuple-element.134.a0_ref.o_ref.refs_0_, ...), custom_call_target="tpu_custom_call" | custom-call | flops 16106127360 | bytes 4718592 | tf_op jit(solution)/shard_map/attend_back/pallas_call | solution.py:545
  395.3 15.5 %attend_back.5 = (bf16[3,1024,256]{2,1,0:T(8,128)(2,1)}, f32[2,8,128]{2,1,0:T(8,128)S(1)}) custom-call(bf16[1024,1536]{1,0:T(8,128)(2,1)} %copy-done.53, bf16[1024,1536]{1,0:T(8,128)(2,1)} %copy-done.53, bf16[1024,1536]{1,0:T(8,128)(2,1)} %copy-done.53, bf16[1024,512]{1,0:T(8,128)(2,1)} %get-tuple-element.134.a0_ref.o_ref.refs_0_, ...), custom_call_target="tpu_custom_call" | custom-call | flops 16106127360 | bytes 4718592 | tf_op jit(solution)/shard_map/attend_back/pallas_call | solution.py:545
  411.0 4.1 add_slots.15
  416.3 5.0 heads_grad.2
  428.0 15.5 %attend_back.6 = (bf16[3,1024,256]{2,1,0:T(8,128)(2,1)}, f32[2,8,128]{2,1,0:T(8,128)S(1)}) custom-call(bf16[1024,1536]{1,0:T(8,128)(2,1)} %copy-done.54, bf16[1024,1536]{1,0:T(8,128)(2,1)} %copy-done.54, bf16[1024,1536]{1,0:T(8,128)(2,1)} %copy-done.54, bf16[1024,512]{1,0:T(8,128)(2,1)} %get-tuple-element.135.a1_ref.refs_1_.o_ref, ...), custom_call_target="tpu_custom_call" | custom-call | flops 16106127360 | bytes 4718592 | tf_op jit(solution)/shard_map/attend_back/pallas_call | solution.py:545
  443.6 15.5 %attend_back.7 = (bf16[3,1024,256]{2,1,0:T(8,128)(2,1)}, f32[2,8,128]{2,1,0:T(8,128)S(1)}) custom-call(bf16[1024,1536]{1,0:T(8,128)(2,1)} %copy-done.54, bf16[1024,1536]{1,0:T(8,128)(2,1)} %copy-done.54, bf16[1024,1536]{1,0:T(8,128)(2,1)} %copy-done.54, bf16[1024,512]{1,0:T(8,128)(2,1)} %get-tuple-element.135.a1_ref.refs_1_.o_ref, ...), custom_call_target="tpu_custom_call" | custom-call | flops 16106127360 | bytes 4718592 | tf_op jit(solution)/shard_map/attend_back/pallas_call | solution.py:545
  472.4 4.9 heads_grad.3
  479.5 3.8 collective-permute-done.39.got
  492.6 5.7 %collective-permute-done.40.refs_0_ = bf16[128,1664]{1,0:T(8,128)(2,1)S(1)} collective-permute-done((bf16[128,1664]{1,0:T(8,128)(2,1)S(1)}, bf16[128,1664]{1,0:T(8,128)(2,1)S(1)}, u32[]{:S(2)}, u32[]{:S(2)}) %collective-permute-start.40) | collective-permute-done | bytes 426016 | tf_op jit(solution)/shard_map/ppermute | solution.py:57
  506.4 11.2 %input_grad.1 = f32[1024,1024]{1,0:T(8,128)} custom-call(f32[1]{0:T(128)} %bitcast.34.scale_ref, f32[1024,1024]{1,0:T(8,128)} %get-tuple-element.216.base_ref, bf16[3,1024,256]{2,1,0:T(8,128)(2,1)S(1)} %copy-done.20, bf16[3,1024,256]{2,1,0:T(8,128)(2,1)S(1)} %copy-done.22, bf16[1024,1664]{1,0:T(8,128)(2,1)} %bitcast.65, ...), custom_call_target="tpu_custom_call" | custom-call | flops 6710886400 | bytes 20971520 | tf_op jit(solution)/shard_map/input_grad/pallas_call | solution.py:1038
  517.7 6.6 %collective-permute-done.43.refs_0_ = bf16[128,2048]{1,0:T(8,128)(2,1)S(1)} collective-permute-done((bf16[128,2048]{1,0:T(8,128)(2,1)S(1)}, bf16[128,2048]{1,0:T(8,128)(2,1)S(1)}, u32[]{:S(2)}, u32[]{:S(2)}) %collective-permute-start.43) | collective-permute-done | bytes 524320 | tf_op jit(solution)/shard_map/ppermute | solution.py:48
  534.2 5.8 %collective-permute-done.45.refs_0_ = bf16[64,1664]{1,0:T(8,128)(2,1)S(1)} collective-permute-done((bf16[64,1664]{1,0:T(8,128)(2,1)S(1)}, bf16[64,1664]{1,0:T(8,128)(2,1)S(1)}, u32[]{:S(2)}, u32[]{:S(2)}) %collective-permute-start.45) | collective-permute-done | bytes 213024 | tf_op jit(solution)/shard_map/ppermute | solution.py:48
  (408 shorter events, 183.8 us)
Async XLA Ops:
  7.2 186.7 %all-gather.3.cloned.1.call-start = ((), (), s32[]{:S(2)}) async-start(), calls=%async_computation.2 | async-start | bytes 8912896 | tf_op jit(solution)/shard_map/all_gather | solution.py:1142
  9.5 205.0 %all-gather.5.cloned.1.call-start = ((), (), s32[]{:S(2)}) async-start(), calls=%async_computation.3 | async-start | bytes 8912896 | tf_op jit(solution)/shard_map/all_gather | solution.py:1142
  10.4 456.4 %reduce-scatter.3.cloned.1.call-start = ((), (), s32[]{:S(2)}) async-start(), calls=%async_computation.4 | async-start | bytes 8912896 | tf_op jit(solution)/shard_map/reduce_scatter | solution.py:1219
  27.9 21.9 %collective-permute-start.3 = (bf16[64,1536]{1,0:T(8,128)(2,1)S(1)}, bf16[64,1536]{1,0:T(8,128)(2,1)S(1)}, u32[]{:S(2)}, u32[]{:S(2)}) collective-permute-start(bf16[64,1536]{1,0:T(8,128)(2,1)S(1)} %pad_maximum_fusion.15.refs_0_), channel_id=1, source_target_pairs={{0,8},{1,9},{2,10},{3,11},{4,12},{5,13},{6,14},{7,15},{8,0},{9,1},... | collective-permute-start | bytes 589832 | tf_op jit(solution)/shard_map/ppermute | solution.py:51
  27.9 21.9 %collective-permute-start.2 = (bf16[64,1536]{1,0:T(8,128)(2,1)S(1)}, bf16[64,1536]{1,0:T(8,128)(2,1)S(1)}, u32[]{:S(2)}, u32[]{:S(2)}) collective-permute-start(bf16[64,1536]{1,0:T(8,128)(2,1)S(1)} %pad_maximum_fusion.15.refs_0_), channel_id=1, source_target_pairs={{0,4},{1,5},{2,6},{3,7},{4,0},{5,1},{6,2},{7,3},{8,12},{9,13},{10,... | collective-permute-start | bytes 589832 | tf_op jit(solution)/shard_map/ppermute | solution.py:48
  73.1 29.7 %collective-permute-start.11 = (bf16[512,1664]{1,0:T(8,128)(2,1)S(1)}, bf16[512,1664]{1,0:T(8,128)(2,1)S(1)}, u32[]{:S(2)}, u32[]{:S(2)}) collective-permute-start(bf16[512,1664]{1,0:T(8,128)(2,1)S(1)} %shard_map.229), channel_id=1, source_target_pairs={{0,1},{1,0},{2,3},{3,2},{4,5},{5,4},{6,7},{7,6},{8,9},{9,8},{10,11... | collective-permute-start | bytes 5111816 | tf_op jit(solution)/shard_map/ppermute | solution.py:60
  73.2 26.2 %collective-permute-start.16 = (bf16[256,512]{1,0:T(8,128)(2,1)S(1)}, bf16[256,512]{1,0:T(8,128)(2,1)S(1)}, u32[]{:S(2)}, u32[]{:S(2)}) collective-permute-start(bf16[256,512]{1,0:T(8,128)(2,1)S(1)} %get-tuple-element.142.refs_0_), channel_id=1, source_target_pairs={{0,8},{1,9},{2,10},{3,11},{4,12},{5,13},{6,14},{7,15},{8,0},{9,1},... | collective-permute-start | bytes 786440 | tf_op jit(solution)/shard_map/ppermute | solution.py:51
  73.3 27.6 %collective-permute-start.10 = (bf16[192,1536]{1,0:T(8,128)(2,1)S(1)}, bf16[192,1536]{1,0:T(8,128)(2,1)S(1)}, u32[]{:S(2)}, u32[]{:S(2)}) collective-permute-start(bf16[192,1536]{1,0:T(8,128)(2,1)S(1)} %pad_maximum_fusion.4), channel_id=1, source_target_pairs={{0,16},{1,17},{2,18},{3,19},{4,20},{5,21},{6,22},{7,23},{8,24},{9,... | collective-permute-start | bytes 1769480 | tf_op jit(solution)/shard_map/ppermute | solution.py:57
  102.8 34.8 %collective-permute-start.21 = (bf16[256,512]{1,0:T(8,128)(2,1)S(1)}, bf16[256,512]{1,0:T(8,128)(2,1)S(1)}, u32[]{:S(2)}, u32[]{:S(2)}) collective-permute-start(bf16[256,512]{1,0:T(8,128)(2,1)S(1)} %get-tuple-element.146.refs_0_), channel_id=1, source_target_pairs={{0,8},{1,9},{2,10},{3,11},{4,12},{5,13},{6,14},{7,15},{8,0},{9,1},... | collective-permute-start | bytes 786440 | tf_op jit(solution)/shard_map/ppermute | solution.py:51
  102.8 33.8 %collective-permute-start.20 = (bf16[256,512]{1,0:T(8,128)(2,1)S(1)}, bf16[256,512]{1,0:T(8,128)(2,1)}, u32[]{:S(2)}, u32[]{:S(2)}) collective-permute-start(bf16[256,512]{1,0:T(8,128)(2,1)S(1)} %get-tuple-element.146.refs_0_), channel_id=1, source_target_pairs={{0,4},{1,5},{2,6},{3,7},{4,0},{5,1},{6,2},{7,3},{8,12},{9,13},{10,... | collective-permute-start | bytes 786440 | tf_op jit(solution)/shard_map/ppermute | solution.py:48
  102.8 34.8 %collective-permute-start.12 = (bf16[192,1024]{1,0:T(8,128)(2,1)}, bf16[192,1024]{1,0:T(8,128)(2,1)}, u32[]{:S(2)}, u32[]{:S(2)}) collective-permute-start(bf16[192,1024]{1,0:T(8,128)(2,1)} %pad_maximum_fusion.13), channel_id=1, source_target_pairs={{0,16},{1,17},{2,18},{3,19},{4,20},{5,21},{6,22},{7,23},{8,24},{9,... | collective-permute-start | bytes 1179656 | tf_op jit(solution)/shard_map/ppermute | solution.py:57
  109.6 30.6 %collective-permute-start.17 = (bf16[512,512]{1,0:T(8,128)(2,1)}, bf16[512,512]{1,0:T(8,128)(2,1)}, u32[]{:S(2)}, u32[]{:S(2)}) collective-permute-start(bf16[512,512]{1,0:T(8,128)(2,1)} %pad_maximum_fusion.9), channel_id=1, source_target_pairs={{0,2},{1,3},{2,0},{3,1},{4,6},{5,7},{6,4},{7,5},{8,10},{9,11},{10,... | collective-permute-start | bytes 1572872 | tf_op jit(solution)/shard_map/ppermute | solution.py:54
  109.6 33.7 %collective-permute-start.13 = (bf16[512,1536]{1,0:T(8,128)(2,1)}, bf16[512,1536]{1,0:T(8,128)(2,1)}, u32[]{:S(2)}, u32[]{:S(2)}) collective-permute-start(bf16[512,1536]{1,0:T(8,128)(2,1)} %shard_map.230), channel_id=1, source_target_pairs={{0,1},{1,0},{2,3},{3,2},{4,5},{5,4},{6,7},{7,6},{8,9},{9,8},{10,11... | collective-permute-start | bytes 4718600 | tf_op jit(solution)/shard_map/ppermute | solution.py:60
  143.3 21.5 %collective-permute-start.22 = (bf16[512,512]{1,0:T(8,128)(2,1)S(1)}, bf16[512,512]{1,0:T(8,128)(2,1)S(1)}, u32[]{:S(2)}, u32[]{:S(2)}) collective-permute-start(bf16[512,512]{1,0:T(8,128)(2,1)S(1)} %pad_maximum_fusion.10), channel_id=1, source_target_pairs={{0,2},{1,3},{2,0},{3,1},{4,6},{5,7},{6,4},{7,5},{8,10},{9,11},{10,... | collective-permute-start | bytes 1572872 | tf_op jit(solution)/shard_map/ppermute | solution.py:54
  145.4 21.4 %collective-permute-start.18 = (bf16[768,512]{1,0:T(8,128)(2,1)S(1)}, bf16[768,512]{1,0:T(8,128)(2,1)S(1)}, u32[]{:S(2)}, u32[]{:S(2)}) collective-permute-start(bf16[768,512]{1,0:T(8,128)(2,1)S(1)} %pad_maximum_fusion.1), channel_id=1, source_target_pairs={{0,16},{1,17},{2,18},{3,19},{4,20},{5,21},{6,22},{7,23},{8,24},{9,... | collective-permute-start | bytes 2359304 | tf_op jit(solution)/shard_map/ppermute | solution.py:57
  164.9 27.8 %collective-permute-start.23 = (bf16[768,512]{1,0:T(8,128)(2,1)S(1)}, bf16[768,512]{1,0:T(8,128)(2,1)S(1)}, u32[]{:S(2)}, u32[]{:S(2)}) collective-permute-start(bf16[768,512]{1,0:T(8,128)(2,1)S(1)} %pad_maximum_fusion.2), channel_id=1, source_target_pairs={{0,16},{1,17},{2,18},{3,19},{4,20},{5,21},{6,22},{7,23},{8,24},{9,... | collective-permute-start | bytes 2359304 | tf_op jit(solution)/shard_map/ppermute | solution.py:57
  168.8 41.1 %collective-permute-start.19 = (bf16[2048,512]{1,0:T(8,128)(2,1)}, bf16[2048,512]{1,0:T(8,128)(2,1)}, u32[]{:S(2)}, u32[]{:S(2)}) collective-permute-start(bf16[2048,512]{1,0:T(8,128)(2,1)} %shard_map.232), channel_id=1, source_target_pairs={{0,1},{1,0},{2,3},{3,2},{4,5},{5,4},{6,7},{7,6},{8,9},{9,8},{10,11... | collective-permute-start | bytes 6291464 | tf_op jit(solution)/shard_map/ppermute | solution.py:60
  268.9 38.3 %collective-permute-start.26 = (bf16[2048,1024]{1,0:T(8,128)(2,1)}, bf16[2048,1024]{1,0:T(8,128)(2,1)}, u32[]{:S(2)}, u32[]{:S(2)}) collective-permute-start(bf16[2048,1024]{1,0:T(8,128)(2,1)} %get-tuple-element.157), channel_id=1, source_target_pairs={{0,1},{1,0},{2,3},{3,2},{4,5},{5,4},{6,7},{7,6},{8,9},{9,8},{10,11... | collective-permute-start | bytes 12582920 | tf_op jit(solution)/shard_map/ppermute | solution.py:60
  271.9 35.2 %collective-permute-start.25 = (f32[8,128]{1,0:T(8,128)S(1)}, f32[8,128]{1,0:T(8,128)S(1)}, u32[]{:S(2)}, u32[]{:S(2)}) collective-permute-start(f32[8,128]{1,0:T(8,128)S(1)} %iota.13), channel_id=1, source_target_pairs={{0,1},{1,0},{2,3},{3,2},{4,5},{5,4},{6,7},{7,6},{8,9},{9,8},{10,11... | collective-permute-start | bytes 12296 | tf_op jit(solution)/shard_map/ppermute | solution.py:64
  309.4 232.8 %reduce-scatter.5.cloned.1.call-start = ((), (), s32[]{:S(2)}) async-start(), calls=%async_computation.5 | async-start | bytes 5570560 | tf_op jit(solution)/shard_map/reduce_scatter | solution.py:1253
  309.4 45.4 %collective-permute-start.28 = (bf16[512,1024]{1,0:T(8,128)(2,1)S(1)}, bf16[512,1024]{1,0:T(8,128)(2,1)S(1)}, u32[]{:S(2)}, u32[]{:S(2)}) collective-permute-start(bf16[512,1024]{1,0:T(8,128)(2,1)S(1)} %add_slots.12), channel_id=1, source_target_pairs={{0,16},{1,17},{2,18},{3,19},{4,20},{5,21},{6,22},{7,23},{8,24},{9,... | collective-permute-start | bytes 3145736 | tf_op jit(solution)/shard_map/ppermute | solution.py:57
  309.8 45.1 %collective-permute-start.27 = (f32[8,128]{1,0:T(8,128)S(1)}, f32[8,128]{1,0:T(8,128)S(1)}, u32[]{:S(2)}, u32[]{:S(2)}) collective-permute-start(f32[8,128]{1,0:T(8,128)S(1)} %add.94), channel_id=1, source_target_pairs={{0,2},{1,3},{2,0},{3,1},{4,6},{5,7},{6,4},{7,5},{8,10},{9,11},{10,... | collective-permute-start | bytes 12296 | tf_op jit(solution)/shard_map/ppermute | solution.py:64
  362.7 58.6 %collective-permute-start.34 = (bf16[768,1024]{1,0:T(8,128)(2,1)}, bf16[768,1024]{1,0:T(8,128)(2,1)S(1)}, u32[]{:S(2)}, u32[]{:S(2)}) collective-permute-start(bf16[768,1024]{1,0:T(8,128)(2,1)} %add_slots.13), channel_id=1, source_target_pairs={{0,2},{1,3},{2,0},{3,1},{4,6},{5,7},{6,4},{7,5},{8,10},{9,11},{10,... | collective-permute-start | bytes 4718600 | tf_op jit(solution)/shard_map/ppermute | solution.py:54
  374.9 36.0 %collective-permute-start.32 = (bf16[256,2048]{1,0:T(8,128)(2,1)}, bf16[256,2048]{1,0:T(8,128)(2,1)S(1)}, u32[]{:S(2)}, u32[]{:S(2)}) collective-permute-start(bf16[256,2048]{1,0:T(8,128)(2,1)} %add_slots.14), channel_id=1, source_target_pairs={{0,16},{1,17},{2,18},{3,19},{4,20},{5,21},{6,22},{7,23},{8,24},{9,... | collective-permute-start | bytes 3145736 | tf_op jit(solution)/shard_map/ppermute | solution.py:57
  376.8 34.1 %collective-permute-start.31 = (f32[8,128]{1,0:T(8,128)S(1)}, f32[8,128]{1,0:T(8,128)S(1)}, u32[]{:S(2)}, u32[]{:S(2)}) collective-permute-start(f32[8,128]{1,0:T(8,128)S(1)} %add.96), channel_id=1, source_target_pairs={{0,8},{1,9},{2,10},{3,11},{4,12},{5,13},{6,14},{7,15},{8,0},{9,1},... | collective-permute-start | bytes 12296 | tf_op jit(solution)/shard_map/ppermute | solution.py:64
  416.0 45.3 %collective-permute-start.37 = (bf16[384,2048]{1,0:T(8,128)(2,1)}, bf16[384,2048]{1,0:T(8,128)(2,1)S(1)}, u32[]{:S(2)}, u32[]{:S(2)}) collective-permute-start(bf16[384,2048]{1,0:T(8,128)(2,1)} %add_slots.15), channel_id=1, source_target_pairs={{0,2},{1,3},{2,0},{3,1},{4,6},{5,7},{6,4},{7,5},{8,10},{9,11},{10,... | collective-permute-start | bytes 4718600 | tf_op jit(solution)/shard_map/ppermute | solution.py:54
  425.8 35.6 %collective-permute-start.35 = (bf16[256,1024]{1,0:T(8,128)(2,1)}, bf16[256,1024]{1,0:T(8,128)(2,1)}, u32[]{:S(2)}, u32[]{:S(2)}) collective-permute-start(bf16[256,1024]{1,0:T(8,128)(2,1)} %get-tuple-element.187), channel_id=1, source_target_pairs={{0,4},{1,5},{2,6},{3,7},{4,0},{5,1},{6,2},{7,3},{8,12},{9,13},{10,... | collective-permute-start | bytes 1572872 | tf_op jit(solution)/shard_map/ppermute | solution.py:48
  425.9 35.4 %collective-permute-start.36 = (bf16[256,1024]{1,0:T(8,128)(2,1)}, bf16[256,1024]{1,0:T(8,128)(2,1)}, u32[]{:S(2)}, u32[]{:S(2)}) collective-permute-start(bf16[256,1024]{1,0:T(8,128)(2,1)} %get-tuple-element.188), channel_id=1, source_target_pairs={{0,8},{1,9},{2,10},{3,11},{4,12},{5,13},{6,14},{7,15},{8,0},{9,1},... | collective-permute-start | bytes 1572872 | tf_op jit(solution)/shard_map/ppermute | solution.py:51
  427.3 33.4 %collective-permute-start.33 = (f32[8,128]{1,0:T(8,128)S(1)}, f32[8,128]{1,0:T(8,128)}, u32[]{:S(2)}, u32[]{:S(2)}) collective-permute-start(f32[8,128]{1,0:T(8,128)S(1)} %add.97), channel_id=1, source_target_pairs={{0,16},{1,17},{2,18},{3,19},{4,20},{5,21},{6,22},{7,23},{8,24},{9,... | collective-permute-start | bytes 12296 | tf_op jit(solution)/shard_map/ppermute | solution.py:64
  489.0 35.3 %collective-permute-start.43 = (bf16[128,2048]{1,0:T(8,128)(2,1)S(1)}, bf16[128,2048]{1,0:T(8,128)(2,1)S(1)}, u32[]{:S(2)}, u32[]{:S(2)}) collective-permute-start(bf16[128,2048]{1,0:T(8,128)(2,1)S(1)} %copy-done.50), channel_id=1, source_target_pairs={{0,4},{1,5},{2,6},{3,7},{4,0},{5,1},{6,2},{7,3},{8,12},{9,13},{10,... | collective-permute-start | bytes 1572872 | tf_op jit(solution)/shard_map/ppermute | solution.py:48
  489.9 36.1 %collective-permute-start.44 = (bf16[128,2048]{1,0:T(8,128)(2,1)S(1)}, bf16[128,2048]{1,0:T(8,128)(2,1)S(1)}, u32[]{:S(2)}, u32[]{:S(2)}) collective-permute-start(bf16[128,2048]{1,0:T(8,128)(2,1)S(1)} %copy-done.48), channel_id=1, source_target_pairs={{0,8},{1,9},{2,10},{3,11},{4,12},{5,13},{6,14},{7,15},{8,0},{9,1},... | collective-permute-start | bytes 1572872 | tf_op jit(solution)/shard_map/ppermute | solution.py:51
  500.4 25.7 %collective-permute-start.41 = (bf16[192,1664]{1,0:T(8,128)(2,1)S(1)}, bf16[192,1664]{1,0:T(8,128)(2,1)S(1)}, u32[]{:S(2)}, u32[]{:S(2)}) collective-permute-start(bf16[192,1664]{1,0:T(8,128)(2,1)S(1)} %add_slots.19), channel_id=1, source_target_pairs={{0,2},{1,3},{2,0},{3,1},{4,6},{5,7},{6,4},{7,5},{8,10},{9,11},{10,... | collective-permute-start | bytes 1916936 | tf_op jit(solution)/shard_map/ppermute | solution.py:54
  (102 other events, 944.3 us)
Sparse Core Ops, SparseCore 0:
  10.2 106.9 all-gather.2
  119.3 76.1 all-gather.4
  309.5 117.4 reduce-scatter.2
  430.8 96.0 reduce-scatter.4

commit v3 on v2

--- a/solution.py
+++ b/solution.py
@@ -140,7 +140,7 @@
         self.groups = NZ * at.nx
         self.core = at.core.reshape(1).astype(jnp.int32)
 
-    def tick(self, tick, gate):
+    def tick(self, tick, gate, strict=False):
         at = self.at
         count = len(self.ready)
         offsets = range(1, at.nx)
@@ -156,6 +156,8 @@
         i = tick - 1
         if 0 <= i < count:
             piece = self.ready[i]
+            if strict:
+                self.near[i], self.far[i] = tie(self.near[i], self.far[i], *gate)[:2]
             rows = piece.shape[0]
             halves = [
                 lax.dynamic_slice_in_dim(part, y * (rows // 2), rows // 2, axis=0) for part in (piece, self.near[i])
@@ -461,7 +463,7 @@
 
 
 def attend_back_kernel(temper, q_ref, k_ref, v_ref, o_ref, g_ref, cos_ref, sin_ref, scale_ref, seg_ref, lse_ref,
-                       g3_ref, gs_ref, q_sc, k_sc, v_sc, g_sc, dq_sc, dk_sc, dv_sc):
+                       g3_ref, gs_ref, q_sc, k_sc, v_sc, g_sc, qo_sc, go_sc, dq_sc, dk_sc, dv_sc):
     length = q_ref.shape[0]
     bf16 = jnp.bfloat16
     f32 = jnp.float32
@@ -495,6 +497,8 @@
             marks = jnp.where(spare == n, parts[n], marks)
         g_sc[head] = jnp.where(own, grad.astype(f32), marks).astype(bf16)
         v_sc[head] = jnp.where(own, v.astype(f32), ((spare >= 0) & (spare < 3)).astype(f32)).astype(bf16)
+        qo_sc[head] = only(q2, head)
+        go_sc[head] = only(grad, head)
     size = min(ROWS_K, length)
     causal = lax.broadcasted_iota(jnp.int32, (size, size), 0) <= lax.broadcasted_iota(
         jnp.int32, (size, size), 1
@@ -506,25 +510,22 @@
         end = at + size
         dqs = []
         for head in range(2):
-            queries = q_sc[head, at:end, :]
-            grads = g_sc[head, at:end, :]
             keys = k_sc[head, :end, :]
-            probs = causal_bottom(jnp.exp2(dot_last(keys, queries) * factor), causal)
-            ds = (probs * dot_last(v_sc[head, :end, :], grads)).astype(bf16)
-            dv = jnp.dot(probs.astype(bf16), grads, preferred_element_type=f32)
-            dk = jnp.dot(ds, queries, preferred_element_type=f32)
+            probs = causal_bottom(jnp.exp2(dot_last(keys, q_sc[head, at:end, :]) * factor), causal)
+            ds = (probs * dot_last(v_sc[head, :end, :], g_sc[head, at:end, :])).astype(bf16)
+            dv = jnp.dot(probs.astype(bf16), go_sc[head, at:end, :], preferred_element_type=f32)
+            dk = jnp.dot(ds, qo_sc[head, at:end, :], preferred_element_type=f32)
             dqs.append(dot_first(ds, keys))
-            if block == blocks - 1:
-                dv_sc[head] = dv
-                dk_sc[head] = dk
+            if block == blocks - 1 and head == 0:
+                dv_sc[...] = dv
+                dk_sc[...] = dk
             else:
-                dv_sc[head, :end, :] += dv
-                dk_sc[head, :end, :] += dk
+                dv_sc[:end, :] += dv
+                dk_sc[:end, :] += dk
         dq_sc[at:end, :] = jnp.where(lanes == 0, dqs[0], dqs[1])
-    lanes = lanes_of((length, PAIR)) // HEAD
-    g3_ref[2] = jnp.where(lanes == 0, dv_sc[0], dv_sc[1]).astype(bf16)
+    g3_ref[2] = dv_sc[...].astype(bf16)
     dq = dq_sc[...] * temper
-    dk = jnp.where(lanes == 0, dk_sc[0], dk_sc[1]) * temper
+    dk = dk_sc[...] * temper
     gs_ref[0] = jnp.broadcast_to(jnp.sum(dq * qn + dk * kn, axis=0, keepdims=True), (8, PAIR))
 
     def unturn(grad, unit, unit_factor):
@@ -554,9 +555,8 @@
             pl.BlockSpec((3, length, PAIR), lambda p: (0, 0, p)),
             pl.BlockSpec((1, 8, PAIR), lambda p: (p, 0, 0)),
         ],
-        scratch_shapes=[pltpu.VMEM((2, length, PAIR), jnp.bfloat16)] * 4
-        + [pltpu.VMEM((length, PAIR), jnp.float32)]
-        + [pltpu.VMEM((2, length, PAIR), jnp.float32)] * 2,
+        scratch_shapes=[pltpu.VMEM((2, length, PAIR), jnp.bfloat16)] * 6
+        + [pltpu.VMEM((length, PAIR), jnp.float32)] * 3,
         out_shape=[
             far_array((3, length, pairs * PAIR), jnp.bfloat16),
             jax.ShapeDtypeStruct((pairs, 8, PAIR), jnp.float32),
@@ -662,7 +662,10 @@
             pl.BlockSpec((width, width), lambda i: (0, 0)), full, pl.BlockSpec((1, width), lambda i: (0, 0)),
         ],
         out_specs=[full] * 4,
-        out_shape=[shape(width, jnp.float32)] * 2 + [shape(width, jnp.bfloat16)] * 2,
+        out_shape=[
+            far_array((rows, width), jnp.float32), far_array((rows, width), jnp.float32),
+            shape(width, jnp.bfloat16), far_array((rows, width), jnp.bfloat16),
+        ],
         compiler_params=pltpu.CompilerParams(vmem_limit_bytes=40 << 20),
         cost_estimate=pl.CostEstimate(flops=2 * rows * width * width, bytes_accessed=20 * rows * width, transcendentals=0),
         name="after_attention",
@@ -1011,15 +1014,12 @@
 
 def input_grad_kernel(scale_ref, base_ref, *refs):
     out_ref = refs[-1]
-    count = len(refs) // 3
     total = base_ref[...]
-    for n in range(count):
-        first, second, w = refs[n * 3 : n * 3 + 3]
-        cols = first.shape[2]
+    for n in range(len(refs) // 2):
+        part, w = refs[2 * n : 2 * n + 2]
+        cols = part.shape[2]
         for p in range(3):
-            at = 2 * p * cols
-            total = total + dot_last(first[p], w[:, at : at + cols])
-            total = total + dot_last(second[p], w[:, at + cols : at + 2 * cols])
+            total = total + dot_last(part[p], w[:, p * cols : (p + 1) * cols])
     out_ref[...] = total * scale_ref[0]
 
 
@@ -1028,12 +1028,10 @@
     tile = min(256, width)
     out = pl.BlockSpec((rows, tile), lambda j: (0, j))
     specs, operands = [], []
-    for n, w in enumerate(weights):
-        for part in parts[2 * n : 2 * n + 2]:
-            specs.append(pl.BlockSpec(part.shape, lambda j: (0, 0, 0), pipeline_mode=pl.Buffered(1)))
-            operands.append(part)
+    for part, w in zip(parts, weights):
+        specs.append(pl.BlockSpec(part.shape, lambda j: (0, 0, 0), pipeline_mode=pl.Buffered(1)))
         specs.append(pl.BlockSpec((tile, w.shape[1]), lambda j: (j, 0)))
-        operands.append(w)
+        operands += [part, w]
     flops = 2 * rows * width * sum(w.shape[1] for w in weights)
     return pl.pallas_call(
         input_grad_kernel,
@@ -1160,7 +1158,6 @@
     weights, qkv, att, lse = {}, [], [], []
     for n in range(2):
         moved = gather.tick(4 + n, gate)
-        late.tick(1 + n, gate)
         gate = gate + gather.sends
         weights[n] = gather.full(n)
         if n == 0:
@@ -1172,6 +1169,7 @@
                 place += size
             f_sqk, f_aa, f_su, f_sg, f_am = shorts
         qkv.append(dot(after(tokens, gate), weights[n][:, : 3 * half]))
+        late.tick(1 + n, [qkv[n]], True)
         out, sums = attention(qkv[n], cosine, sine, f_sqk, segs, n * half)
         att.append(out)
         lse.append(sums)
@@ -1227,10 +1225,8 @@
     g3, g_scale = {}, []
 
     def back(n, gate):
-        part = pairs // 2
         out, sums = attention_back(
-            qkv[n // 2], att[n // 2], after(g_att, gate), lse[n // 2], cosine, sine, f_sqk, segs,
-            n // 2 * half, n % 2 * part, part,
+            qkv[n], att[n], after(g_att, gate), lse[n], cosine, sine, f_sqk, segs, n * half, 0, pairs
         )
         g3[n] = out
         g_scale.append(sums[:, 0, :].reshape(-1))
@@ -1245,23 +1241,21 @@
     gate = moved + [g_att]
     moved, gate = window(gate, ["up"])
     moved += counted.step(gate)
-    back(0, gate)
-    gate = moved + back(1, [g3[0]])
+    gate = moved + back(0, gate)
     over_x, gate = window(gate, ["up"])
     over_x += counted.step(gate)
-    attended = heads_grad(after(tokens, gate), [g3[0], g3[1]], attended)
+    attended = heads_grad(after(tokens, gate), [g3[0]], attended)
     own_att = lax.psum_scatter(attended, "shard", scatter_dimension=0, tiled=True)
     moved, gate = window([attended], ["down"])
-    back(2, gate)
-    first_up = after(first_up.reshape(2 * each, ff // 2), [g3[2]])
+    gate = moved + over_x + back(1, gate)
+    first_up = after(first_up.reshape(2 * each, ff // 2), gate)
     last_up = at.along_y(first_up)
-    gate = moved + over_x + back(3, [g3[2]])
     counts = counted.total()
     count = jnp.maximum(counts[4, 0], 1.0)
     loss = counts[0, 0] / count
     scale = rows * at.reps * at.shards / count
     over_z, gate = window(gate, ["up"])
-    sides = heads_grad(after(x_sorted, gate), [g3[2], g3[3]], wide=PAIR)
+    sides = heads_grad(after(x_sorted, gate), [g3[1]], wide=PAIR)
     shorts = [
         jnp.concatenate(g_scale), grad_aa.reshape(-1), jnp.concatenate([su0, su1], axis=1).reshape(-1),
         jnp.concatenate([sg0, sg1], axis=1).reshape(-1), grad_am.reshape(-1),
@@ -1282,7 +1276,7 @@
     last_down, _ = window(gate, ["down"])
     moved += last_down
     grad_x = input_grad(
-        scale.reshape(1), after(gx_base, sends), [g3[n] for n in range(4)], [weights[0], weights[1]]
+        scale.reshape(1), after(gx_base, sends), [g3[0], g3[1]], [weights[0], weights[1]]
     )
     gate = moved + over_z + [grad_x]
     gate, _ = window(gate, ["qkv1", "up"])

time: 565 us -> 550 us (0.973)
  waiting for transfers between devices: 80.5 us -> 96.4 us
  Pallas kernels: 317 us -> 302 us
  local copies, waits for them, and re-layouts: 53 us -> 43.3 us
  starting transfers between devices: 63.1 us -> 56.1 us
    ppermute x13, starting transfers between devices: 23.7 us -> 11.1 us  [along_y(): lax.ppermute(value, AXES, self.moves(lambda r, z, x, c: (r ^ 1, z, x, c)))]
    pallas_call x5, Pallas kernels: 18 us -> 7.12 us  [weave(): pl.pallas_call(partial(weave_kernel, columns), out_shape=jax.ShapeDtypeSt...]
    ppermute x8, waiting for transfers between devices: 15.5 us -> 25.1 us  [along_x(): lax.ppermute(value, AXES, self.moves(lambda r, z, x, c: (r, z, x ^ j, c)))]
    all_gather x2, waiting for transfers between devices: 0.02 us -> 9.12 us  [body(): lax.all_gather(columns(w_upgate, [n * ff // 2, ff + n * ff // 2], ff // 2...]
    ppermute x13, waiting for transfers between devices: 11.2 us -> 19.6 us  [along_y(): lax.ppermute(value, AXES, self.moves(lambda r, z, x, c: (r ^ 1, z, x, c)))]
    ppermute x8, waiting for transfers between devices: 30.7 us -> 23.8 us  [near_z(): lax.ppermute(value, AXES, self.moves(lambda r, z, x, c: (r, z ^ 1, x, c)))]
    pallas_call x4 -> x2, Pallas kernels: 61.6 us -> 55.2 us  [attention_back(): pl.pallas_call(partial(attend_back_kernel, math.sqrt(HEAD)), grid=(pairs,...]
    unnamed x168 -> x152, local copies, waits for them, and re-layouts: 32.6 us -> 27.7 us
  transfers between devices with their start and end apart: 54 -> 54, of which waited for: 18 -> 21; matrix products, arithmetic and copies ran while one was open for 9% -> 8% of each run, Pallas kernels for 49% -> 49%
where the time goes in v3:
time: 550 us; the launch traced here: 545 us
  Pallas kernels  302 us (55%)
  waiting for transfers between devices  96.4 us (18%)
  starting transfers between devices  56.1 us (10%)
  local copies, waits for them, and re-layouts  43.3 us (8%)
  between operations  17.8 us (3%)
  other arithmetic  17.2 us (3%)
  matrix products  12.2 us (2%)
    pallas_call x2, Pallas kernels, feed_back(): pl.pallas_call(partial(feed_back_kernel, steps, each, last), grid=(steps,...  80.1 us
    pallas_call x2, Pallas kernels, attention_back(): pl.pallas_call(partial(attend_back_kernel, math.sqrt(HEAD)), grid=(pairs,...  55.2 us
    pallas_call x12, Pallas kernels, add_slots(): pl.pallas_call(partial(slots_kernel, plan, rows, len(terms)), in_specs=[p...  30.9 us
    unnamed x152, local copies, waits for them, and re-layouts  27.7 us
    pallas_call x2, Pallas kernels, feed_up(): pl.pallas_call(up_kernel, grid=(steps,), in_specs=[pl.BlockSpec((rows, wi...  27.7 us
    ppermute x8, waiting for transfers between devices, along_x(): lax.ppermute(value, AXES, self.moves(lambda r, z, x, c: (r, z, x ^ j, c)))  25.1 us
    ppermute x8, waiting for transfers between devices, near_z(): lax.ppermute(value, AXES, self.moves(lambda r, z, x, c: (r, z ^ 1, x, c)))  23.8 us
    pallas_call x2, Pallas kernels, attention(): pl.pallas_call(partial(attend_kernel, math.sqrt(HEAD)), grid=(pairs,), in...  23.2 us
  transfers between devices with their start and end apart: 54, of which 21 were waited for; matrix products, arithmetic and copies ran while one was open for 8% of the time, Pallas kernels for 49%

profile of v3, /device:TPU:0, one launch (start us, length us, event | category | flops | bytes accessed | tf_op | source)
XLA Modules:
  0.0 545.4 jit_solution(3167473643096461324)
XLA Ops:
  27.0 4.2 collective-permute-start.2
  31.2 3.9 collective-permute-start.3
  40.0 6.8 %collective-permute-done.2.refs_1_ = bf16[64,1536]{1,0:T(8,128)(2,1)S(1)} collective-permute-done((bf16[64,1536]{1,0:T(8,128)(2,1)S(1)}, bf16[64,1536]{1,0:T(8,128)(2,1)S(1)}, u32[]{:S(2)}, u32[]{:S(2)}) %collective-permute-start.2) | collective-permute-done | bytes 196640 | tf_op jit(solution)/shard_map/ppermute | solution.py:48
  46.9 6.6 %collective-permute-done.3.refs_2_ = bf16[64,1536]{1,0:T(8,128)(2,1)S(1)} collective-permute-done((bf16[64,1536]{1,0:T(8,128)(2,1)S(1)}, bf16[64,1536]{1,0:T(8,128)(2,1)S(1)}, u32[]{:S(2)}, u32[]{:S(2)}) %collective-permute-start.3) | collective-permute-done | bytes 196640 | tf_op jit(solution)/shard_map/ppermute | solution.py:51
  61.0 9.6 %collective-permute-done.7 = bf16[128,1536]{1,0:T(8,128)(2,1)S(1)} collective-permute-done((bf16[128,1536]{1,0:T(8,128)(2,1)S(1)}, bf16[128,1536]{1,0:T(8,128)(2,1)S(1)}, u32[]{:S(2)}, u32[]{:S(2)}) %collective-permute-start.7) | collective-permute-done | bytes 393248 | tf_op jit(solution)/shard_map/ppermute | solution.py:54
  77.8 5.4 collective-permute-done.9
  89.5 4.8 convolution_convert_fusion.1.q_ref.k_ref.v_ref
  110.3 11.6 %attend.2 = (bf16[1024,512]{1,0:T(8,128)(2,1)}, f32[1024,512]{1,0:T(8,128)}) custom-call(bf16[1024,1536]{1,0:T(8,128)(2,1)S(1)} %copy-done.48, bf16[1024,1536]{1,0:T(8,128)(2,1)S(1)} %copy-done.48, bf16[1024,1536]{1,0:T(8,128)(2,1)S(1)} %copy-done.48, f32[1024,128]{1,0:T(8,128)S(1)} %copy-done.23, f32[1024,128]{1,0:T(8,128)S(1)} %copy-done.25, ...), custom_call_target="tpu_custom_call" | custom-call | flops 4294967296 | bytes 4194304 | tf_op jit(solution)/shard_map/attend/pallas_call | solution.py:431
  131.7 11.7 %attend.3 = (bf16[1024,512]{1,0:T(8,128)(2,1)}, f32[1024,512]{1,0:T(8,128)}) custom-call(bf16[1024,1536]{1,0:T(8,128)(2,1)S(1)} %convolution_convert_fusion.q_ref.k_ref.v_ref, bf16[1024,1536]{1,0:T(8,128)(2,1)S(1)} %convolution_convert_fusion.q_ref.k_ref.v_ref, bf16[1024,1536]{1,0:T(8,128)(2,1)S(1)} %convolution_convert_fusion.q_ref.k_ref.v_ref, ...), custom_call_target="tpu_custom_call" | custom-call | flops 4294967296 | bytes 4194304 | tf_op jit(solution)/shard_map/attend/pallas_call | solution.py:431
  143.4 4.8 collective-permute-done.22
  153.3 8.9 %after_attention.1 = (f32[1024,1024]{1,0:T(8,128)}, f32[1024,1024]{1,0:T(8,128)}, bf16[1024,1024]{1,0:T(8,128)(2,1)S(1)}, bf16[1024,1024]{1,0:T(8,128)(2,1)}) custom-call(s32[1]{0:T(128)} %bitcast.core_ref.core, bf16[1024,512]{1,0:T(8,128)(2,1)} %get-tuple-element.132.a0_ref.o_ref.refs_0_, bf16[1024,512]{1,0:T(8,128)(2,1)} %get-tuple-element.133.a1_ref.refs_1_.o_ref, ...), custom_call_target="tpu_custom_call" | custom-call | flops 2147483648 | bytes 20971520 | tf_op jit(solution)/shard_map/after_attention/pallas_call | solution.py:657
  163.5 4.2 collective-permute-done.23
  170.6 13.9 %feed_up.2 = (bf16[1024,4096]{1,0:T(8,128)(2,1)}, bf16[1024,4096]{1,0:T(8,128)(2,1)}, bf16[1024,4096]{1,0:T(8,128)(2,1)}) custom-call(bf16[1024,1024]{1,0:T(8,128)(2,1)S(1)} %copy-done.15, bf16[1024,4096]{1,0:T(8,128)(2,1)} %all-gather.3.cloned.1.call-done.wu_ref.wg_ref, bf16[1024,4096]{1,0:T(8,128)(2,1)} %all-gather.3.cloned.1.call-done.wu_ref.wg_ref, ...), custom_call_target="tpu_custom_call" | custom-call | flops 8589934592 | bytes 23068672 | tf_op jit(solution)/shard_map/feed_up/pallas_call | solution.py:701
  189.3 9.1 %all-gather.5.cloned.1.call-done.wu_ref.wg_ref = bf16[1024,4096]{1,0:T(8,128)(2,1)} async-done(((bf16[64,4096]{1,0:T(8,128)(2,1)}), bf16[1024,4096]{1,0:T(8,128)(2,1)}) %all-gather.5.cloned.1.call-update) | async-done | bytes 8388624 | tf_op jit(solution)/shard_map/all_gather | solution.py:1140
  200.0 13.8 %feed_up.3 = (bf16[1024,4096]{1,0:T(8,128)(2,1)}, bf16[1024,4096]{1,0:T(8,128)(2,1)}, bf16[1024,4096]{1,0:T(8,128)(2,1)}) custom-call(bf16[1024,1024]{1,0:T(8,128)(2,1)S(1)} %copy-done.16, bf16[1024,4096]{1,0:T(8,128)(2,1)} %all-gather.5.cloned.1.call-done.wu_ref.wg_ref, ...), custom_call_target="tpu_custom_call", output_to_operand_aliasing={{0}: (5, {}), {1}: (6, {}), {2}: (7, {})} | custom-call | flops 8589934592 | bytes 23068672 | tf_op jit(solution)/shard_map/feed_up/pallas_call | solution.py:701
  217.9 21.3 %finish.1 = (bf16[1024,1024]{1,0:T(8,128)(2,1)}, bf16[1024,1024]{1,0:T(8,128)(2,1)S(1)}, f32[1024,1024]{1,0:T(8,128)}, f32[1,1024]{1,0:T(1,128)S(1)}, f32[1,1024]{1,0:T(1,128)S(1)}) custom-call(bf16[1024,4096]{1,0:T(8,128)(2,1)} %get-tuple-element.139.hid_ref.h_ref, bf16[4096,512]{1,0:T(8,128)(2,1)} %bitcast.57, bf16[4096,512]{1,0:T(8,128)(2,1)} %bitcast.60, ...), custom_call_target="tpu_custom_call" | custom-call | flops 8589934592 | bytes 33554432 | tf_op jit(solution)/shard_map/finish/pallas_call | solution.py:772
  239.2 12.2 %down_grad.1 = (bf16[2048,1024]{1,0:T(8,128)(2,1)}, bf16[2048,1024]{1,0:T(8,128)(2,1)}) custom-call(s32[1]{0:T(128)} %bitcast.core_ref.core, bf16[1024,4096]{1,0:T(8,128)(2,1)S(1)} %bitcast.54, bf16[1024,1024]{1,0:T(8,128)(2,1)S(1)} %get-tuple-element.167.g_ref), custom_call_target="tpu_custom_call" | custom-call | flops 8589934592 | bytes 18874368 | tf_op jit(solution)/shard_map/down_grad/pallas_call | solution.py:922
  254.6 35.2 %feed_back.2 = (f32[1,2048]{1,0:T(1,128)}, f32[1,2048]{1,0:T(1,128)}, bf16[16,2,64,2048]{3,2,1,0:T(8,128)(2,1)}, f32[1024,1024]{1,0:T(8,128)}) custom-call(bf16[1024,1024]{1,0:T(8,128)(2,1)} %copy-done.50, bf16[1024,1024]{1,0:T(8,128)(2,1)} %copy-done.14, bf16[4096,512]{1,0:T(8,128)(2,1)} %bitcast.58, bf16[4096,512]{1,0:T(8,128)(2,1)} %bitcast.61, ...), custom_call_target="tpu_custom_call" | custom-call | flops 21474836480 | bytes 58720256 | tf_op jit(solution)/shard_map/feed_back/pallas_call | solution.py:893
  294.3 44.8 %feed_back.3 = (f32[1,2048]{1,0:T(1,128)}, f32[1,2048]{1,0:T(1,128)}, bf16[8,2,64,2048]{3,2,1,0:T(8,128)(2,1)}, bf16[8,2,64,2048]{3,2,1,0:T(8,128)(2,1)}, bf16[1...) custom-call(bf16[1024,1024]{1,0:T(8,128)(2,1)} %copy-done.50, ...), custom_call_target="tpu_custom_call" | custom-call | flops 21474836480 | bytes 58720256 | tf_op jit(solution)/shard_map/feed_back/pallas_call | solution.py:893
  341.9 4.1 add_slots.13
  360.2 27.6 %attend_back.2 = (bf16[3,1024,512]{2,1,0:T(8,128)(2,1)}, f32[4,8,128]{2,1,0:T(8,128)S(1)}) custom-call(bf16[1024,1536]{1,0:T(8,128)(2,1)} %convolution_convert_fusion.1.q_ref.k_ref.v_ref, bf16[1024,1536]{1,0:T(8,128)(2,1)} %convolution_convert_fusion.1.q_ref.k_ref.v_ref, bf16[1024,1536]{1,0:T(8,128)(2,1)} %convolution_convert_fusion.1.q_ref.k_ref.v_ref, ...), custom_call_target="tpu_custom_call" | custom-call | flops 32212254720 | bytes 9437184 | tf_op jit(solution)/shard_map/attend_back/pallas_call | solution.py:546
  387.9 4.1 add_slots.15
  393.7 5.1 heads_grad.2
  398.9 5.5 collective-permute-done.34.refs_1_.refs_2_
  413.4 27.6 %attend_back.3 = (bf16[3,1024,512]{2,1,0:T(8,128)(2,1)}, f32[4,8,128]{2,1,0:T(8,128)S(1)}) custom-call(bf16[1024,1536]{1,0:T(8,128)(2,1)} %copy-done.49, bf16[1024,1536]{1,0:T(8,128)(2,1)} %copy-done.49, bf16[1024,1536]{1,0:T(8,128)(2,1)} %copy-done.49, bf16[1024,512]{1,0:T(8,128)(2,1)} %get-tuple-element.133.a1_ref.refs_1_.o_ref, ...), custom_call_target="tpu_custom_call" | custom-call | flops 32212254720 | bytes 9437184 | tf_op jit(solution)/shard_map/attend_back/pallas_call | solution.py:546
  452.8 4.9 heads_grad.3
  461.0 3.8 collective-permute-done.39.got
  472.9 6.9 %collective-permute-done.40.refs_0_ = bf16[128,1664]{1,0:T(8,128)(2,1)S(1)} collective-permute-done((bf16[128,1664]{1,0:T(8,128)(2,1)S(1)}, bf16[128,1664]{1,0:T(8,128)(2,1)S(1)}, u32[]{:S(2)}, u32[]{:S(2)}) %collective-permute-start.40) | collective-permute-done | bytes 426016 | tf_op jit(solution)/shard_map/ppermute | solution.py:57
  486.6 12.1 %input_grad.1 = f32[1024,1024]{1,0:T(8,128)} custom-call(f32[1]{0:T(128)} %bitcast.34.scale_ref, f32[1024,1024]{1,0:T(8,128)} %get-tuple-element.212.base_ref, bf16[3,1024,512]{2,1,0:T(8,128)(2,1)S(1)} %copy-done.11, bf16[1024,1664]{1,0:T(8,128)(2,1)} %bitcast.65, bf16[3,1024,512]{2,1,0:T(8,128)(2,1)} %get-tuple-element.191.refs_0_.refs_2_, ...), custom_call_target="tpu_custom_call" | custom-call | flops 6710886400 | bytes 20971520 | tf_op jit(solution)/shard_map/input_grad/pallas_call | solution.py:1036
  498.7 6.5 %collective-permute-done.43.refs_0_ = bf16[128,2048]{1,0:T(8,128)(2,1)S(1)} collective-permute-done((bf16[128,2048]{1,0:T(8,128)(2,1)S(1)}, bf16[128,2048]{1,0:T(8,128)(2,1)S(1)}, u32[]{:S(2)}, u32[]{:S(2)}) %collective-permute-start.43) | collective-permute-done | bytes 524320 | tf_op jit(solution)/shard_map/ppermute | solution.py:48
  515.4 6.1 %collective-permute-done.45.refs_0_ = bf16[64,1664]{1,0:T(8,128)(2,1)S(1)} collective-permute-done((bf16[64,1664]{1,0:T(8,128)(2,1)S(1)}, bf16[64,1664]{1,0:T(8,128)(2,1)S(1)}, u32[]{:S(2)}, u32[]{:S(2)}) %collective-permute-start.45) | collective-permute-done | bytes 213024 | tf_op jit(solution)/shard_map/ppermute | solution.py:48
  529.3 5.1 collective-permute-done.49
  (386 shorter events, 175.4 us)
Async XLA Ops:
  7.2 161.8 %all-gather.3.cloned.1.call-start = ((), (), s32[]{:S(2)}) async-start(), calls=%async_computation.2 | async-start | bytes 8912896 | tf_op jit(solution)/shard_map/all_gather | solution.py:1140
  9.4 189.0 %all-gather.5.cloned.1.call-start = ((), (), s32[]{:S(2)}) async-start(), calls=%async_computation.3 | async-start | bytes 8912896 | tf_op jit(solution)/shard_map/all_gather | solution.py:1140
  10.4 438.0 %reduce-scatter.3.cloned.1.call-start = ((), (), s32[]{:S(2)}) async-start(), calls=%async_computation.4 | async-start | bytes 8912896 | tf_op jit(solution)/shard_map/reduce_scatter | solution.py:1217
  27.0 19.8 %collective-permute-start.2 = (bf16[64,1536]{1,0:T(8,128)(2,1)S(1)}, bf16[64,1536]{1,0:T(8,128)(2,1)S(1)}, u32[]{:S(2)}, u32[]{:S(2)}) collective-permute-start(bf16[64,1536]{1,0:T(8,128)(2,1)S(1)} %pad_maximum_fusion.15.refs_0_), channel_id=1, source_target_pairs={{0,4},{1,5},{2,6},{3,7},{4,0},{5,1},{6,2},{7,3},{8,12},{9,13},{10,... | collective-permute-start | bytes 589832 | tf_op jit(solution)/shard_map/ppermute | solution.py:48
  31.2 22.3 %collective-permute-start.3 = (bf16[64,1536]{1,0:T(8,128)(2,1)S(1)}, bf16[64,1536]{1,0:T(8,128)(2,1)S(1)}, u32[]{:S(2)}, u32[]{:S(2)}) collective-permute-start(bf16[64,1536]{1,0:T(8,128)(2,1)S(1)} %pad_maximum_fusion.15.refs_0_), channel_id=1, source_target_pairs={{0,8},{1,9},{2,10},{3,11},{4,12},{5,13},{6,14},{7,15},{8,0},{9,1},... | collective-permute-start | bytes 589832 | tf_op jit(solution)/shard_map/ppermute | solution.py:51
  74.1 27.6 %collective-permute-start.15 = (bf16[256,512]{1,0:T(8,128)(2,1)S(1)}, bf16[256,512]{1,0:T(8,128)(2,1)}, u32[]{:S(2)}, u32[]{:S(2)}) collective-permute-start(bf16[256,512]{1,0:T(8,128)(2,1)S(1)} %get-tuple-element.140.refs_0_), channel_id=1, source_target_pairs={{0,4},{1,5},{2,6},{3,7},{4,0},{5,1},{6,2},{7,3},{8,12},{9,13},{10,... | collective-permute-start | bytes 786440 | tf_op jit(solution)/shard_map/ppermute | solution.py:48
  75.8 27.2 %collective-permute-start.16 = (bf16[256,512]{1,0:T(8,128)(2,1)S(1)}, bf16[256,512]{1,0:T(8,128)(2,1)S(1)}, u32[]{:S(2)}, u32[]{:S(2)}) collective-permute-start(bf16[256,512]{1,0:T(8,128)(2,1)S(1)} %get-tuple-element.140.refs_0_), channel_id=1, source_target_pairs={{0,8},{1,9},{2,10},{3,11},{4,12},{5,13},{6,14},{7,15},{8,0},{9,1},... | collective-permute-start | bytes 786440 | tf_op jit(solution)/shard_map/ppermute | solution.py:51
  94.3 34.3 %collective-permute-start.20 = (bf16[256,512]{1,0:T(8,128)(2,1)S(1)}, bf16[256,512]{1,0:T(8,128)(2,1)}, u32[]{:S(2)}, u32[]{:S(2)}) collective-permute-start(bf16[256,512]{1,0:T(8,128)(2,1)S(1)} %get-tuple-element.146.refs_0_), channel_id=1, source_target_pairs={{0,4},{1,5},{2,6},{3,7},{4,0},{5,1},{6,2},{7,3},{8,12},{9,13},{10,... | collective-permute-start | bytes 786440 | tf_op jit(solution)/shard_map/ppermute | solution.py:48
  94.8 33.9 %collective-permute-start.21 = (bf16[256,512]{1,0:T(8,128)(2,1)S(1)}, bf16[256,512]{1,0:T(8,128)(2,1)S(1)}, u32[]{:S(2)}, u32[]{:S(2)}) collective-permute-start(bf16[256,512]{1,0:T(8,128)(2,1)S(1)} %get-tuple-element.146.refs_0_), channel_id=1, source_target_pairs={{0,8},{1,9},{2,10},{3,11},{4,12},{5,13},{6,14},{7,15},{8,0},{9,1},... | collective-permute-start | bytes 786440 | tf_op jit(solution)/shard_map/ppermute | solution.py:51
  97.6 25.1 %collective-permute-start.13 = (bf16[512,1536]{1,0:T(8,128)(2,1)}, bf16[512,1536]{1,0:T(8,128)(2,1)}, u32[]{:S(2)}, u32[]{:S(2)}) collective-permute-start(bf16[512,1536]{1,0:T(8,128)(2,1)} %shard_map.230), channel_id=1, source_target_pairs={{0,1},{1,0},{2,3},{3,2},{4,5},{5,4},{6,7},{7,6},{8,9},{9,8},{10,11... | collective-permute-start | bytes 4718600 | tf_op jit(solution)/shard_map/ppermute | solution.py:60
  101.7 20.2 %collective-permute-start.12 = (bf16[192,1024]{1,0:T(8,128)(2,1)}, bf16[192,1024]{1,0:T(8,128)(2,1)S(1)}, u32[]{:S(2)}, u32[]{:S(2)}) collective-permute-start(bf16[192,1024]{1,0:T(8,128)(2,1)} %pad_maximum_fusion.13), channel_id=1, source_target_pairs={{0,16},{1,17},{2,18},{3,19},{4,20},{5,21},{6,22},{7,23},{8,24},{9,... | collective-permute-start | bytes 1179656 | tf_op jit(solution)/shard_map/ppermute | solution.py:57
  122.7 25.5 %collective-permute-start.14 = (bf16[512,1024]{1,0:T(8,128)(2,1)S(1)}, bf16[512,1024]{1,0:T(8,128)(2,1)S(1)}, u32[]{:S(2)}, u32[]{:S(2)}) collective-permute-start(bf16[512,1024]{1,0:T(8,128)(2,1)S(1)} %shard_map.231), channel_id=1, source_target_pairs={{0,1},{1,0},{2,3},{3,2},{4,5},{5,4},{6,7},{7,6},{8,9},{9,8},{10,11... | collective-permute-start | bytes 3145736 | tf_op jit(solution)/shard_map/ppermute | solution.py:60
  130.9 19.7 %collective-permute-start.18 = (bf16[768,512]{1,0:T(8,128)(2,1)S(1)}, bf16[768,512]{1,0:T(8,128)(2,1)S(1)}, u32[]{:S(2)}, u32[]{:S(2)}) collective-permute-start(bf16[768,512]{1,0:T(8,128)(2,1)S(1)} %pad_maximum_fusion.1), channel_id=1, source_target_pairs={{0,16},{1,17},{2,18},{3,19},{4,20},{5,21},{6,22},{7,23},{8,24},{9,... | collective-permute-start | bytes 2359304 | tf_op jit(solution)/shard_map/ppermute | solution.py:57
  148.2 19.6 %collective-permute-start.23 = (bf16[768,512]{1,0:T(8,128)(2,1)S(1)}, bf16[768,512]{1,0:T(8,128)(2,1)S(1)}, u32[]{:S(2)}, u32[]{:S(2)}) collective-permute-start(bf16[768,512]{1,0:T(8,128)(2,1)S(1)} %pad_maximum_fusion.2), channel_id=1, source_target_pairs={{0,16},{1,17},{2,18},{3,19},{4,20},{5,21},{6,22},{7,23},{8,24},{9,... | collective-permute-start | bytes 2359304 | tf_op jit(solution)/shard_map/ppermute | solution.py:57
  153.1 31.7 %collective-permute-start.19 = (bf16[2048,512]{1,0:T(8,128)(2,1)}, bf16[2048,512]{1,0:T(8,128)(2,1)}, u32[]{:S(2)}, u32[]{:S(2)}) collective-permute-start(bf16[2048,512]{1,0:T(8,128)(2,1)} %shard_map.232), channel_id=1, source_target_pairs={{0,1},{1,0},{2,3},{3,2},{4,5},{5,4},{6,7},{7,6},{8,9},{9,8},{10,11... | collective-permute-start | bytes 6291464 | tf_op jit(solution)/shard_map/ppermute | solution.py:60
  184.5 29.3 %collective-permute-start.24 = (bf16[2048,512]{1,0:T(8,128)(2,1)S(1)}, bf16[2048,512]{1,0:T(8,128)(2,1)}, u32[]{:S(2)}, u32[]{:S(2)}) collective-permute-start(bf16[2048,512]{1,0:T(8,128)(2,1)S(1)} %shard_map.233), channel_id=1, source_target_pairs={{0,1},{1,0},{2,3},{3,2},{4,5},{5,4},{6,7},{7,6},{8,9},{9,8},{10,11... | collective-permute-start | bytes 6291464 | tf_op jit(solution)/shard_map/ppermute | solution.py:60
  251.4 38.4 %collective-permute-start.26 = (bf16[2048,1024]{1,0:T(8,128)(2,1)}, bf16[2048,1024]{1,0:T(8,128)(2,1)}, u32[]{:S(2)}, u32[]{:S(2)}) collective-permute-start(bf16[2048,1024]{1,0:T(8,128)(2,1)} %get-tuple-element.159), channel_id=1, source_target_pairs={{0,1},{1,0},{2,3},{3,2},{4,5},{5,4},{6,7},{7,6},{8,9},{9,8},{10,11... | collective-permute-start | bytes 12582920 | tf_op jit(solution)/shard_map/ppermute | solution.py:60
  254.3 35.5 %collective-permute-start.25 = (f32[8,128]{1,0:T(8,128)S(1)}, f32[8,128]{1,0:T(8,128)S(1)}, u32[]{:S(2)}, u32[]{:S(2)}) collective-permute-start(f32[8,128]{1,0:T(8,128)S(1)} %iota.13), channel_id=1, source_target_pairs={{0,1},{1,0},{2,3},{3,2},{4,5},{5,4},{6,7},{7,6},{8,9},{9,8},{10,11... | collective-permute-start | bytes 12296 | tf_op jit(solution)/shard_map/ppermute | solution.py:64
  292.1 223.3 %reduce-scatter.5.cloned.1.call-start = ((), (), s32[]{:S(2)}) async-start(), calls=%async_computation.5 | async-start | bytes 5570560 | tf_op jit(solution)/shard_map/reduce_scatter | solution.py:1248
  292.2 47.0 %collective-permute-start.28 = (bf16[512,1024]{1,0:T(8,128)(2,1)S(1)}, bf16[512,1024]{1,0:T(8,128)(2,1)S(1)}, u32[]{:S(2)}, u32[]{:S(2)}) collective-permute-start(bf16[512,1024]{1,0:T(8,128)(2,1)S(1)} %add_slots.12), channel_id=1, source_target_pairs={{0,16},{1,17},{2,18},{3,19},{4,20},{5,21},{6,22},{7,23},{8,24},{9,... | collective-permute-start | bytes 3145736 | tf_op jit(solution)/shard_map/ppermute | solution.py:57
  293.7 45.4 %collective-permute-start.27 = (f32[8,128]{1,0:T(8,128)S(1)}, f32[8,128]{1,0:T(8,128)S(1)}, u32[]{:S(2)}, u32[]{:S(2)}) collective-permute-start(f32[8,128]{1,0:T(8,128)S(1)} %add.94), channel_id=1, source_target_pairs={{0,2},{1,3},{2,0},{3,1},{4,6},{5,7},{6,4},{7,5},{8,10},{9,11},{10,... | collective-permute-start | bytes 12296 | tf_op jit(solution)/shard_map/ppermute | solution.py:64
  354.3 50.0 %collective-permute-start.34 = (bf16[768,1024]{1,0:T(8,128)(2,1)}, bf16[768,1024]{1,0:T(8,128)(2,1)S(1)}, u32[]{:S(2)}, u32[]{:S(2)}) collective-permute-start(bf16[768,1024]{1,0:T(8,128)(2,1)} %add_slots.13), channel_id=1, source_target_pairs={{0,2},{1,3},{2,0},{3,1},{4,6},{5,7},{6,4},{7,5},{8,10},{9,11},{10,... | collective-permute-start | bytes 4718600 | tf_op jit(solution)/shard_map/ppermute | solution.py:54
  359.0 28.9 %collective-permute-start.32 = (bf16[256,2048]{1,0:T(8,128)(2,1)}, bf16[256,2048]{1,0:T(8,128)(2,1)S(1)}, u32[]{:S(2)}, u32[]{:S(2)}) collective-permute-start(bf16[256,2048]{1,0:T(8,128)(2,1)} %add_slots.14), channel_id=1, source_target_pairs={{0,16},{1,17},{2,18},{3,19},{4,20},{5,21},{6,22},{7,23},{8,24},{9,... | collective-permute-start | bytes 3145736 | tf_op jit(solution)/shard_map/ppermute | solution.py:57
  359.3 28.6 %collective-permute-start.31 = (f32[8,128]{1,0:T(8,128)S(1)}, f32[8,128]{1,0:T(8,128)S(1)}, u32[]{:S(2)}, u32[]{:S(2)}) collective-permute-start(f32[8,128]{1,0:T(8,128)S(1)} %add.96), channel_id=1, source_target_pairs={{0,8},{1,9},{2,10},{3,11},{4,12},{5,13},{6,14},{7,15},{8,0},{9,1},... | collective-permute-start | bytes 12296 | tf_op jit(solution)/shard_map/ppermute | solution.py:64
  393.0 50.2 %collective-permute-start.37 = (bf16[384,2048]{1,0:T(8,128)(2,1)}, bf16[384,2048]{1,0:T(8,128)(2,1)S(1)}, u32[]{:S(2)}, u32[]{:S(2)}) collective-permute-start(bf16[384,2048]{1,0:T(8,128)(2,1)} %add_slots.15), channel_id=1, source_target_pairs={{0,2},{1,3},{2,0},{3,1},{4,6},{5,7},{6,4},{7,5},{8,10},{9,11},{10,... | collective-permute-start | bytes 4718600 | tf_op jit(solution)/shard_map/ppermute | solution.py:54
  408.7 34.4 %collective-permute-start.35 = (bf16[256,1024]{1,0:T(8,128)(2,1)}, bf16[256,1024]{1,0:T(8,128)(2,1)}, u32[]{:S(2)}, u32[]{:S(2)}) collective-permute-start(bf16[256,1024]{1,0:T(8,128)(2,1)} %get-tuple-element.187), channel_id=1, source_target_pairs={{0,4},{1,5},{2,6},{3,7},{4,0},{5,1},{6,2},{7,3},{8,12},{9,13},{10,... | collective-permute-start | bytes 1572872 | tf_op jit(solution)/shard_map/ppermute | solution.py:48
  408.9 34.2 %collective-permute-start.36 = (bf16[256,1024]{1,0:T(8,128)(2,1)}, bf16[256,1024]{1,0:T(8,128)(2,1)}, u32[]{:S(2)}, u32[]{:S(2)}) collective-permute-start(bf16[256,1024]{1,0:T(8,128)(2,1)} %get-tuple-element.188), channel_id=1, source_target_pairs={{0,8},{1,9},{2,10},{3,11},{4,12},{5,13},{6,14},{7,15},{8,0},{9,1},... | collective-permute-start | bytes 1572872 | tf_op jit(solution)/shard_map/ppermute | solution.py:51
  412.2 30.2 %collective-permute-start.33 = (f32[8,128]{1,0:T(8,128)S(1)}, f32[8,128]{1,0:T(8,128)}, u32[]{:S(2)}, u32[]{:S(2)}) collective-permute-start(f32[8,128]{1,0:T(8,128)S(1)} %add.97), channel_id=1, source_target_pairs={{0,16},{1,17},{2,18},{3,19},{4,20},{5,21},{6,22},{7,23},{8,24},{9,... | collective-permute-start | bytes 12296 | tf_op jit(solution)/shard_map/ppermute | solution.py:64
  471.3 34.0 %collective-permute-start.43 = (bf16[128,2048]{1,0:T(8,128)(2,1)S(1)}, bf16[128,2048]{1,0:T(8,128)(2,1)S(1)}, u32[]{:S(2)}, u32[]{:S(2)}) collective-permute-start(bf16[128,2048]{1,0:T(8,128)(2,1)S(1)} %copy-done.46), channel_id=1, source_target_pairs={{0,4},{1,5},{2,6},{3,7},{4,0},{5,1},{6,2},{7,3},{8,12},{9,13},{10,... | collective-permute-start | bytes 1572872 | tf_op jit(solution)/shard_map/ppermute | solution.py:48
  472.1 36.1 %collective-permute-start.44 = (bf16[128,2048]{1,0:T(8,128)(2,1)S(1)}, bf16[128,2048]{1,0:T(8,128)(2,1)S(1)}, u32[]{:S(2)}, u32[]{:S(2)}) collective-permute-start(bf16[128,2048]{1,0:T(8,128)(2,1)S(1)} %copy-done.44), channel_id=1, source_target_pairs={{0,8},{1,9},{2,10},{3,11},{4,12},{5,13},{6,14},{7,15},{8,0},{9,1},... | collective-permute-start | bytes 1572872 | tf_op jit(solution)/shard_map/ppermute | solution.py:51
  481.9 26.3 %collective-permute-start.41 = (bf16[192,1664]{1,0:T(8,128)(2,1)S(1)}, bf16[192,1664]{1,0:T(8,128)(2,1)S(1)}, u32[]{:S(2)}, u32[]{:S(2)}) collective-permute-start(bf16[192,1664]{1,0:T(8,128)(2,1)S(1)} %add_slots.19), channel_id=1, source_target_pairs={{0,2},{1,3},{2,0},{3,1},{4,6},{5,7},{6,4},{7,5},{8,10},{9,11},{10,... | collective-permute-start | bytes 1916936 | tf_op jit(solution)/shard_map/ppermute | solution.py:54
  485.9 22.3 %collective-permute-start.42 = (bf16[256,1024]{1,0:T(8,128)(2,1)S(1)}, bf16[256,1024]{1,0:T(8,128)(2,1)S(1)}, u32[]{:S(2)}, u32[]{:S(2)}) collective-permute-start(bf16[256,1024]{1,0:T(8,128)(2,1)S(1)} %add_slots.20), channel_id=1, source_target_pairs={{0,16},{1,17},{2,18},{3,19},{4,20},{5,21},{6,22},{7,23},{8,24},{9,... | collective-permute-start | bytes 1572872 | tf_op jit(solution)/shard_map/ppermute | solution.py:57
  (94 other events, 922.0 us)
Sparse Core Ops, SparseCore 0:
  10.2 107.8 all-gather.2
  120.2 78.2 all-gather.4
  292.2 115.9 reduce-scatter.2
  413.5 94.6 reduce-scatter.4
